TPU v7x, 128 devices: a whole 4x4x4 slice. The times are simulated.
128 devices in a mesh: dev: 128 (over x, y, z, core).
Axes of the slice: x: 4, y: 4, z: 4, core: 2. Of those that a mesh axis runs over, the one named last changes fastest.
Arguments:
- features: bfloat16 [65536, 1024], P('dev'), may hold values from -6 to 6
- w_hidden: bfloat16 [1024, 512], replicated, may hold values from -0.1875 to 0.1875
- w_out: bfloat16 [512, 128], replicated, may hold values from -0.25 to 0.25
- items: bfloat16 [262144, 128], P('dev'), may hold values from -200 to 200
- routes: int32 [65536, 4], P('dev'), may hold values from 0 to 2047, all different within a row; in each aligned block of 512 rows (0 to 511, 512 to 1023, ...) at most 2 rows name the same one
- cluster_slot: int32 [2048], replicated, may hold values from 0 to 2047, each once
- sample_ids: int32 [2048, 4096], P('dev'), may hold values from 0 to 127
- sample_counts: int32 [2048, 4096], P('dev'), may hold values from 1 to 4095
- positives: int32 [65536, 4], P('dev'), may hold values from 0 to 4095
Outputs:
- slot_loss: float32 [2048], P('dev')
- grad_hidden: float32 [1024, 512], replicated
- grad_out: float32 [512, 128], replicated
- item_grad: float32 [262144, 128], P('dev')
Inputs may be any that keep to these rules, and one draw needn't show every extreme that they name: `routes`: each row names 4 different clusters; within the rows of one device no cluster is named more than 2 times; every cluster is named by some row. `cluster_slot`: each cluster has one slot.
All inputs are finite; a program needn't handle non-finite values.
Results may differ from a plain program's by a relative error of at most 0.012.
The roundings to bfloat16 on the way count: a program that leaves them out, or rounds other values in their place, can miss the bound.
Values may be sent and summed in bfloat16 or wider, within the bound.
No kernel may reach another device: no remote copies, remote signals or barrier semaphores. Data moves between devices by JAX's collectives and lax.ppermute only.
A program may use at most 128 MiB of HBM per device.

v0:
```python
import math

import jax
import jax.numpy as jnp
from jax import lax
from jax.sharding import PartitionSpec as P


def silu_grad(value):
    sig = jax.nn.sigmoid(value)
    return sig * (1.0 + value * (1.0 - sig))


def slot_ranks(keys):
    order = jnp.argsort(keys, stable=True)
    sorted_keys = keys[order]
    first = jnp.searchsorted(sorted_keys, sorted_keys, side="left")
    ranked = jnp.arange(keys.shape[0], dtype=jnp.int32) - first
    return jnp.zeros_like(keys).at[order].set(ranked)


def score_block(queries, targets, block_items, table_ids, counts):
    item_rows = block_items.shape[1]
    picks = (
        table_ids[:, :, None] == lax.broadcasted_iota(jnp.int32, table_ids.shape + (item_rows,), 2)
    ).astype(jnp.bfloat16)
    table = jnp.einsum(
        "csi,cie->cse", picks, block_items, preferred_element_type=jnp.float32
    ).astype(jnp.bfloat16)
    scores = jnp.einsum("cqe,cse->cqs", queries, table, preferred_element_type=jnp.float32)
    scores = scores - jnp.log(counts.astype(jnp.float32))[:, None, :]
    top = jnp.max(scores, axis=2, keepdims=True)
    expo = jnp.exp(scores - top)
    total = jnp.sum(expo, axis=2, keepdims=True)
    hit = lax.broadcasted_iota(jnp.int32, scores.shape, 2) == targets[:, :, None]
    picked = jnp.sum(jnp.where(hit, scores, 0.0), axis=2)
    losses = jnp.log(total[:, :, 0]) + top[:, :, 0] - picked
    live = targets >= 0
    cluster_loss = jnp.sum(jnp.where(live, losses, 0.0), axis=1) / jnp.sum(
        live.astype(jnp.float32), axis=1
    )
    weight = (expo / total - hit.astype(jnp.float32)).astype(jnp.bfloat16)
    wsum = jnp.einsum("cqs,csi->cqi", weight, picks, preferred_element_type=jnp.float32)
    dquery = jnp.einsum(
        "cqi,cie->cqe", wsum, block_items.astype(jnp.float32), precision=lax.Precision.HIGHEST
    ).astype(jnp.bfloat16)
    dtable = jnp.einsum(
        "cqi,cqe->cie", wsum, queries.astype(jnp.float32), precision=lax.Precision.HIGHEST
    )
    return (cluster_loss, dquery, dtable)


def owner_range(got_query, got_target, items, sample_ids, sample_counts, first, count):
    local_clusters = sample_ids.shape[0]
    width = items.shape[1]
    item_rows = items.shape[0] // local_clusters
    cluster_items = items.reshape(local_clusters, item_rows, width)
    block = math.gcd(count, 4)

    def step(carry, index):
        start = first + index * block
        queries = lax.dynamic_slice_in_dim(got_query, start, block, 0)
        targets = lax.dynamic_slice_in_dim(got_target, start, block, 0)
        table_ids = lax.dynamic_slice_in_dim(sample_ids, start, block, 0)
        counts = lax.dynamic_slice_in_dim(sample_counts, start, block, 0)
        block_items = lax.dynamic_slice_in_dim(cluster_items, start, block, 0)
        cluster_loss, dquery, dtable = score_block(queries, targets, block_items, table_ids, counts)
        return (carry, (cluster_loss, dquery, dtable))

    _, (losses, dquery, dtable) = lax.scan(
        step, jnp.zeros((), jnp.float32), jnp.arange(count // block, dtype=jnp.int32)
    )
    losses = losses.reshape((count,))
    dquery = dquery.reshape((count,) + dquery.shape[2:])
    grads = dtable.reshape((count * item_rows, width))
    return (grads, losses, dquery)


def local(
    features, w_hidden, w_out, items, routes, cluster_slot, sample_ids, sample_counts, positives
):
    devices = lax.axis_size("dev")
    users, visits = routes.shape
    clusters = cluster_slot.shape[0]
    local_clusters = sample_ids.shape[0]
    width = w_out.shape[1]
    capacity = max(2, 2 * users * visits // (local_clusters * devices))
    pre = jnp.dot(features, w_hidden, preferred_element_type=jnp.float32)
    hidden = jax.nn.silu(pre).astype(jnp.bfloat16)
    query = jnp.dot(hidden, w_out, preferred_element_type=jnp.float32).astype(jnp.bfloat16)
    flat_slots = jnp.take(cluster_slot, routes.reshape(-1), axis=0)
    ranks = slot_ranks(flat_slots)
    place = flat_slots * capacity + ranks
    send_query = (
        jnp.zeros((clusters * capacity, width), jnp.bfloat16)
        .at[place]
        .set(jnp.repeat(query, visits, axis=0))
    )
    send_target = (
        jnp.full((clusters * capacity,), -1, jnp.int32).at[place].set(positives.reshape(-1))
    )
    got_query, got_target = (
        lax.all_to_all(
            send_query.reshape(clusters, capacity, width),
            "dev",
            split_axis=0,
            concat_axis=1,
            tiled=True,
        ),
        lax.all_to_all(
            send_target.reshape(clusters, capacity), "dev", split_axis=0, concat_axis=1, tiled=True
        ),
    )
    grads, slot_loss, dq_all = owner_range(
        got_query, got_target, items, sample_ids, sample_counts, 0, local_clusters
    )
    returned = lax.all_to_all(dq_all, "dev", split_axis=1, concat_axis=0, tiled=True).reshape(
        clusters * capacity, width
    )
    dq_pairs = jnp.take(returned, place, axis=0).astype(jnp.float32).reshape(users, visits, width)
    dq_total = jnp.sum(dq_pairs, axis=1).astype(jnp.bfloat16)
    local_out = jnp.dot(hidden.T, dq_total, preferred_element_type=jnp.float32)
    dhidden = jnp.dot(dq_total, w_out.T, preferred_element_type=jnp.float32)
    dpre = (dhidden * silu_grad(pre)).astype(jnp.bfloat16)
    local_hidden = jnp.dot(features.T, dpre, preferred_element_type=jnp.float32)
    grad_hidden, grad_out = lax.psum((local_hidden, local_out), "dev")
    return (slot_loss, grad_hidden, grad_out, grads)


def solution(mesh):
    in_specs = (
        P("dev", None),
        P(),
        P(),
        P("dev", None),
        P("dev", None),
        P(),
        P("dev", None),
        P("dev", None),
        P("dev", None),
    )
    out_specs = (P("dev"), P(), P(), P("dev", None))
    return jax.shard_map(local, mesh=mesh, in_specs=in_specs, out_specs=out_specs, check_vma=False)
```

profile of v0, /device:TPU:1, one launch (start us, length us, event | category | flops | bytes accessed | tf_op | source)
XLA Modules:
  0.0 579.7 jit_solution(11802738402833302580)
XLA Ops:
  8.5 10.2 %gather_fusion.1 = s32[2048]{0:T(1024)S(1)} fusion(s32[2048]{0:T(1024)} %param.18, s32[2048]{0:T(1024)S(1)} %broadcast_clamp_fusion.3), kind=kCustom, calls=%fused_computation.1 | custom fusion | bytes 24576 | tf_op jit(solution)/shard_map/jit(_take)/gather | solution.py:91
  23.8 11.8 %gather_fusion.2 = s32[2048]{0:T(1024)S(1)} fusion(s32[2048]{0:T(1024)S(1)} %and_select_fusion, s32[2048]{0:T(1024)S(1)} %get-tuple-element.234), kind=kCustom, calls=%fused_computation.2 | custom fusion | bytes 24576 | tf_op jit(solution)/shard_map/gather | solution.py:16
  35.6 142.4 %while.40 = (s32[]{:T(128)}, u32[2048]{0:T(1024)S(1)}, u32[2048]{0:T(1024)S(1)}, s32[2048]{0:T(1024)S(1)}, s32[]{:T(128)}, /*index=5*/s32[]{:T(128)}, s32[]{}) while((s32[]{:T(128)}, u32[2048]{0:T(1024)S(1)}, u32[2048]{0:T(1024)S(1)}, s32[2048]{0:T(1024)S(1)}, s32[]{:T(128)}, /*index=5*/s32[]{:T(128)}, s32[]{}) %tuple.75), condition=%wide.region_2.3_spmd.clone, body=%wide.region_1.2_spmd.clone.sunk | while | flops 38916 | bytes 135277 | solution.py:17
  35.7 11.8 %gather_fusion = s32[2048]{0:T(1024)S(1)} fusion(s32[2048]{0:T(1024)S(1)} %get-tuple-element.361, u32[2048]{0:T(1024)S(1)} %broadcast_clamp_fusion.5), kind=kCustom, calls=%fused_computation.clone.clone.1 | custom fusion | bytes 24576 | tf_op jit(solution)/shard_map/jit(searchsorted)/jit(_searchsorted_scan_impl)/vmap(jit(_searchsorted_scan_impl))/while/body/eval_jaxpr/gather | solution.py:17
  47.5 11.8 %gather_fusion = s32[2048]{0:T(1024)S(1)} fusion(s32[2048]{0:T(1024)S(1)} %get-tuple-element.361, u32[2048]{0:T(1024)S(1)} %broadcast_clamp_fusion.5), kind=kCustom, calls=%fused_computation.clone.clone.1 | custom fusion | bytes 24576 | tf_op jit(solution)/shard_map/jit(searchsorted)/jit(_searchsorted_scan_impl)/vmap(jit(_searchsorted_scan_impl))/while/body/eval_jaxpr/gather | solution.py:17
  59.4 11.8 %gather_fusion = s32[2048]{0:T(1024)S(1)} fusion(s32[2048]{0:T(1024)S(1)} %get-tuple-element.361, u32[2048]{0:T(1024)S(1)} %broadcast_clamp_fusion.5), kind=kCustom, calls=%fused_computation.clone.clone.1 | custom fusion | bytes 24576 | tf_op jit(solution)/shard_map/jit(searchsorted)/jit(_searchsorted_scan_impl)/vmap(jit(_searchsorted_scan_impl))/while/body/eval_jaxpr/gather | solution.py:17
  71.3 11.8 %gather_fusion = s32[2048]{0:T(1024)S(1)} fusion(s32[2048]{0:T(1024)S(1)} %get-tuple-element.361, u32[2048]{0:T(1024)S(1)} %broadcast_clamp_fusion.5), kind=kCustom, calls=%fused_computation.clone.clone.1 | custom fusion | bytes 24576 | tf_op jit(solution)/shard_map/jit(searchsorted)/jit(_searchsorted_scan_impl)/vmap(jit(_searchsorted_scan_impl))/while/body/eval_jaxpr/gather | solution.py:17
  83.1 11.8 %gather_fusion = s32[2048]{0:T(1024)S(1)} fusion(s32[2048]{0:T(1024)S(1)} %get-tuple-element.361, u32[2048]{0:T(1024)S(1)} %broadcast_clamp_fusion.5), kind=kCustom, calls=%fused_computation.clone.clone.1 | custom fusion | bytes 24576 | tf_op jit(solution)/shard_map/jit(searchsorted)/jit(_searchsorted_scan_impl)/vmap(jit(_searchsorted_scan_impl))/while/body/eval_jaxpr/gather | solution.py:17
  95.0 11.8 %gather_fusion = s32[2048]{0:T(1024)S(1)} fusion(s32[2048]{0:T(1024)S(1)} %get-tuple-element.361, u32[2048]{0:T(1024)S(1)} %broadcast_clamp_fusion.5), kind=kCustom, calls=%fused_computation.clone.clone.1 | custom fusion | bytes 24576 | tf_op jit(solution)/shard_map/jit(searchsorted)/jit(_searchsorted_scan_impl)/vmap(jit(_searchsorted_scan_impl))/while/body/eval_jaxpr/gather | solution.py:17
  106.9 11.8 %gather_fusion = s32[2048]{0:T(1024)S(1)} fusion(s32[2048]{0:T(1024)S(1)} %get-tuple-element.361, u32[2048]{0:T(1024)S(1)} %broadcast_clamp_fusion.5), kind=kCustom, calls=%fused_computation.clone.clone.1 | custom fusion | bytes 24576 | tf_op jit(solution)/shard_map/jit(searchsorted)/jit(_searchsorted_scan_impl)/vmap(jit(_searchsorted_scan_impl))/while/body/eval_jaxpr/gather | solution.py:17
  118.7 11.8 %gather_fusion = s32[2048]{0:T(1024)S(1)} fusion(s32[2048]{0:T(1024)S(1)} %get-tuple-element.361, u32[2048]{0:T(1024)S(1)} %broadcast_clamp_fusion.5), kind=kCustom, calls=%fused_computation.clone.clone.1 | custom fusion | bytes 24576 | tf_op jit(solution)/shard_map/jit(searchsorted)/jit(_searchsorted_scan_impl)/vmap(jit(_searchsorted_scan_impl))/while/body/eval_jaxpr/gather | solution.py:17
  130.6 11.8 %gather_fusion = s32[2048]{0:T(1024)S(1)} fusion(s32[2048]{0:T(1024)S(1)} %get-tuple-element.361, u32[2048]{0:T(1024)S(1)} %broadcast_clamp_fusion.5), kind=kCustom, calls=%fused_computation.clone.clone.1 | custom fusion | bytes 24576 | tf_op jit(solution)/shard_map/jit(searchsorted)/jit(_searchsorted_scan_impl)/vmap(jit(_searchsorted_scan_impl))/while/body/eval_jaxpr/gather | solution.py:17
  142.5 11.8 %gather_fusion = s32[2048]{0:T(1024)S(1)} fusion(s32[2048]{0:T(1024)S(1)} %get-tuple-element.361, u32[2048]{0:T(1024)S(1)} %broadcast_clamp_fusion.5), kind=kCustom, calls=%fused_computation.clone.clone.1 | custom fusion | bytes 24576 | tf_op jit(solution)/shard_map/jit(searchsorted)/jit(_searchsorted_scan_impl)/vmap(jit(_searchsorted_scan_impl))/while/body/eval_jaxpr/gather | solution.py:17
  154.3 11.8 %gather_fusion = s32[2048]{0:T(1024)S(1)} fusion(s32[2048]{0:T(1024)S(1)} %get-tuple-element.361, u32[2048]{0:T(1024)S(1)} %broadcast_clamp_fusion.5), kind=kCustom, calls=%fused_computation.clone.clone.1 | custom fusion | bytes 24576 | tf_op jit(solution)/shard_map/jit(searchsorted)/jit(_searchsorted_scan_impl)/vmap(jit(_searchsorted_scan_impl))/while/body/eval_jaxpr/gather | solution.py:17
  166.2 11.8 %gather_fusion = s32[2048]{0:T(1024)S(1)} fusion(s32[2048]{0:T(1024)S(1)} %get-tuple-element.361, u32[2048]{0:T(1024)S(1)} %broadcast_clamp_fusion.5), kind=kCustom, calls=%fused_computation.clone.clone.1 | custom fusion | bytes 24576 | tf_op jit(solution)/shard_map/jit(searchsorted)/jit(_searchsorted_scan_impl)/vmap(jit(_searchsorted_scan_impl))/while/body/eval_jaxpr/gather | solution.py:17
  197.6 11.5 %all-to-all-start = ((s32[128,16,2]{1,2,0:T(2,128)}), s32[128,16,2]{1,2,0:T(2,128)S(1)}, u32[]{:S(2)}, u32[]{:S(2)}) async-start(s32[128,16,2]{1,2,0:T(2,128)} %copy.40), calls=%async_computation | async-start | bytes 262144 | tf_op jit(solution)/shard_map/all_to_all | solution.py:110
  230.1 19.2 %all-to-all-done.1 = bf16[2048,2,128]{2,1,0:T(2,128)(2,1)S(1)} async-done(((bf16[2048,2,128]{2,1,0:T(2,128)(2,1)}), bf16[2048,2,128]{2,1,0:T(2,128)(2,1)S(1)}, u32[]{:S(2)}, u32[]{:S(2)}) %all-to-all-start.1) | async-done | bytes 1048608 | tf_op jit(solution)/shard_map/all_to_all | solution.py:103
  249.6 131.4 %while.39 = (s32[]{:T(128)}, f32[4,4]{1,0:T(4,128)S(1)}, bf16[4,4,256,128]{3,1,0,2:T(4,128)(2,1)}, f32[4,4,128,128]{3,2,1,0:T(8,128)}, s32[4]{0:T(128)S(1)}, /*i...) while((s32[]{:T(128)}, f32[4,4]{1,0:T(4,128)S(1)}, ...), condition=%wide.region_12.13_spmd, body=%wide.region_6.12_spmd.sunk | while | flops 3156365312 | bytes 54909272 | solution.py:70
  269.5 10.3 %fusion.59 = f32[4,256,128]{2,1,0:T(8,128)S(1)} fusion(f32[4,256,4096]{2,1,0:T(8,128)} %get-tuple-element.331, f32[4,256]{1,0:T(4,128)S(1)} %get-tuple-element.335, s32[4,256]{1,0:T(4,128)S(1)} %get-tuple-element.333, f32[4,256]{1,0:T(4,128)S(1)} %get-tuple-element.332, f32[4,4096]{1,0:T(4,128)S(1)} %convert_log_fusion.2, ...), kind=kOutput, calls=%fused_computation.14.clone.1 | convolution fusion | flops 1105199104 | bytes 17444864 | tf_op jit(solution)/shard_map/while/body/eval_jaxpr/cqs,csi->cqi/dot_general | solution.py:43
  302.3 10.3 %fusion.59 = f32[4,256,128]{2,1,0:T(8,128)S(1)} fusion(f32[4,256,4096]{2,1,0:T(8,128)} %get-tuple-element.331, f32[4,256]{1,0:T(4,128)S(1)} %get-tuple-element.335, s32[4,256]{1,0:T(4,128)S(1)} %get-tuple-element.333, f32[4,256]{1,0:T(4,128)S(1)} %get-tuple-element.332, f32[4,4096]{1,0:T(4,128)S(1)} %convert_log_fusion.2, ...), kind=kOutput, calls=%fused_computation.14.clone.1 | convolution fusion | flops 1105199104 | bytes 17444864 | tf_op jit(solution)/shard_map/while/body/eval_jaxpr/cqs,csi->cqi/dot_general | solution.py:43
  335.2 10.3 %fusion.59 = f32[4,256,128]{2,1,0:T(8,128)S(1)} fusion(f32[4,256,4096]{2,1,0:T(8,128)} %get-tuple-element.331, f32[4,256]{1,0:T(4,128)S(1)} %get-tuple-element.335, s32[4,256]{1,0:T(4,128)S(1)} %get-tuple-element.333, f32[4,256]{1,0:T(4,128)S(1)} %get-tuple-element.332, f32[4,4096]{1,0:T(4,128)S(1)} %convert_log_fusion.2, ...), kind=kOutput, calls=%fused_computation.14.clone.1 | convolution fusion | flops 1105199104 | bytes 17444864 | tf_op jit(solution)/shard_map/while/body/eval_jaxpr/cqs,csi->cqi/dot_general | solution.py:43
  368.0 10.3 %fusion.59 = f32[4,256,128]{2,1,0:T(8,128)S(1)} fusion(f32[4,256,4096]{2,1,0:T(8,128)} %get-tuple-element.331, f32[4,256]{1,0:T(4,128)S(1)} %get-tuple-element.335, s32[4,256]{1,0:T(4,128)S(1)} %get-tuple-element.333, f32[4,256]{1,0:T(4,128)S(1)} %get-tuple-element.332, f32[4,4096]{1,0:T(4,128)S(1)} %convert_log_fusion.2, ...), kind=kOutput, calls=%fused_computation.14.clone.1 | convolution fusion | flops 1105199104 | bytes 17444864 | tf_op jit(solution)/shard_map/while/body/eval_jaxpr/cqs,csi->cqi/dot_general | solution.py:43
  386.7 18.4 %all-to-all-done.2 = bf16[16,256,128]{2,0,1:T(8,128)(2,1)S(1)} async-done(((bf16[16,256,128]{2,0,1:T(8,128)(2,1)}), bf16[16,256,128]{2,0,1:T(8,128)(2,1)S(1)}, u32[]{:S(2)}, u32[]{:S(2)}) %all-to-all-start.2) | async-done | bytes 1048608 | tf_op jit(solution)/shard_map/all_to_all | solution.py:117
  421.3 147.0 %all-reduce.3.cloned.1.call-done = (f32[1024,512]{0,1:T(8,128)}, f32[512,128]{1,0:T(8,128)}) async-done(((f32[1024,512]{0,1:T(8,128)}, f32[512,128]{1,0:T(8,128)}), (f32[1024,512]{0,1:T(8,128)}, f32[512,128]{1,0:T(8,128)})) %all-reduce.3.cloned.1.call-update) | async-done | bytes 2359312 | tf_op jit(solution)/shard_map/psum | solution.py:126
  (161 shorter events, 161.1 us)
Async XLA Ops:
  7.2 201.9 %copy-start = (bf16[512,1024]{1,0:T(8,128)(2,1)S(1)}, bf16[512,1024]{1,0:T(8,128)(2,1)}, u32[]{:S(2)}) copy-start(bf16[512,1024]{1,0:T(8,128)(2,1)} %param.13) | copy-start | bytes 3145732
  35.6 151.1 %copy-start.6 = (s32[512,4]{0,1:T(4,128)S(1)}, s32[512,4]{0,1:T(4,128)}, u32[]{:S(2)}) copy-start(s32[512,4]{0,1:T(4,128)} %param.21) | copy-start | bytes 24580
  35.6 177.3 %copy-start.3 = (bf16[512,128]{1,0:T(8,128)(2,1)S(1)}, bf16[512,128]{1,0:T(8,128)(2,1)}, u32[]{:S(2)}) copy-start(bf16[512,128]{1,0:T(8,128)(2,1)} %param.15) | copy-start | bytes 393220
  178.0 71.5 %copy-start.1 = (bf16[2048,128]{1,0:T(8,128)(2,1)S(1)}, bf16[2048,128]{1,0:T(8,128)(2,1)}, u32[]{:S(2)}) copy-start(bf16[2048,128]{1,0:T(8,128)(2,1)} %param.16) | copy-start | bytes 1572868
  186.7 62.9 %copy-start.5 = (s32[2048]{0:T(1024)}, s32[2048]{0:T(1024)S(1)}, u32[]{:S(2)}) copy-start(s32[2048]{0:T(1024)S(1)} %get-tuple-element.231) | copy-start | bytes 24580
  197.6 22.6 %all-to-all-start = ((s32[128,16,2]{1,2,0:T(2,128)}), s32[128,16,2]{1,2,0:T(2,128)S(1)}, u32[]{:S(2)}, u32[]{:S(2)}) async-start(s32[128,16,2]{1,2,0:T(2,128)} %copy.40), calls=%async_computation | async-start | bytes 262144 | tf_op jit(solution)/shard_map/all_to_all | solution.py:110
  212.1 0.8 copy-start.2
  220.2 29.0 %all-to-all-start.1 = ((bf16[2048,2,128]{2,1,0:T(2,128)(2,1)}), bf16[2048,2,128]{2,1,0:T(2,128)(2,1)S(1)}, u32[]{:S(2)}, u32[]{:S(2)}) async-start(bf16[2048,2,128]{2,1,0:T(2,128)(2,1)} %bitcast.8), calls=%async_computation.1 | async-start | bytes 2097152 | tf_op jit(solution)/shard_map/all_to_all | solution.py:103
  249.6 136.1 %copy-start.7 = (pred[2048]{0:T(1024)(128)(4,1)S(1)}, pred[2048]{0:T(1024)(128)(4,1)}, u32[]{:S(2)}) copy-start(pred[2048]{0:T(1024)(128)(4,1)} %get-tuple-element.230) | copy-start | bytes 6148
  249.6 167.5 %copy-start.4 = (bf16[512,128]{1,0:T(8,128)(2,1)S(1)}, bf16[512,128]{1,0:T(8,128)(2,1)}, u32[]{:S(2)}) copy-start(bf16[512,128]{1,0:T(8,128)(2,1)} %param.15) | copy-start | bytes 393220
  381.0 24.0 %all-to-all-start.2 = ((bf16[16,256,128]{2,0,1:T(8,128)(2,1)}), bf16[16,256,128]{2,0,1:T(8,128)(2,1)S(1)}, u32[]{:S(2)}, u32[]{:S(2)}) async-start(bf16[16,256,128]{2,0,1:T(8,128)(2,1)} %bitcast.58), calls=%async_computation.2 | async-start | bytes 2097152 | tf_op jit(solution)/shard_map/all_to_all | solution.py:117
  385.6 182.7 %all-reduce.3.cloned.1.call-start = ((), (), s32[]{:S(2)}) async-start(), calls=%async_computation.3 | async-start | bytes 4718592 | tf_op jit(solution)/shard_map/psum | solution.py:126
Sparse Core Ops, SparseCore 0:
  420.8 147.4 all-reduce.2
where the time goes:
time: 581 us; the launch traced here: 580 us
  local copies, waits for them, and re-layouts  215 us (37%)
  waiting for transfers between devices  185 us (32%)
  matrix products  87.4 us (15%)
  other arithmetic  49.4 us (9%)
  starting transfers between devices  25.9 us (4%)
  between operations  14.3 us (2%)
    psum x1, waiting for transfers between devices, local(): grad_hidden, grad_out = lax.psum((local_hidden, local_out), 'dev')  147 us
    gather x12, local copies, waits for them, and re-layouts, slot_ranks(): first = jnp.searchsorted(sorted_keys, sorted_keys, side='left')  141 us
    dot_general x4, matrix products, score_block(): jnp.einsum('cqs,csi->cqi', weight, picks, preferred_element_type=jnp.floa...  41.3 us
    reduce_sum x4, other arithmetic, score_block(): total = jnp.sum(expo, axis=2, keepdims=True)  35.3 us
    dot_general x4, matrix products, score_block(): jnp.einsum('cqe,cse->cqs', queries, table, preferred_element_type=jnp.flo...  30.2 us
    all_to_all x1, waiting for transfers between devices, local(): lax.all_to_all(send_query.reshape(clusters, capacity, width), 'dev', spli...  19.2 us
    all_to_all x1, waiting for transfers between devices, local(): lax.all_to_all(dq_all, 'dev', split_axis=1, concat_axis=0, tiled=True)  18.4 us
    gather x1, local copies, waits for them, and re-layouts, slot_ranks(): sorted_keys = keys[order]  11.8 us
  transfers between devices with their start and end apart: 4, of which 3 were waited for; matrix products, arithmetic and copies ran while one was open for 2% of the time, Pallas kernels for 0%

commit v1 on v0

v1 whole, which is shorter than its diff:
```python
import jax
import jax.numpy as jnp
from jax import lax
from jax.experimental import pallas as pl
from jax.experimental.pallas import tpu as pltpu
from jax.sharding import PartitionSpec as P

F32 = jnp.float32
BF16 = jnp.bfloat16
NONE = -3.0e38
KEY = 4096
LANES = 128


def vmem(count):
    return [pl.BlockSpec(memory_space=pltpu.VMEM)] * count


def params(megabytes):
    return pltpu.CompilerParams(vmem_limit_bytes=megabytes << 20)


def iota(shape, axis):
    return lax.broadcasted_iota(jnp.int32, shape, axis)


def one_hot(mask):
    return jnp.where(mask, 1.0, 0.0).astype(BF16)


def mm(a, b, dims=((1,), (0,))):
    return lax.dot_general(a, b, (dims, ((), ())), preferred_element_type=F32)


def route_body(
    routes_ref, pos_ref, cslot_ref, feat_ref, wh_ref, wo_ref, send_ref, place_ref, pre_ref, tail_ref
):
    users = routes_ref.shape[1]
    visits = routes_ref.shape[0]
    clusters = cslot_ref.shape[0] * LANES
    devices, rows, width = send_ref.shape
    local = clusters // devices
    cslot = cslot_ref[...]
    high = ((cslot >> 6) << 6).astype(F32).astype(BF16)
    low = (cslot & 63).astype(F32).astype(BF16)
    lane_at = iota((LANES, users), 0)
    row_at = iota((cslot.shape[0], users), 0)
    user_at = iota((1, users), 1)
    slots = []
    keys = []
    for r in range(visits):
        cluster = routes_ref[r : r + 1, :]
        pick = one_hot(lane_at == (cluster & (LANES - 1)))
        found = mm(high, pick) + mm(low, pick)
        slot = jnp.sum(jnp.where(row_at == (cluster >> 7), found, 0.0), axis=0, keepdims=True)
        slots.append(slot)
        keys.append((user_at * KEY + pos_ref[r : r + 1, :]).astype(F32))
    pre = mm(feat_ref[...], wh_ref[...])
    pre_ref[...] = pre
    hidden = (pre * jax.nn.sigmoid(pre)).astype(BF16)
    query = mm(hidden, wo_ref[...]).astype(BF16)
    block = LANES
    groups = block // local
    sub = iota((block, users), 0).astype(F32)
    lane_user = iota((block, users), 1).astype(F32)
    tail_lane = iota((block, LANES), 1)
    tail_row = iota((block, LANES), 0)
    tail_hit = ((tail_lane & (local - 1)) == (tail_row & (local - 1))) & (tail_lane < 4 * local)
    tail_kind = tail_lane // local
    for b in range(clusters // block):
        slot_at = sub + float(b * block)
        key = jnp.full((block, users), -1.0, F32)
        for r in range(visits):
            key = jnp.where(slot_at == slots[r], keys[r], key)
        most = jnp.max(key, axis=1, keepdims=True)
        least = jnp.min(jnp.where(key < 0.0, 3.0e38, key), axis=1, keepdims=True)
        some = most >= 0.0
        both = most > least
        first = jnp.where(some, least, -1.0)
        second = jnp.where(both, most, -1.0)
        ends = []
        parts = []
        for chosen in (first, second):
            user = jnp.floor(chosen * (1.0 / KEY))
            mark = chosen - user * KEY + 1.0
            mark = jnp.where(chosen < 0.0, 0.0, mark)
            top = jnp.floor(mark * (1.0 / 64.0))
            ends += [top, mark - top * 64.0]
            parts.append(jnp.where(lane_user == user, 1.0, 0.0).reshape(groups, local, users))
        place = jnp.concatenate(parts, axis=1).reshape(2 * block, users).astype(BF16)
        place_ref[b * 2 * block : (b + 1) * 2 * block, :] = place
        tail = jnp.where(
            tail_kind == 0,
            ends[0],
            jnp.where(tail_kind == 1, ends[1], jnp.where(tail_kind == 2, ends[2], ends[3])),
        )
        tail = jnp.where(tail_hit, tail, 0.0).reshape(groups, local, LANES)
        tail_ref[b * groups : (b + 1) * groups, :] = jnp.sum(tail, axis=1)
        sent = mm(place, query).astype(BF16)
        send_ref[b * groups : (b + 1) * groups, 0 : 2 * local, :] = sent.reshape(
            groups, 2 * local, width
        )
    tails = jnp.broadcast_to(tail_ref[...][:, None, :], (devices, rows - 2 * local, width))
    send_ref[:, 2 * local : rows, :] = tails.astype(BF16)


def route(routes, positives, cluster_slot, features, w_hidden, w_out, devices):
    users, visits = routes.shape
    clusters = cluster_slot.shape[0]
    width = w_out.shape[1]
    hid = w_hidden.shape[1]
    rows = 2 * clusters // devices + 8
    return pl.pallas_call(
        route_body,
        out_shape=(
            jax.ShapeDtypeStruct((devices, rows, width), BF16),
            jax.ShapeDtypeStruct((2 * clusters, users), BF16),
            jax.ShapeDtypeStruct((users, hid), F32),
        ),
        in_specs=vmem(6),
        out_specs=vmem(3),
        scratch_shapes=[pltpu.VMEM((devices, LANES), F32)],
        compiler_params=params(48),
        name="route",
    )(
        routes.T,
        positives.T,
        cluster_slot.reshape(clusters // LANES, LANES),
        features,
        w_hidden,
        w_out,
    )


def table_body(ids_ref, counts_ref, mass_ref, tabs_ref, inv_ref):
    total = ids_ref.shape[0]
    chunks = total // 16
    ids = ids_ref[...]
    counts = counts_ref[...]
    inv_ref[...] = 1.0 / counts.astype(F32)
    tabs_ref[:, 0:LANES] = (ids * 4096).astype(F32).astype(BF16)
    tabs_ref[:, LANES : 2 * LANES] = ((counts >> 6) << 6).astype(F32).astype(BF16)
    tabs_ref[:, 2 * LANES : 3 * LANES] = (counts & 63).astype(F32).astype(BF16)
    item_at = iota((LANES, LANES), 0)
    lane_at = iota((LANES, LANES), 1)
    mass_ref[...] = jnp.zeros_like(mass_ref)

    def cluster(k, carry):
        acc = jnp.zeros((LANES, LANES), F32)
        for h in range(chunks):
            at = k * chunks + h
            hit = item_at == ids_ref[pl.ds(at, 1), :]
            acc = acc + jnp.where(hit, inv_ref[pl.ds(at, 1), :], 0.0)
        column = jnp.sum(acc, axis=1, keepdims=True)
        mass_ref[...] = jnp.where(lane_at == k, column, mass_ref[...])
        return carry

    lax.fori_loop(0, 16, cluster, 0)


def tables(sample_ids, sample_counts):
    total = sample_ids.size // LANES
    return pl.pallas_call(
        table_body,
        out_shape=(
            jax.ShapeDtypeStruct((LANES, LANES), F32),
            jax.ShapeDtypeStruct((total, 3 * LANES), BF16),
        ),
        in_specs=vmem(2),
        out_specs=vmem(2),
        scratch_shapes=[pltpu.VMEM((total, LANES), F32)],
        compiler_params=params(16),
        cost_estimate=pl.CostEstimate(flops=30_000_000, bytes_accessed=1 << 20, transcendentals=0),
        name="tables",
    )(sample_ids.reshape(total, LANES), sample_counts.reshape(total, LANES))


def owner_body(
    got_ref, items_ref, mass_ref, tabs_ref, dq_ref, weight_ref, q_ref, loss_ref, got32_ref, dq32_ref
):
    devices, rows, width = got_ref.shape
    local = q_ref.shape[0]
    chunks = tabs_ref.shape[0] // local
    got32_ref[...] = got_ref[...].astype(F32).reshape(devices * rows, width)
    tail = got32_ref[pl.ds(2 * local, devices, stride=rows), :].T
    pairs = 2 * devices
    item_at = iota((LANES, pairs), 0)
    row_at = iota((chunks, pairs), 0)
    loss_lane = iota((1, LANES), 1)
    losses = jnp.zeros((1, LANES), F32)
    mass = mass_ref[...]
    for k in range(local):
        marks = []
        for c in range(2):
            top = tail[(2 * c) * local + k : (2 * c) * local + k + 1, :]
            low = tail[(2 * c + 1) * local + k : (2 * c + 1) * local + k + 1, :]
            marks.append(top * 64.0 + low)
        mark = jnp.concatenate(marks, axis=1)
        live = mark > 0.0
        target = jnp.where(live, mark - 1.0, 0.0).astype(jnp.int32)
        pick = one_hot(item_at == (target & (LANES - 1)))
        tab = tabs_ref[k * chunks : (k + 1) * chunks, :]
        found = (
            mm(tab[:, 0:LANES], pick)
            + mm(tab[:, LANES : 2 * LANES], pick)
            + mm(tab[:, 2 * LANES : 3 * LANES], pick)
        )
        packed = jnp.sum(
            jnp.where(row_at == (target >> 7), found, 0.0), axis=0, keepdims=True
        ).astype(jnp.int32)
        item = jnp.where(live, packed >> 12, -1)
        count = (packed & 4095).astype(F32)
        queries = jnp.concatenate(
            [
                got32_ref[pl.ds(k, devices, stride=rows), :],
                got32_ref[pl.ds(local + k, devices, stride=rows), :],
            ],
            axis=0,
        ).astype(BF16)
        q_ref[k] = queries
        block = items_ref[k * LANES : (k + 1) * LANES, :]
        column = mass[:, k : k + 1]
        scores = mm(block, queries, ((1,), (1,)))
        masked = jnp.where(column > 0.0, scores, NONE)
        top = jnp.max(masked, axis=0, keepdims=True)
        expo = jnp.exp(masked - top) * column
        total = jnp.sum(expo, axis=0, keepdims=True)
        hit = item_at == item
        picked = jnp.sum(jnp.where(hit, scores, 0.0), axis=0, keepdims=True)
        loss = jnp.log(total) + top - (picked - jnp.log(count))
        loss = jnp.sum(jnp.where(live, loss, 0.0), axis=1, keepdims=True) / jnp.sum(
            jnp.where(live, 1.0, 0.0), axis=1, keepdims=True
        )
        losses = jnp.where(loss_lane == k, loss, losses)
        weight = expo * (1.0 / total) - jnp.where(hit, 1.0, 0.0)
        high = weight.astype(BF16)
        low = (weight - high.astype(F32)).astype(BF16)
        weight_ref[k, :, 0:pairs] = high
        weight_ref[k, :, pairs : 2 * pairs] = low
        dq = mm(high, block, ((0,), (0,))) + mm(low, block, ((0,), (0,)))
        dq32_ref[pl.ds(k, devices, stride=2 * local), :] = dq[0:devices, :]
        dq32_ref[pl.ds(local + k, devices, stride=2 * local), :] = dq[devices:pairs, :]
    loss_ref[...] = losses
    dq_ref[...] = dq32_ref[...].reshape(devices, 2 * local, width).astype(BF16)


def owner(got, items, mass, tabs):
    devices, rows, width = got.shape
    local = items.shape[0] // LANES
    return pl.pallas_call(
        owner_body,
        out_shape=(
            jax.ShapeDtypeStruct((devices, 2 * local, width), BF16),
            jax.ShapeDtypeStruct((local, LANES, 4 * devices), BF16),
            jax.ShapeDtypeStruct((local, 2 * devices, width), BF16),
            jax.ShapeDtypeStruct((1, LANES), F32),
        ),
        in_specs=vmem(4),
        out_specs=vmem(4),
        scratch_shapes=[
            pltpu.VMEM((devices * rows, width), F32),
            pltpu.VMEM((devices * 2 * local, width), F32),
        ],
        compiler_params=params(40),
        name="owner",
    )(got, items, mass, tabs)


def item_body(weight_ref, q_ref, grad_ref):
    pairs = q_ref.shape[1]
    weight = weight_ref[0]
    queries = q_ref[0]
    grad_ref[...] = mm(weight[:, 0:pairs], queries) + mm(weight[:, pairs : 2 * pairs], queries)


def item_grads(weight, queries):
    local, pairs, width = queries.shape
    return pl.pallas_call(
        item_body,
        grid=(local,),
        out_shape=jax.ShapeDtypeStruct((local * LANES, width), F32),
        in_specs=[
            pl.BlockSpec((1, LANES, 2 * pairs), lambda k: (k, 0, 0)),
            pl.BlockSpec((1, pairs, width), lambda k: (k, 0, 0)),
        ],
        out_specs=pl.BlockSpec((LANES, width), lambda k: (k, 0)),
        compiler_params=params(8),
        cost_estimate=pl.CostEstimate(
            flops=270_000_000, bytes_accessed=4 << 20, transcendentals=0
        ),
        name="item_grads",
    )(weight, queries)


def tower_body(back_ref, place_ref, pre_ref, feat_ref, wo_ref, grad_ref):
    devices, rows, width = back_ref.shape
    back = back_ref[...].reshape(devices * rows, width)
    dq_t = mm(back, place_ref[...], ((0,), (0,))).astype(BF16)
    pre = pre_ref[...]
    sig = jax.nn.sigmoid(pre)
    hidden = (pre * sig).astype(BF16)
    out_t = mm(dq_t, hidden)
    dhidden = mm(dq_t.astype(F32).T.astype(BF16), wo_ref[...], ((1,), (1,)))
    dpre = (dhidden * (sig * (1.0 + pre * (1.0 - sig)))).astype(BF16)
    big = mm(feat_ref[...], dpre)
    parts = [
        big[:, c * LANES : (c + 1) * LANES].reshape(devices, 8, LANES)
        for c in range(big.shape[1] // LANES)
    ]
    for c in range(0, len(parts), 2):
        grad_ref[:, c * 8 : c * 8 + 16, :] = jnp.concatenate(parts[c : c + 2], axis=1).astype(BF16)
    small = out_t.T
    filled = small.shape[0] // 8
    at = len(parts) * 8
    grad_ref[0:filled, at : at + 8, :] = small.reshape(filled, 8, LANES).astype(BF16)
    grad_ref[filled:devices, at : at + 8, :] = jnp.zeros((devices - filled, 8, LANES), BF16)


def tower_back(back, place, pre, features_t, w_out):
    devices = back.shape[0]
    rows = (pre.shape[1] * features_t.shape[0] // devices) // LANES + 8
    return pl.pallas_call(
        tower_body,
        out_shape=jax.ShapeDtypeStruct((devices, rows, LANES), BF16),
        in_specs=vmem(5),
        out_specs=vmem(1)[0],
        compiler_params=params(48),
        name="tower_back",
    )(back, place, pre, features_t, w_out)


def sum_body(parts_ref, out_ref):
    total = jnp.sum(parts_ref[...].astype(F32), axis=0, keepdims=True)
    out_ref[...] = jnp.broadcast_to(total, out_ref.shape).astype(BF16)


def sum_parts(parts):
    return pl.pallas_call(
        sum_body,
        out_shape=jax.ShapeDtypeStruct(parts.shape, BF16),
        in_specs=vmem(1),
        out_specs=vmem(1)[0],
        compiler_params=params(24),
        name="sum_parts",
    )(parts)


def spread_body(in_ref, hidden_ref, out_ref):
    devices = in_ref.shape[0]
    got = in_ref[...].astype(F32)
    blocks = hidden_ref.shape[1] // LANES
    for c in range(blocks):
        hidden_ref[:, c * LANES : (c + 1) * LANES] = got[:, c * 8 : c * 8 + 8, :].reshape(
            devices * 8, LANES
        )
    filled = out_ref.shape[0] // 8
    out_ref[...] = got[0:filled, blocks * 8 : blocks * 8 + 8, :].reshape(out_ref.shape)


def spread(summed, hidden_shape, out_shape):
    return pl.pallas_call(
        spread_body,
        out_shape=(
            jax.ShapeDtypeStruct(hidden_shape, F32),
            jax.ShapeDtypeStruct(out_shape, F32),
        ),
        in_specs=vmem(1),
        out_specs=vmem(2),
        compiler_params=params(24),
        name="spread",
    )(summed)


def exchange(x):
    return lax.all_to_all(x, "dev", split_axis=0, concat_axis=0, tiled=True)


def local(
    features, w_hidden, w_out, items, routes, cluster_slot, sample_ids, sample_counts, positives
):
    devices = lax.axis_size("dev")
    send, place, pre = route(routes, positives, cluster_slot, features, w_hidden, w_out, devices)
    mass, tabs = tables(sample_ids, sample_counts)
    features_t = features.T
    got = exchange(send)
    dq, weight, queries, losses = owner(got, items, mass, tabs)
    back = exchange(dq)
    item_grad = item_grads(weight, queries)
    partial = tower_back(back, place, pre, features_t, w_out)
    summed = sum_parts(exchange(partial))
    grad_hidden, grad_out = spread(exchange(summed), w_hidden.shape, w_out.shape)
    slot_loss = losses[0, : sample_ids.shape[0]]
    return (slot_loss, grad_hidden, grad_out, item_grad)


def solution(mesh):
    in_specs = (
        P("dev", None),
        P(),
        P(),
        P("dev", None),
        P("dev", None),
        P(),
        P("dev", None),
        P("dev", None),
        P("dev", None),
    )
    out_specs = (P("dev"), P(), P(), P("dev", None))
    return jax.shard_map(local, mesh=mesh, in_specs=in_specs, out_specs=out_specs, check_vma=False)
```

time: 581 us -> 145 us (0.25)
  local copies, waits for them, and re-layouts: 215 us -> 13.3 us
  waiting for transfers between devices: 185 us -> 48.9 us
  matrix products: 87.4 us -> 0 us
  other arithmetic: 49.4 us -> 0 us
  Pallas kernels: 0 us -> 33.9 us
  blocking collectives: 0 us -> 26.4 us
  between operations: 14.3 us -> 0.78 us
    gather x15 -> x0, local copies, waits for them, and re-layouts: 170 us -> none  [the longest x12 141 us: slot_ranks(): first = jnp.searchsorted(sorted_keys, sorted_keys, side='left')]
    psum x1 -> x0, waiting for transfers between devices: 147 us -> none  [local(): grad_hidden, grad_out = lax.psum((local_hidden, local_out), 'dev')]
    dot_general x20 -> x0, matrix products: 87.4 us -> none  [the longest x4 41.3 us: score_block(): jnp.einsum('cqs,csi->cqi', weight, picks, preferred_element_type=jnp.floa...]
    reduce_sum x9 -> x0, other arithmetic: 38.8 us -> none  [the longest x4 35.3 us: score_block(): total = jnp.sum(expo, axis=2, keepdims=True)]
    pallas_call x0 -> x7, Pallas kernels: none -> 33.9 us  [the longest x1 7.44 us: owner(): pl.pallas_call(owner_body, out_shape=(jax.ShapeDtypeStruct((devices, 2 *...]
    all_to_all x0 -> x1, blocking collectives: none -> 26.4 us  [exchange(): return lax.all_to_all(x, 'dev', split_axis=0, concat_axis=0, tiled=True)]
    scatter x3 -> x0, local copies, waits for them, and re-layouts: 22.9 us -> none  [the longest x1 8.06 us: local(): jnp.full((clusters * capacity,), -1, jnp.int32).at[place]]
    all_to_all x3, waiting for transfers between devices: 37.5 us -> 48.9 us  [exchange(): return lax.all_to_all(x, 'dev', split_axis=0, concat_axis=0, tiled=True)]
  transfers between devices with their start and end apart: 4 -> 3, of which waited for: 3 -> 3; matrix products, arithmetic and copies ran while one was open for 2% -> 1% of each run, Pallas kernels for 0% -> 9%
where the time goes in v1:
time: 145 us; the launch traced here: 144 us
  waiting for transfers between devices  48.9 us (34%)
  Pallas kernels  33.9 us (23%)
  blocking collectives  26.4 us (18%)
  starting transfers between devices  20.9 us (14%)
  local copies, waits for them, and re-layouts  13.3 us (9%)
    all_to_all x3, waiting for transfers between devices, exchange(): return lax.all_to_all(x, 'dev', split_axis=0, concat_axis=0, tiled=True)  48.9 us
    all_to_all x1, blocking collectives, exchange(): return lax.all_to_all(x, 'dev', split_axis=0, concat_axis=0, tiled=True)  26.4 us
    all_to_all x3, starting transfers between devices, exchange(): return lax.all_to_all(x, 'dev', split_axis=0, concat_axis=0, tiled=True)  20.9 us
    unnamed x37, local copies, waits for them, and re-layouts  12.7 us
    pallas_call x1, Pallas kernels, owner(): pl.pallas_call(owner_body, out_shape=(jax.ShapeDtypeStruct((devices, 2 *...  7.44 us
    pallas_call x1, Pallas kernels, route(): pl.pallas_call(route_body, out_shape=(jax.ShapeDtypeStruct((devices, rows...  7.12 us
    pallas_call x1, Pallas kernels, item_grads(): pl.pallas_call(item_body, grid=(local,), out_shape=jax.ShapeDtypeStruct((...  6.59 us
    pallas_call x1, Pallas kernels, tables(): pl.pallas_call(table_body, out_shape=(jax.ShapeDtypeStruct((LANES, LANES)...  5.8 us
  transfers between devices with their start and end apart: 3, of which 3 were waited for; matrix products, arithmetic and copies ran while one was open for 1% of the time, Pallas kernels for 9%

profile of v1, /device:TPU:1, one launch (start us, length us, event | category | flops | bytes accessed | tf_op | source)
XLA Modules:
  0.0 144.2 jit_solution(13400609182360454231)
XLA Ops:
  0.6 1.2 copy-done
  1.9 1.2 copy-done.6
  3.1 0.9 copy-done.10
  4.0 0.7 copy-done.13
  6.1 7.1 %route.1 = (bf16[128,40,128]{2,1,0:T(8,128)(2,1)}, bf16[4096,512]{1,0:T(8,128)(2,1)}, f32[512,512]{1,0:T(8,128)S(1)}) custom-call(s32[4,512]{1,0:T(4,128)S(1)} %bitcast.7, s32[4,512]{1,0:T(4,128)S(1)} %bitcast.8, s32[16,128]{1,0:T(8,128)S(1)} %bitcast.9, bf16[512,1024]{1,0:T(8,128)(2,1)S(1)} %copy-done, bf16[1024,512]{1,0:T(8,128)(2,1)S(1)} %copy-done.6, ...), custom_call_target="tpu_custom_call" | custom-call | tf_op jit(solution)/shard_map/route/pallas_call | solution.py:113
  13.2 1.0 copy-done.4
  14.2 11.5 %all-to-all-start = ((bf16[128,40,128]{2,1,0:T(8,128)(2,1)}), bf16[128,40,128]{2,1,0:T(8,128)(2,1)S(1)}, u32[]{:S(2)}, u32[]{:S(2)}) async-start(bf16[128,40,128]{2,1,0:T(8,128)(2,1)} %get-tuple-element.15), calls=%async_computation | async-start | bytes 2621440 | tf_op jit(solution)/shard_map/all_to_all | solution.py:375
  25.8 5.8 %tables.1 = (f32[128,128]{1,0:T(8,128)S(1)}, bf16[512,384]{1,0:T(8,128)(2,1)S(1)}) custom-call(s32[512,128]{1,0:T(8,128)S(1)} %reshape.18.ids_ref, s32[512,128]{1,0:T(8,128)S(1)} %reshape.19.counts_ref), custom_call_target="tpu_custom_call" | custom-call | flops 30000000 | bytes 1048576 | tf_op jit(solution)/shard_map/tables/pallas_call | solution.py:163
  31.6 16.1 %all-to-all-done.got_ref = bf16[128,40,128]{2,1,0:T(8,128)(2,1)S(1)} async-done(((bf16[128,40,128]{2,1,0:T(8,128)(2,1)}), bf16[128,40,128]{2,1,0:T(8,128)(2,1)S(1)}, u32[]{:S(2)}, u32[]{:S(2)}) %all-to-all-start) | async-done | bytes 1310752 | tf_op jit(solution)/shard_map/all_to_all | solution.py:375
  47.8 7.4 %owner.1 = (bf16[128,32,128]{2,1,0:T(8,128)(2,1)S(1)}, bf16[16,128,512]{2,1,0:T(8,128)(2,1)S(1)}, bf16[16,256,128]{2,1,0:T(8,128)(2,1)S(1)}, f32[1,128]{1,0:T(1,128)S(1)}) custom-call(bf16[128,40,128]{2,1,0:T(8,128)(2,1)S(1)} %all-to-all-done.got_ref, bf16[2048,128]{1,0:T(8,128)(2,1)S(1)} %copy-done.12, f32[128,128]{1,0:T(8,128)S(1)} %get-tuple-element.16.mass_ref, ...), custom_call_target="tpu_custom_call" | custom-call | tf_op jit(solution)/shard_map/owner/pallas_call | solution.py:250
  55.2 1.3 copy-done.2
  56.5 1.0 copy-done.7
  57.5 1.0 copy-done.8
  58.5 4.7 %all-to-all-start.1 = ((bf16[128,32,128]{2,1,0:T(8,128)(2,1)}), bf16[128,32,128]{2,1,0:T(8,128)(2,1)S(1)}, u32[]{:S(2)}, u32[]{:S(2)}) async-start(bf16[128,32,128]{2,1,0:T(8,128)(2,1)} %copy-done.7), calls=%async_computation.1 | async-start | bytes 2097152 | tf_op jit(solution)/shard_map/all_to_all | solution.py:375
  63.8 18.8 %all-to-all-done.1.back_ref = bf16[128,32,128]{2,1,0:T(8,128)(2,1)S(1)} async-done(((bf16[128,32,128]{2,1,0:T(8,128)(2,1)}), bf16[128,32,128]{2,1,0:T(8,128)(2,1)S(1)}, u32[]{:S(2)}, u32[]{:S(2)}) %all-to-all-start.1) | async-done | bytes 1048608 | tf_op jit(solution)/shard_map/all_to_all | solution.py:375
  82.7 1.2 copy-done.5
  83.9 4.0 %tower_back.1 = bf16[128,40,128]{2,1,0:T(8,128)(2,1)S(1)} custom-call(bf16[128,32,128]{2,1,0:T(8,128)(2,1)S(1)} %all-to-all-done.1.back_ref, bf16[4096,512]{1,0:T(8,128)(2,1)} %get-tuple-element.20.place_ref, f32[512,512]{1,0:T(8,128)S(1)} %copy-done.5, bf16[1024,512]{1,0:T(8,128)(2,1)S(1)} %bitcast.6, bf16[512,128]{1,0:T(8,128)(2,1)S(1)} %copy-done.11), custom_call_target="tpu_custom_call" | custom-call | tf_op jit(solution)/shard_map/tower_back/pallas_call | solution.py:322
  87.8 26.4 %all_to_all.20.parts_ref = bf16[128,40,128]{2,1,0:T(8,128)(2,1)S(1)} all-to-all(bf16[128,40,128]{2,1,0:T(8,128)(2,1)S(1)} %tower_back.1), channel_id=1, replica_groups=mesh['dev'=128] {'dev'}, dimensions={0} | all-to-all | bytes 2621440 | tf_op jit(solution)/shard_map/all_to_all | solution.py:375
  114.2 1.4 sum_parts.1
  115.6 4.7 %all-to-all-start.3 = ((bf16[128,40,128]{2,1,0:T(8,128)(2,1)}), bf16[128,40,128]{2,1,0:T(8,128)(2,1)S(1)}, u32[]{:S(2)}, u32[]{:S(2)}) async-start(bf16[128,40,128]{2,1,0:T(8,128)(2,1)} %sum_parts.1), calls=%async_computation.3 | async-start | bytes 2621440 | tf_op jit(solution)/shard_map/all_to_all | solution.py:375
  120.3 1.2 copy-done.9
  121.5 6.6 %item_grads.1 = f32[2048,128]{1,0:T(8,128)} custom-call(bf16[16,128,512]{2,1,0:T(8,128)(2,1)S(1)} %copy-done.3, bf16[16,256,128]{2,1,0:T(8,128)(2,1)S(1)} %copy-done.9), custom_call_target="tpu_custom_call" | custom-call | flops 270000000 | bytes 4194304 | tf_op jit(solution)/shard_map/item_grads/pallas_call | solution.py:278
  128.6 13.9 %all-to-all-done.3.in_ref = bf16[128,40,128]{2,1,0:T(8,128)(2,1)S(1)} async-done(((bf16[128,40,128]{2,1,0:T(8,128)(2,1)}), bf16[128,40,128]{2,1,0:T(8,128)(2,1)S(1)}, u32[]{:S(2)}, u32[]{:S(2)}) %all-to-all-start.3) | async-done | bytes 1310752 | tf_op jit(solution)/shard_map/all_to_all | solution.py:375
  142.5 1.7 %spread.1 = (f32[1024,512]{1,0:T(8,128)}, f32[512,128]{1,0:T(8,128)}) custom-call(bf16[128,40,128]{2,1,0:T(8,128)(2,1)S(1)} %all-to-all-done.3.in_ref), custom_call_target="tpu_custom_call" | custom-call | tf_op jit(solution)/shard_map/spread/pallas_call | solution.py:361
  (30 shorter events, 2.6 us)
Async XLA Ops:
  0.6 1.2 copy-start
  1.9 1.2 copy-start.6
  3.1 0.9 copy-start.10
  4.0 0.7 copy-start.13
  4.7 0.7 copy-start.14
  5.4 0.7 copy-start.15
  13.2 1.0 copy-start.4
  14.2 11.5 %copy-start.16 = (s32[16,4096]{1,0:T(8,128)S(1)}, s32[16,4096]{1,0:T(8,128)}, u32[]{:S(2)}) copy-start(s32[16,4096]{1,0:T(8,128)} %param.15) | copy-start | bytes 786436
  14.2 11.6 %copy-start.17 = (s32[16,4096]{1,0:T(8,128)S(1)}, s32[16,4096]{1,0:T(8,128)}, u32[]{:S(2)}) copy-start(s32[16,4096]{1,0:T(8,128)} %param.16) | copy-start | bytes 786436
  14.2 33.6 %all-to-all-start = ((bf16[128,40,128]{2,1,0:T(8,128)(2,1)}), bf16[128,40,128]{2,1,0:T(8,128)(2,1)S(1)}, u32[]{:S(2)}, u32[]{:S(2)}) async-start(bf16[128,40,128]{2,1,0:T(8,128)(2,1)} %get-tuple-element.15), calls=%async_computation | async-start | bytes 2621440 | tf_op jit(solution)/shard_map/all_to_all | solution.py:375
  25.7 22.1 %copy-start.12 = (bf16[2048,128]{1,0:T(8,128)(2,1)S(1)}, bf16[2048,128]{1,0:T(8,128)(2,1)}, u32[]{:S(2)}) copy-start(bf16[2048,128]{1,0:T(8,128)(2,1)} %items_ref.1) | copy-start | bytes 1572868
  55.2 1.3 copy-start.2
  56.5 1.0 copy-start.7
  57.5 1.0 copy-start.8
  58.5 4.7 %copy-start.1 = (bf16[512,1024]{1,0:T(8,128)(2,1)S(1)}, bf16[512,1024]{1,0:T(8,128)(2,1)}, u32[]{:S(2)}) copy-start(bf16[512,1024]{1,0:T(8,128)(2,1)} %feat_ref.1) | copy-start | bytes 3145732
  58.5 24.1 %all-to-all-start.1 = ((bf16[128,32,128]{2,1,0:T(8,128)(2,1)}), bf16[128,32,128]{2,1,0:T(8,128)(2,1)S(1)}, u32[]{:S(2)}, u32[]{:S(2)}) async-start(bf16[128,32,128]{2,1,0:T(8,128)(2,1)} %copy-done.7), calls=%async_computation.1 | async-start | bytes 2097152 | tf_op jit(solution)/shard_map/all_to_all | solution.py:375
  63.2 19.4 %copy-start.11 = (bf16[512,128]{1,0:T(8,128)(2,1)S(1)}, bf16[512,128]{1,0:T(8,128)(2,1)}, u32[]{:S(2)}) copy-start(bf16[512,128]{1,0:T(8,128)(2,1)} %wo_ref.3) | copy-start | bytes 393220
  82.7 1.2 copy-start.5
  115.6 4.7 %copy-start.3 = (bf16[16,128,512]{2,1,0:T(8,128)(2,1)S(1)}, bf16[16,128,512]{2,1,0:T(8,128)(2,1)}, u32[]{:S(2)}) copy-start(bf16[16,128,512]{2,1,0:T(8,128)(2,1)} %copy-done.2) | copy-start | bytes 6291460
  115.6 27.0 %all-to-all-start.3 = ((bf16[128,40,128]{2,1,0:T(8,128)(2,1)}), bf16[128,40,128]{2,1,0:T(8,128)(2,1)S(1)}, u32[]{:S(2)}, u32[]{:S(2)}) async-start(bf16[128,40,128]{2,1,0:T(8,128)(2,1)} %sum_parts.1), calls=%async_computation.3 | async-start | bytes 2621440 | tf_op jit(solution)/shard_map/all_to_all | solution.py:375
  120.3 1.2 copy-start.9

commit v2 on v1

v2 whole, which is shorter than its diff:
```python
import jax
import jax.numpy as jnp
from jax import lax
from jax.experimental import pallas as pl
from jax.experimental.pallas import tpu as pltpu
from jax.sharding import PartitionSpec as P

F32 = jnp.float32
BF16 = jnp.bfloat16
NONE = -3.0e38
KEY = 4096
LANES = 128


def vmem(count):
    return [pl.BlockSpec(memory_space=pltpu.VMEM)] * count


def in_hbm(arrays):
    return tuple(pltpu.with_memory_space_constraint(a, pltpu.HBM) for a in arrays)


def outs_hbm(arrays):
    return tuple(pltpu.HBM(a.shape, a.dtype) for a in arrays)


def hbm(count):
    return [pl.BlockSpec(memory_space=pltpu.HBM)] * count


def params(megabytes):
    return pltpu.CompilerParams(vmem_limit_bytes=megabytes << 20)


def iota(shape, axis):
    return lax.broadcasted_iota(jnp.int32, shape, axis)


def one_hot(mask):
    return jnp.where(mask, 1.0, 0.0).astype(BF16)


def mm(a, b, dims=((1,), (0,))):
    return lax.dot_general(a, b, (dims, ((), ())), preferred_element_type=F32)


def route_body(
    routes_hbm,
    pos_hbm,
    cslot_hbm,
    feat_hbm,
    wh_hbm,
    wo_hbm,
    send_hbm,
    place_hbm,
    mine_hbm,
    other_hbm,
    routes_ref,
    pos_ref,
    cslot_ref,
    feat_ref,
    wh_ref,
    wo_ref,
    send_ref,
    place_ref,
    mine_ref,
    other_ref,
    in_sem,
    out_sem,
    send_sem,
    place_sem,
):
    loads = [
        pltpu.make_async_copy(src, dst, in_sem.at[i])
        for i, (src, dst) in enumerate(
            [
                (routes_hbm, routes_ref),
                (pos_hbm, pos_ref),
                (cslot_hbm, cslot_ref),
                (feat_hbm, feat_ref),
                (wh_hbm, wh_ref),
                (wo_hbm, wo_ref),
            ]
        )
    ]
    for load in loads:
        load.start()
    visits, users = routes_ref.shape
    clusters = cslot_ref.shape[0] * LANES
    devices, rows, width = send_ref.shape
    local = clusters // devices
    for load in loads[:3]:
        load.wait()
    cslot = cslot_ref[...]
    high = ((cslot >> 6) << 6).astype(F32).astype(BF16)
    low = (cslot & 63).astype(F32).astype(BF16)
    lane_at = iota((LANES, users), 0)
    row_at = iota((cslot.shape[0], users), 0)
    user_at = iota((1, users), 1)
    slots = []
    keys = []
    for r in range(visits):
        cluster = routes_ref[r : r + 1, :]
        pick = one_hot(lane_at == (cluster & (LANES - 1)))
        found = mm(high, pick) + mm(low, pick)
        slot = jnp.sum(jnp.where(row_at == (cluster >> 7), found, 0.0), axis=0, keepdims=True)
        slots.append(slot)
        keys.append((user_at * KEY + pos_ref[r : r + 1, :] + 1).astype(F32))
    for load in loads[3:]:
        load.wait()
    pre = mm(feat_ref[...], wh_ref[...])
    half = pre.shape[1] // 2
    core = lax.axis_index("dev") % 2
    mine_ref[...] = jnp.where(core == 0, pre[:, 0:half], pre[:, half:])
    other_ref[...] = jnp.where(core == 0, pre[:, half:], pre[:, 0:half])
    stores = [
        pltpu.make_async_copy(mine_ref, mine_hbm, out_sem.at[0]),
        pltpu.make_async_copy(other_ref, other_hbm, out_sem.at[1]),
    ]
    for store in stores:
        store.start()
    hidden = (pre * jax.nn.sigmoid(pre)).astype(BF16)
    query = mm(hidden, wo_ref[...]).astype(BF16)
    block = LANES
    groups = block // local
    sub = iota((block, users), 0).astype(F32)
    lane_user = iota((block, users), 1).astype(F32)
    tail_lane = iota((block, LANES), 1)
    tail_row = iota((block, LANES), 0)
    tail_hit = ((tail_lane & (local - 1)) == (tail_row & (local - 1))) & (tail_lane < 4 * local)
    tail_kind = tail_lane // local
    for b in range(clusters // block):
        slot_at = sub + float(b * block)
        key = jnp.zeros((block, users), F32)
        for r in range(visits):
            key = jnp.where(slot_at == slots[r], keys[r], key)
        most = jnp.max(key, axis=1, keepdims=True)
        rest = jnp.sum(key, axis=1, keepdims=True) - most
        ends = []
        parts = []
        for chosen in (most, rest):
            user = jnp.floor((chosen - 1.0) * (1.0 / KEY))
            mark = jnp.where(chosen > 0.0, chosen - user * KEY, 0.0)
            top = jnp.floor(mark * (1.0 / 64.0))
            ends += [top, mark - top * 64.0]
            parts.append(jnp.where(lane_user == user, 1.0, 0.0).reshape(groups, local, users))
        place = jnp.concatenate(parts, axis=1).reshape(2 * block, users).astype(BF16)
        span = pl.ds(b * 2 * block, 2 * block)
        place_ref[span, :] = place
        stores.append(
            pltpu.make_async_copy(place_ref.at[span, :], place_hbm.at[span, :], place_sem.at[b])
        )
        stores[-1].start()
        tail = jnp.where(
            tail_kind == 0,
            ends[0],
            jnp.where(tail_kind == 1, ends[1], jnp.where(tail_kind == 2, ends[2], ends[3])),
        )
        tail = jnp.where(tail_hit, tail, 0.0).reshape(groups, local, LANES)
        tail = jnp.sum(tail, axis=1)
        span = pl.ds(b * groups, groups)
        sent = mm(place, query).astype(BF16)
        send_ref[span, 0 : 2 * local, :] = sent.reshape(groups, 2 * local, width)
        send_ref[span, 2 * local : rows, :] = jnp.broadcast_to(
            tail[:, None, :], (groups, rows - 2 * local, width)
        ).astype(BF16)
        stores.append(pltpu.make_async_copy(send_ref.at[span], send_hbm.at[span], send_sem.at[b]))
        stores[-1].start()
    for store in stores:
        store.wait()


def route(routes, positives, cluster_slot, features, w_hidden, w_out, devices):
    users, visits = routes.shape
    clusters = cluster_slot.shape[0]
    width = w_out.shape[1]
    hid = w_hidden.shape[1]
    rows = 2 * clusters // devices + 8
    args = (
        routes.T,
        positives.T,
        cluster_slot.reshape(clusters // LANES, LANES),
        features,
        w_hidden,
        w_out,
    )
    outs = (
        jax.ShapeDtypeStruct((devices, rows, width), BF16),
        jax.ShapeDtypeStruct((2 * clusters, users), BF16),
        jax.ShapeDtypeStruct((users, hid // 2), F32),
        jax.ShapeDtypeStruct((users, hid // 2), F32),
    )
    return pl.pallas_call(
        route_body,
        out_shape=outs_hbm(outs),
        in_specs=hbm(6),
        out_specs=hbm(4),
        scratch_shapes=[pltpu.VMEM(a.shape, a.dtype) for a in args + outs]
        + [
            pltpu.SemaphoreType.DMA((6,)),
            pltpu.SemaphoreType.DMA((2,)),
            pltpu.SemaphoreType.DMA((clusters // LANES,)),
            pltpu.SemaphoreType.DMA((clusters // LANES,)),
        ],
        compiler_params=params(48),
        name="route",
    )(*in_hbm(args))


def table_body(ids_ref, counts_ref, mass_ref, tabs_ref, inv_ref):
    clusters = tabs_ref.shape[0]
    chunks = ids_ref.shape[0] // clusters
    ids = ids_ref[...]
    counts = counts_ref[...]
    inv_ref[...] = 1.0 / counts.astype(F32)
    digits = ((ids * 4096), ((counts >> 6) << 6), (counts & 63))
    for d, digit in enumerate(digits):
        tabs_ref[:, d * chunks : (d + 1) * chunks, :] = (
            digit.astype(F32).reshape(clusters, chunks, LANES).astype(BF16)
        )
    item_at = iota((LANES, LANES), 0)
    lane_at = iota((LANES, LANES), 1)
    mass_ref[...] = jnp.zeros_like(mass_ref)

    def cluster(k, carry):
        acc = jnp.zeros((LANES, LANES), F32)
        for h in range(chunks):
            at = k * chunks + h
            hit = item_at == ids_ref[pl.ds(at, 1), :]
            acc = acc + jnp.where(hit, inv_ref[pl.ds(at, 1), :], 0.0)
        column = jnp.sum(acc, axis=1, keepdims=True)
        mass_ref[...] = jnp.where(lane_at == k, column, mass_ref[...])
        return carry

    lax.fori_loop(0, clusters, cluster, 0)


def tables(sample_ids, sample_counts):
    clusters, samples = sample_ids.shape
    total = sample_ids.size // LANES
    return pl.pallas_call(
        table_body,
        out_shape=(
            jax.ShapeDtypeStruct((LANES, LANES), F32),
            jax.ShapeDtypeStruct((clusters, 3 * samples // LANES, LANES), BF16),
        ),
        in_specs=vmem(2),
        out_specs=vmem(2),
        scratch_shapes=[pltpu.VMEM((total, LANES), F32)],
        compiler_params=params(16),
        cost_estimate=pl.CostEstimate(flops=30_000_000, bytes_accessed=1 << 20, transcendentals=0),
        name="tables",
    )(sample_ids.reshape(total, LANES), sample_counts.reshape(total, LANES))


def owner_body(
    got_ref,
    items_ref,
    mass_ref,
    tabs_ref,
    dq_hbm,
    weight_hbm,
    q_hbm,
    loss_ref,
    got32_ref,
    dq32_ref,
    dq_ref,
    weight_ref,
    q_ref,
    dq_sem,
    weight_sem,
    q_sem,
):
    devices, rows, width = got_ref.shape
    local = q_ref.shape[0]
    chunks = tabs_ref.shape[1] // 3
    got32_ref[...] = got_ref[...].astype(F32).reshape(devices * rows, width)
    tail = got32_ref[pl.ds(2 * local, devices, stride=rows), :].T
    pairs = 2 * devices
    item_at = iota((LANES, pairs), 0)
    row_at = iota((chunks, pairs), 0)
    loss_lane = iota((1, LANES), 1)
    losses = jnp.zeros((1, LANES), F32)
    mass = mass_ref[...]
    stores = []
    for k in range(local):
        marks = []
        for c in range(2):
            top = tail[(2 * c) * local + k : (2 * c) * local + k + 1, :]
            low = tail[(2 * c + 1) * local + k : (2 * c + 1) * local + k + 1, :]
            marks.append(top * 64.0 + low)
        mark = jnp.concatenate(marks, axis=1)
        live = mark > 0.0
        target = jnp.where(live, mark - 1.0, 0.0).astype(jnp.int32)
        pick = one_hot(item_at == (target & (LANES - 1)))
        found = mm(tabs_ref[k], pick)
        found = found[0:chunks] + found[chunks : 2 * chunks] + found[2 * chunks : 3 * chunks]
        packed = jnp.sum(
            jnp.where(row_at == (target >> 7), found, 0.0), axis=0, keepdims=True
        ).astype(jnp.int32)
        item = jnp.where(live, packed >> 12, -1)
        count = (packed & 4095).astype(F32)
        queries = jnp.concatenate(
            [
                got32_ref[pl.ds(k, devices, stride=rows), :],
                got32_ref[pl.ds(local + k, devices, stride=rows), :],
            ],
            axis=0,
        ).astype(BF16)
        q_ref[k] = queries
        stores.append(pltpu.make_async_copy(q_ref.at[k], q_hbm.at[k], q_sem.at[k]))
        stores[-1].start()
        block = items_ref[k * LANES : (k + 1) * LANES, :]
        column = mass[:, k : k + 1]
        scores = mm(block, queries, ((1,), (1,)))
        masked = jnp.where(column > 0.0, scores, NONE)
        top = jnp.max(masked, axis=0, keepdims=True)
        expo = jnp.exp(masked - top) * column
        total = jnp.sum(expo, axis=0, keepdims=True)
        hit = item_at == item
        picked = jnp.sum(jnp.where(hit, scores, 0.0), axis=0, keepdims=True)
        loss = jnp.log(total) + top - (picked - jnp.log(count))
        loss = jnp.sum(jnp.where(live, loss, 0.0), axis=1, keepdims=True) / jnp.sum(
            jnp.where(live, 1.0, 0.0), axis=1, keepdims=True
        )
        losses = jnp.where(loss_lane == k, loss, losses)
        weight = (expo * (1.0 / total) - jnp.where(hit, 1.0, 0.0)).astype(BF16)
        weight_ref[k] = weight
        stores.append(pltpu.make_async_copy(weight_ref.at[k], weight_hbm.at[k], weight_sem.at[k]))
        stores[-1].start()
        dq = mm(weight, block, ((0,), (0,)))
        dq32_ref[pl.ds(k, devices, stride=2 * local), :] = dq[0:devices, :]
        dq32_ref[pl.ds(local + k, devices, stride=2 * local), :] = dq[devices:pairs, :]
    loss_ref[...] = losses
    quarter = devices // 4
    for part in range(4):
        span = pl.ds(part * quarter, quarter)
        flat = quarter * 2 * local
        dq_ref[span] = (
            dq32_ref[part * flat : (part + 1) * flat, :]
            .reshape(quarter, 2 * local, width)
            .astype(BF16)
        )
        stores.append(pltpu.make_async_copy(dq_ref.at[span], dq_hbm.at[span], dq_sem.at[part]))
        stores[-1].start()
    for store in stores:
        store.wait()


def owner(got, items, mass, tabs):
    devices, rows, width = got.shape
    local = items.shape[0] // LANES
    outs = (
        jax.ShapeDtypeStruct((devices, 2 * local, width), BF16),
        jax.ShapeDtypeStruct((local, LANES, 2 * devices), BF16),
        jax.ShapeDtypeStruct((local, 2 * devices, width), BF16),
    )
    return pl.pallas_call(
        owner_body,
        out_shape=outs_hbm(outs) + (jax.ShapeDtypeStruct((1, LANES), F32),),
        in_specs=vmem(4),
        out_specs=hbm(3) + vmem(1),
        scratch_shapes=[
            pltpu.VMEM((devices * rows, width), F32),
            pltpu.VMEM((devices * 2 * local, width), F32),
        ]
        + [pltpu.VMEM(a.shape, a.dtype) for a in outs]
        + [
            pltpu.SemaphoreType.DMA((4,)),
            pltpu.SemaphoreType.DMA((local,)),
            pltpu.SemaphoreType.DMA((local,)),
        ],
        compiler_params=params(40),
        name="owner",
    )(got, items, mass, tabs)


def item_body(weight_ref, q_ref, grad_ref):
    for k in range(weight_ref.shape[0]):
        grad_ref[k * LANES : (k + 1) * LANES, :] = mm(weight_ref[k], q_ref[k])


def item_grads(weight, queries):
    local, pairs, width = queries.shape
    step = 4
    return pl.pallas_call(
        item_body,
        grid=(local // step,),
        out_shape=jax.ShapeDtypeStruct((local * LANES, width), F32),
        in_specs=[
            pl.BlockSpec((step, LANES, pairs), lambda k: (k, 0, 0)),
            pl.BlockSpec((step, pairs, width), lambda k: (k, 0, 0)),
        ],
        out_specs=pl.BlockSpec((step * LANES, width), lambda k: (k, 0)),
        compiler_params=params(8),
        cost_estimate=pl.CostEstimate(
            flops=135_000_000, bytes_accessed=3 << 20, transcendentals=0
        ),
        name="item_grads",
    )(weight, queries)


def ready_body(mine_ref, theirs_ref, hidden_ref, slope_ref):
    users = mine_ref.shape[0]
    for i, ref in enumerate((mine_ref, theirs_ref)):
        pre = ref[...]
        sig = jax.nn.sigmoid(pre)
        hidden_ref[:, i * users : (i + 1) * users] = (pre * sig).T.astype(BF16)
        slope_ref[i * users : (i + 1) * users, :] = sig * (1.0 + pre * (1.0 - sig))


def ready(mine, theirs):
    users, half = mine.shape
    return pl.pallas_call(
        ready_body,
        out_shape=(
            jax.ShapeDtypeStruct((half, 2 * users), BF16),
            jax.ShapeDtypeStruct((2 * users, half), F32),
        ),
        in_specs=vmem(2),
        out_specs=vmem(2),
        compiler_params=params(16),
        cost_estimate=pl.CostEstimate(
            flops=3_000_000, bytes_accessed=3 << 20, transcendentals=1 << 19
        ),
        name="ready",
    )(mine, theirs)


def collect_body(back_ref, place_hbm, dq_ref, place_ref, sem):
    devices, rows, width = back_ref.shape
    parts = sem.shape[0]
    step = place_ref.shape[0] // parts
    loads = []
    for i in range(parts):
        span = pl.ds(i * step, step)
        loads.append(
            pltpu.make_async_copy(place_hbm.at[span, :], place_ref.at[span, :], sem.at[i])
        )
        loads[-1].start()
    total = jnp.zeros((width, place_ref.shape[1]), F32)
    group = devices // parts
    for i in range(parts):
        back = back_ref[i * group : (i + 1) * group].reshape(step, width)
        loads[i].wait()
        total = total + mm(back, place_ref[i * step : (i + 1) * step, :], ((0,), (0,)))
    dq_ref[...] = total.T.astype(BF16)


def collect(back, place):
    users = place.shape[1]
    return pl.pallas_call(
        collect_body,
        out_shape=jax.ShapeDtypeStruct((users, back.shape[2]), BF16),
        in_specs=vmem(1) + hbm(1),
        out_specs=vmem(1)[0],
        scratch_shapes=[pltpu.VMEM(place.shape, BF16), pltpu.SemaphoreType.DMA((4,))],
        compiler_params=params(24),
        name="collect",
    )(back, place)


def tower_body(dq_ref, other_ref, hidden_ref, slope_ref, feat_ref, feat_other_ref, wo_ref, grad_ref):
    users = dq_ref.shape[0]
    half = hidden_ref.shape[0]
    peers = grad_ref.shape[0]
    core = lax.axis_index("dev") % 2
    w_out = wo_ref[pl.ds(pl.multiple_of(core * half, half), half), :]
    big = None
    small = None
    for i, (dq, feat) in enumerate(((dq_ref, feat_ref), (other_ref, feat_other_ref))):
        dq = dq[...]
        dhidden = mm(dq, w_out, ((1,), (1,)))
        dpre = (dhidden * slope_ref[i * users : (i + 1) * users, :]).astype(BF16)
        part = mm(feat[...], dpre)
        big = part if big is None else big + part
        part = mm(hidden_ref[:, i * users : (i + 1) * users], dq)
        small = part if small is None else small + part
    tall = big.shape[0] // peers
    blocks = half // LANES
    for c in range(blocks):
        grad_ref[:, c * tall : (c + 1) * tall, :] = (
            big[:, c * LANES : (c + 1) * LANES].reshape(peers, tall, LANES).astype(BF16)
        )
    filled = half // 8
    at = blocks * tall
    grad_ref[0:filled, at : at + 8, :] = small.reshape(filled, 8, LANES).astype(BF16)
    grad_ref[filled:peers, at : at + 8, :] = jnp.zeros((peers - filled, 8, LANES), BF16)


def tower_back(dq, other, hidden, slope, features_t, features_other_t, w_out, peers):
    half = hidden.shape[0]
    rows = half * features_t.shape[0] // peers // LANES + 8
    return pl.pallas_call(
        tower_body,
        out_shape=jax.ShapeDtypeStruct((peers, rows, LANES), BF16),
        in_specs=vmem(7),
        out_specs=vmem(1)[0],
        compiler_params=params(40),
        name="tower_back",
    )(dq, other, hidden, slope, features_t, features_other_t, w_out)


def sum_body(parts_ref, out_ref):
    total = jnp.sum(parts_ref[...].astype(F32), axis=0, keepdims=True)
    out_ref[...] = jnp.broadcast_to(total, out_ref.shape).astype(BF16)


def sum_parts(parts):
    return pl.pallas_call(
        sum_body,
        out_shape=jax.ShapeDtypeStruct(parts.shape, BF16),
        in_specs=vmem(1),
        out_specs=vmem(1)[0],
        compiler_params=params(24),
        name="sum_parts",
    )(parts)


def spread_body(mine_ref, other_ref, hidden_ref, out_ref):
    peers = mine_ref.shape[0]
    core = lax.axis_index("dev") % 2
    half = out_ref.shape[0] // 2
    tall = hidden_ref.shape[0] // peers
    blocks = half // LANES
    filled = half // 8
    for side, ref in ((core, mine_ref), (1 - core, other_ref)):
        got = ref[...].astype(F32)
        for c in range(blocks):
            at = pl.multiple_of(side * half + c * LANES, LANES)
            hidden_ref[:, pl.ds(at, LANES)] = got[:, c * tall : (c + 1) * tall, :].reshape(
                hidden_ref.shape[0], LANES
            )
        at = blocks * tall
        out_ref[pl.ds(pl.multiple_of(side * half, half), half), :] = got[
            0:filled, at : at + 8, :
        ].reshape(half, LANES)


def spread(mine, other, hidden_shape, out_shape):
    return pl.pallas_call(
        spread_body,
        out_shape=(
            jax.ShapeDtypeStruct(hidden_shape, F32),
            jax.ShapeDtypeStruct(out_shape, F32),
        ),
        in_specs=vmem(2),
        out_specs=vmem(2),
        compiler_params=params(24),
        name="spread",
    )(mine, other)


def exchange(x):
    return lax.all_to_all(x, "dev", split_axis=0, concat_axis=0, tiled=True)


def exchange_peers(x):
    devices = lax.axis_size("dev")
    groups = [list(range(c, devices, 2)) for c in range(2)]
    return lax.all_to_all(
        x, "dev", split_axis=0, concat_axis=0, axis_index_groups=groups, tiled=True
    )


def swap(x):
    devices = lax.axis_size("dev")
    return lax.ppermute(x, "dev", [(d, d ^ 1) for d in range(devices)])


def local(
    features, w_hidden, w_out, items, routes, cluster_slot, sample_ids, sample_counts, positives
):
    devices = lax.axis_size("dev")
    features_other = swap(features)
    send, place, mine, other = route(
        routes, positives, cluster_slot, features, w_hidden, w_out, devices
    )
    mass, tabs = tables(sample_ids, sample_counts)
    got = exchange(send)
    theirs = swap(other)
    got, mass, tabs, theirs, features_other = lax.optimization_barrier(
        (got, mass, tabs, theirs, features_other)
    )
    dq_slots, weight, queries, losses = owner(got, items, mass, tabs)
    back = exchange(dq_slots)
    hidden, slope = ready(mine, theirs)
    item_grad = item_grads(weight, queries)
    features_t, features_other_t = features.T, features_other.T
    back, hidden, slope, item_grad, features_t, features_other_t = lax.optimization_barrier(
        (back, hidden, slope, item_grad, features_t, features_other_t)
    )
    dq = collect(back, place)
    partial = tower_back(
        dq, swap(dq), hidden, slope, features_t, features_other_t, w_out, devices // 2
    )
    summed = exchange_peers(sum_parts(exchange_peers(partial)))
    grad_hidden, grad_out = spread(summed, swap(summed), w_hidden.shape, w_out.shape)
    slot_loss = losses[0, : sample_ids.shape[0]]
    return (slot_loss, grad_hidden, grad_out, item_grad)


def solution(mesh):
    in_specs = (
        P("dev", None),
        P(),
        P(),
        P("dev", None),
        P("dev", None),
        P(),
        P("dev", None),
        P("dev", None),
        P("dev", None),
    )
    out_specs = (P("dev"), P(), P(), P("dev", None))
    return jax.shard_map(local, mesh=mesh, in_specs=in_specs, out_specs=out_specs, check_vma=False)
```

time: 145 us -> 127 us (0.88)
  waiting for transfers between devices: 48.9 us -> 24.8 us
  blocking collectives: 26.4 us -> 34.1 us
  Pallas kernels: 33.9 us -> 30.1 us
  starting transfers between devices: 20.9 us -> 22.5 us
    all_to_all x3 -> x2, waiting for transfers between devices: 48.9 us -> 22.6 us  [exchange(): return lax.all_to_all(x, 'dev', split_axis=0, concat_axis=0, tiled=True)]
    all_to_all x1 -> x2, blocking collectives: 26.4 us -> 34.1 us  [exchange_peers(): lax.all_to_all(x, 'dev', split_axis=0, concat_axis=0, axis_index_groups=g...]
    ppermute x0 -> x4, starting transfers between devices: none -> 6.23 us  [swap(): return lax.ppermute(x, 'dev', [(d, d ^ 1) for d in range(devices)])]
    all_to_all x3 -> x2, starting transfers between devices: 20.9 us -> 16.3 us  [exchange(): return lax.all_to_all(x, 'dev', split_axis=0, concat_axis=0, tiled=True)]
    pallas_call x4 -> x6, Pallas kernels: 25.1 us -> 22.5 us  [the longest x1 8.03 us: route(): pl.pallas_call(route_body, out_shape=outs_hbm(outs), in_specs=hbm(6), out...]
    ppermute x0 -> x4, waiting for transfers between devices: none -> 2.2 us  [swap(): return lax.ppermute(x, 'dev', [(d, d ^ 1) for d in range(devices)])]
    unnamed x37 -> x31, local copies, waits for them, and re-layouts: 12.7 us -> 11.4 us
  transfers between devices with their start and end apart: 3 -> 6, of which waited for: 3 -> 4; matrix products, arithmetic and copies ran while one was open for 1% -> 2% of each run, Pallas kernels for 9% -> 7%
where the time goes in v2:
time: 127 us; the launch traced here: 126 us
  blocking collectives  34.1 us (27%)
  Pallas kernels  30.1 us (24%)
  waiting for transfers between devices  24.8 us (20%)
  starting transfers between devices  22.5 us (18%)
  local copies, waits for them, and re-layouts  13.9 us (11%)
    all_to_all x2, blocking collectives, exchange_peers(): lax.all_to_all(x, 'dev', split_axis=0, concat_axis=0, axis_index_groups=g...  34.1 us
    all_to_all x2, waiting for transfers between devices, exchange(): return lax.all_to_all(x, 'dev', split_axis=0, concat_axis=0, tiled=True)  22.6 us
    all_to_all x2, starting transfers between devices, exchange(): return lax.all_to_all(x, 'dev', split_axis=0, concat_axis=0, tiled=True)  16.3 us
    unnamed x31, local copies, waits for them, and re-layouts  11.4 us
    pallas_call x1, Pallas kernels, route(): pl.pallas_call(route_body, out_shape=outs_hbm(outs), in_specs=hbm(6), out...  8.03 us
    pallas_call x1, Pallas kernels, owner(): pl.pallas_call(owner_body, out_shape=outs_hbm(outs) + (jax.ShapeDtypeStru...  7.92 us
    ppermute x4, starting transfers between devices, swap(): return lax.ppermute(x, 'dev', [(d, d ^ 1) for d in range(devices)])  6.23 us
    pallas_call x1, Pallas kernels, tables(): pl.pallas_call(table_body, out_shape=(jax.ShapeDtypeStruct((LANES, LANES)...  5.83 us
  transfers between devices with their start and end apart: 6, of which 4 were waited for; matrix products, arithmetic and copies ran while one was open for 2% of the time, Pallas kernels for 7%

profile of v2, /device:TPU:1, one launch (start us, length us, event | category | flops | bytes accessed | tf_op | source)
XLA Modules:
  0.0 126.2 jit_solution(2664808130058197110)
XLA Ops:
  0.6 8.0 %route.1 = (bf16[128,40,128]{2,1,0:T(8,128)(2,1)}, bf16[4096,512]{1,0:T(8,128)(2,1)}, f32[512,256]{1,0:T(8,128)}, f32[512,256]{1,0:T(8,128)}) custom-call(s32[4,512]{1,0:T(4,128)} %bitcast.8, s32[4,512]{1,0:T(4,128)} %bitcast.9, s32[16,128]{1,0:T(8,128)} %bitcast.10, bf16[512,1024]{1,0:T(8,128)(2,1)} %feat_hbm.1, bf16[1024,512]{1,0:T(8,128)(2,1)} %wh_hbm.1, ...), custom_call_target="tpu_custom_call" | custom-call | tf_op jit(solution)/shard_map/route/pallas_call | solution.py:193
  8.7 11.5 %all-to-all-start = ((bf16[128,40,128]{2,1,0:T(8,128)(2,1)}), bf16[128,40,128]{2,1,0:T(8,128)(2,1)S(1)}, u32[]{:S(2)}, u32[]{:S(2)}) async-start(bf16[128,40,128]{2,1,0:T(8,128)(2,1)} %get-tuple-element.29), calls=%async_computation | async-start | bytes 2621440 | tf_op jit(solution)/shard_map/all_to_all | solution.py:555
  20.8 1.1 collective-permute-start.1
  22.2 1.0 reshape.18.ids_ref
  23.2 1.0 reshape.19.counts_ref
  24.2 5.8 %tables.1 = (f32[128,128]{1,0:T(8,128)S(1)}, bf16[16,96,128]{2,1,0:T(8,128)(2,1)S(1)}) custom-call(s32[512,128]{1,0:T(8,128)S(1)} %reshape.18.ids_ref, s32[512,128]{1,0:T(8,128)S(1)} %reshape.19.counts_ref), custom_call_target="tpu_custom_call" | custom-call | flops 30000000 | bytes 1048576 | tf_op jit(solution)/shard_map/tables/pallas_call | solution.py:241
  31.6 10.7 %all-to-all-done.got_ref = bf16[128,40,128]{2,1,0:T(8,128)(2,1)S(1)} async-done(((bf16[128,40,128]{2,1,0:T(8,128)(2,1)}), bf16[128,40,128]{2,1,0:T(8,128)(2,1)S(1)}, u32[]{:S(2)}, u32[]{:S(2)}) %all-to-all-start) | async-done | bytes 1310752 | tf_op jit(solution)/shard_map/all_to_all | solution.py:555
  42.3 1.0 copy-done.11
  44.3 7.9 %owner.1 = (bf16[128,32,128]{2,1,0:T(8,128)(2,1)}, bf16[16,128,256]{2,1,0:T(8,128)(2,1)}, bf16[16,256,128]{2,1,0:T(8,128)(2,1)}, f32[1,128]{1,0:T(1,128)S(1)}) custom-call(bf16[128,40,128]{2,1,0:T(8,128)(2,1)S(1)} %all-to-all-done.got_ref, bf16[2048,128]{1,0:T(8,128)(2,1)S(1)} %copy-done.11, f32[128,128]{1,0:T(8,128)S(1)} %get-tuple-element.34.mass_ref, ...), custom_call_target="tpu_custom_call" | custom-call | tf_op jit(solution)/shard_map/owner/pallas_call | solution.py:358
  52.3 4.7 %all-to-all-start.1 = ((bf16[128,32,128]{2,1,0:T(8,128)(2,1)}), bf16[128,32,128]{2,1,0:T(8,128)(2,1)S(1)}, u32[]{:S(2)}, u32[]{:S(2)}) async-start(bf16[128,32,128]{2,1,0:T(8,128)(2,1)} %get-tuple-element.37), calls=%async_computation.1 | async-start | bytes 2097152 | tf_op jit(solution)/shard_map/all_to_all | solution.py:555
  57.0 1.0 copy-done.8
  58.1 1.0 copy-done.10
  61.3 1.2 copy-done.2
  62.5 2.1 %item_grads.1 = f32[2048,128]{1,0:T(8,128)} custom-call(bf16[16,128,256]{2,1,0:T(8,128)(2,1)S(1)} %copy-done.1, bf16[16,256,128]{2,1,0:T(8,128)(2,1)S(1)} %copy-done.2), custom_call_target="tpu_custom_call" | custom-call | flops 135000000 | bytes 3145728 | tf_op jit(solution)/shard_map/item_grads/pallas_call | solution.py:386
  64.6 11.9 %all-to-all-done.1.back_ref = bf16[128,32,128]{2,1,0:T(8,128)(2,1)S(1)} async-done(((bf16[128,32,128]{2,1,0:T(8,128)(2,1)}), bf16[128,32,128]{2,1,0:T(8,128)(2,1)S(1)}, u32[]{:S(2)}, u32[]{:S(2)}) %all-to-all-start.1) | async-done | bytes 1048608 | tf_op jit(solution)/shard_map/all_to_all | solution.py:555
  76.4 2.2 %copy-done = bf16[4096,512]{1,0:T(8,128)(2,1)S(1)} copy-done((bf16[4096,512]{1,0:T(8,128)(2,1)S(1)}, bf16[4096,512]{1,0:T(8,128)(2,1)}, u32[]{:S(2)}) %copy-start) | copy-done | bytes 4194328
  78.6 1.4 %collect.1.dq_ref = bf16[512,128]{1,0:T(8,128)(2,1)S(1)} custom-call(bf16[128,32,128]{2,1,0:T(8,128)(2,1)S(1)} %all-to-all-done.1.back_ref, bf16[4096,512]{1,0:T(8,128)(2,1)S(1)} %copy-done), custom_call_target="tpu_custom_call" | custom-call | tf_op jit(solution)/shard_map/collect/pallas_call | solution.py:452
  80.1 1.3 collective-permute-start.2
  82.3 2.6 %tower_back.1 = bf16[64,40,128]{2,1,0:T(8,128)(2,1)S(1)} custom-call(bf16[512,128]{1,0:T(8,128)(2,1)S(1)} %collect.1.dq_ref, bf16[512,128]{1,0:T(8,128)(2,1)S(1)} %collective-permute-done.2.other_ref, bf16[256,1024]{1,0:T(8,128)(2,1)S(1)} %copy-done.6, f32[1024,256]{1,0:T(8,128)S(1)} %copy-done.4, bf16[1024,512]{1,0:T(8,128)(2,1)S(1)} %bitcast.7, ...), custom_call_target="tpu_custom_call" | custom-call | tf_op jit(solution)/shard_map/tower_back/pallas_call | solution.py:494
  84.9 17.6 %all_to_all.20.parts_ref = bf16[64,40,128]{2,1,0:T(8,128)(2,1)S(1)} all-to-all(bf16[64,40,128]{2,1,0:T(8,128)(2,1)S(1)} %tower_back.1), channel_id=1, replica_groups={{0,2,4,6,8,10,12,14,16,18,20,22,24,26,28,30,32,34,36,38,40,42,44,46,48,..., dimensions={0} | all-to-all | bytes 1310720 | tf_op jit(solution)/shard_map/all_to_all | solution.py:561
  102.7 16.5 %all_to_all.21.mine_ref = bf16[64,40,128]{2,1,0:T(8,128)(2,1)S(1)} all-to-all(bf16[64,40,128]{2,1,0:T(8,128)(2,1)S(1)} %sum_parts.1), channel_id=1, replica_groups={{0,2,4,6,8,10,12,14,16,18,20,22,24,26,28,30,32,34,36,38,40,42,44,46,48,..., dimensions={0} | all-to-all | bytes 1310720 | tf_op jit(solution)/shard_map/all_to_all | solution.py:561
  119.2 3.5 %collective-permute-start.3 = (bf16[64,40,128]{2,1,0:T(8,128)(2,1)S(1)}, bf16[64,40,128]{2,1,0:T(8,128)(2,1)S(1)}, u32[]{:S(2)}, u32[]{:S(2)}) collective-permute-start(bf16[64,40,128]{2,1,0:T(8,128)(2,1)S(1)} %all_to_all.21.mine_ref), channel_id=1, source_target_pairs={{0,1},{1,0},{2,3},{3,2},{4,5},{5,4},{6,7},{7,6},{8,9},{9,8},{10,11... | collective-permute-start | bytes 1966088 | tf_op jit(solution)/shard_map/ppermute | solution.py:568
  123.3 1.2 collective-permute-done.3.other_ref
  124.5 1.7 %spread.1 = (f32[1024,512]{1,0:T(8,128)}, f32[512,128]{1,0:T(8,128)}) custom-call(bf16[64,40,128]{2,1,0:T(8,128)(2,1)S(1)} %all_to_all.21.mine_ref, bf16[64,40,128]{2,1,0:T(8,128)(2,1)S(1)} %collective-permute-done.3.other_ref), custom_call_target="tpu_custom_call" | custom-call | tf_op jit(solution)/shard_map/spread/pallas_call | solution.py:541
  (33 shorter events, 7.2 us)
Async XLA Ops:
  0.6 19.6 %copy-start.14 = (bf16[512,1024]{1,0:T(8,128)(2,1)S(1)}, bf16[512,1024]{1,0:T(8,128)(2,1)}, u32[]{:S(2)}) copy-start(bf16[512,1024]{1,0:T(8,128)(2,1)} %feat_hbm.1) | copy-start | bytes 3145732
  8.7 33.6 %all-to-all-start = ((bf16[128,40,128]{2,1,0:T(8,128)(2,1)}), bf16[128,40,128]{2,1,0:T(8,128)(2,1)S(1)}, u32[]{:S(2)}, u32[]{:S(2)}) async-start(bf16[128,40,128]{2,1,0:T(8,128)(2,1)} %get-tuple-element.29), calls=%async_computation | async-start | bytes 2621440 | tf_op jit(solution)/shard_map/all_to_all | solution.py:555
  20.8 10.8 %collective-permute-start.1 = (bf16[512,1024]{0,1:T(8,128)(2,1)S(1)}, bf16[512,1024]{0,1:T(8,128)(2,1)}, u32[]{:S(2)}, u32[]{:S(2)}) collective-permute-start(bf16[512,1024]{0,1:T(8,128)(2,1)S(1)} %copy.13), channel_id=1, source_target_pairs={{0,1},{1,0},{2,3},{3,2},{4,5},{5,4},{6,7},{7,6},{8,9},{9,8},{10,11... | collective-permute-start | bytes 3145736 | tf_op jit(solution)/shard_map/ppermute | solution.py:568
  21.9 8.9 %collective-permute-start = (f32[512,256]{1,0:T(8,128)}, f32[512,256]{1,0:T(8,128)S(1)}, u32[]{:S(2)}, u32[]{:S(2)}) collective-permute-start(f32[512,256]{1,0:T(8,128)} %get-tuple-element.32), channel_id=1, source_target_pairs={{0,1},{1,0},{2,3},{3,2},{4,5},{5,4},{6,7},{7,6},{8,9},{9,8},{10,11... | collective-permute-start | bytes 1572872 | tf_op jit(solution)/shard_map/ppermute | solution.py:568
  30.0 0.8 copy-start.12
  30.8 0.8 copy-start.9
  42.3 1.0 copy-start.11
  43.3 1.0 copy-start.13
  52.3 9.0 %copy-start.1 = (bf16[16,128,256]{2,1,0:T(8,128)(2,1)S(1)}, bf16[16,128,256]{2,1,0:T(8,128)(2,1)}, u32[]{:S(2)}) copy-start(bf16[16,128,256]{2,1,0:T(8,128)(2,1)} %get-tuple-element.42.weight_ref) | copy-start | bytes 3145732
  52.3 24.2 %all-to-all-start.1 = ((bf16[128,32,128]{2,1,0:T(8,128)(2,1)}), bf16[128,32,128]{2,1,0:T(8,128)(2,1)S(1)}, u32[]{:S(2)}, u32[]{:S(2)}) async-start(bf16[128,32,128]{2,1,0:T(8,128)(2,1)} %get-tuple-element.37), calls=%async_computation.1 | async-start | bytes 2097152 | tf_op jit(solution)/shard_map/all_to_all | solution.py:555
  57.0 1.0 copy-start.8
  58.1 1.0 copy-start.10
  59.5 1.0 copy-start.3
  60.5 0.8 copy-start.5
  61.3 1.2 copy-start.2
  76.4 2.2 %copy-start = (bf16[4096,512]{1,0:T(8,128)(2,1)S(1)}, bf16[4096,512]{1,0:T(8,128)(2,1)}, u32[]{:S(2)}) copy-start(bf16[4096,512]{1,0:T(8,128)(2,1)} %get-tuple-element.46.place_hbm) | copy-start | bytes 12582916
  78.6 3.7 %copy-start.4 = (f32[1024,256]{1,0:T(8,128)S(1)}, f32[1024,256]{1,0:T(8,128)}, u32[]{:S(2)}) copy-start(f32[1024,256]{1,0:T(8,128)} %copy-done.3) | copy-start | bytes 3145732
  78.6 3.7 %copy-start.6 = (bf16[256,1024]{1,0:T(8,128)(2,1)S(1)}, bf16[256,1024]{1,0:T(8,128)(2,1)}, u32[]{:S(2)}) copy-start(bf16[256,1024]{1,0:T(8,128)(2,1)} %copy-done.5) | copy-start | bytes 1572868
  78.6 3.7 %copy-start.7 = (bf16[512,128]{1,0:T(8,128)(2,1)S(1)}, bf16[512,128]{1,0:T(8,128)(2,1)}, u32[]{:S(2)}) copy-start(bf16[512,128]{1,0:T(8,128)(2,1)} %wo_ref.1) | copy-start | bytes 393220
  80.1 2.2 %collective-permute-start.2 = (bf16[512,128]{1,0:T(8,128)(2,1)S(1)}, bf16[512,128]{1,0:T(8,128)(2,1)S(1)}, u32[]{:S(2)}, u32[]{:S(2)}) collective-permute-start(bf16[512,128]{1,0:T(8,128)(2,1)S(1)} %collect.1.dq_ref), channel_id=1, source_target_pairs={{0,1},{1,0},{2,3},{3,2},{4,5},{5,4},{6,7},{7,6},{8,9},{9,8},{10,11... | collective-permute-start | bytes 393224 | tf_op jit(solution)/shard_map/ppermute | solution.py:568
  119.2 5.3 %collective-permute-start.3 = (bf16[64,40,128]{2,1,0:T(8,128)(2,1)S(1)}, bf16[64,40,128]{2,1,0:T(8,128)(2,1)S(1)}, u32[]{:S(2)}, u32[]{:S(2)}) collective-permute-start(bf16[64,40,128]{2,1,0:T(8,128)(2,1)S(1)} %all_to_all.21.mine_ref), channel_id=1, source_target_pairs={{0,1},{1,0},{2,3},{3,2},{4,5},{5,4},{6,7},{7,6},{8,9},{9,8},{10,11... | collective-permute-start | bytes 1966088 | tf_op jit(solution)/shard_map/ppermute | solution.py:568

commit v3 on v2

v3 whole, which is shorter than its diff:
```python
import jax
import jax.numpy as jnp
from jax import lax
from jax.experimental import pallas as pl
from jax.experimental.pallas import tpu as pltpu
from jax.sharding import PartitionSpec as P

F32 = jnp.float32
BF16 = jnp.bfloat16
NONE = -3.0e38
KEY = 4096
AHEAD = 1
LANES = 128


def vmem(count):
    return [pl.BlockSpec(memory_space=pltpu.VMEM)] * count


def in_hbm(arrays):
    return tuple(pltpu.with_memory_space_constraint(a, pltpu.HBM) for a in arrays)


def outs_hbm(arrays):
    return tuple(pltpu.HBM(a.shape, a.dtype) for a in arrays)


def hbm(count):
    return [pl.BlockSpec(memory_space=pltpu.HBM)] * count


def params(megabytes):
    return pltpu.CompilerParams(vmem_limit_bytes=megabytes << 20)


def iota(shape, axis):
    return lax.broadcasted_iota(jnp.int32, shape, axis)


def one_hot(mask):
    return jnp.where(mask, 1.0, 0.0).astype(BF16)


def mm(a, b, dims=((1,), (0,))):
    return lax.dot_general(a, b, (dims, ((), ())), preferred_element_type=F32)


def route_body(
    routes_hbm,
    pos_hbm,
    cslot_hbm,
    feat_hbm,
    wh_hbm,
    wo_hbm,
    send_hbm,
    named_hbm,
    mine_hbm,
    other_hbm,
    routes_ref,
    pos_ref,
    cslot_ref,
    feat_ref,
    wh_ref,
    wo_ref,
    send_ref,
    named_ref,
    mine_ref,
    other_ref,
    place_ref,
    in_sem,
    out_sem,
    send_sem,
):
    loads = [
        pltpu.make_async_copy(src, dst, in_sem.at[i])
        for i, (src, dst) in enumerate(
            [
                (routes_hbm, routes_ref),
                (pos_hbm, pos_ref),
                (cslot_hbm, cslot_ref),
                (feat_hbm, feat_ref),
                (wh_hbm, wh_ref),
                (wo_hbm, wo_ref),
            ]
        )
    ]
    for load in loads:
        load.start()
    visits, users = routes_ref.shape
    clusters = cslot_ref.shape[0] * LANES
    devices, rows, width = send_ref.shape
    local = clusters // devices
    for load in loads[:3]:
        load.wait()
    cslot = cslot_ref[...]
    row_at = iota((cslot.shape[0], LANES), 0)
    user_at = iota((1, users), 1)
    slots = []
    keys = []
    for r in range(visits):
        found = []
        for part in range(users // LANES):
            cluster = routes_ref[r : r + 1, part * LANES : (part + 1) * LANES]
            lane = jnp.broadcast_to(cluster & (LANES - 1), cslot.shape)
            row = jnp.take_along_axis(cslot, lane, axis=1)
            found.append(
                jnp.sum(jnp.where(row_at == (cluster >> 7), row, 0), axis=0, keepdims=True)
            )
        slots.append(jnp.concatenate(found, axis=1).astype(F32))
        keys.append((user_at * KEY + pos_ref[r : r + 1, :] + 1).astype(F32))
    block = LANES
    groups = block // local
    sub = iota((block, users), 0).astype(F32)
    lane_user = iota((block, users), 1).astype(F32)
    tail_lane = iota((block, LANES), 1)
    tail_row = iota((block, LANES), 0)
    tail_hit = ((tail_lane & (local - 1)) == (tail_row & (local - 1))) & (tail_lane < 4 * local)
    tail_kind = tail_lane // local
    stores = []
    named_lane = iota((block, LANES), 1)
    named = [jnp.zeros((block, LANES), F32)]

    def assign(b):
        slot_at = sub + float(b * block)
        key = jnp.zeros((block, users), F32)
        for r in range(visits):
            key = jnp.where(slot_at == slots[r], keys[r], key)
        most = jnp.max(key, axis=1, keepdims=True)
        rest = jnp.sum(key, axis=1, keepdims=True) - most
        ends = []
        parts = []
        for c, chosen in enumerate((most, rest)):
            user = jnp.floor((chosen - 1.0) * (1.0 / KEY))
            named[0] = jnp.where(named_lane == 2 * b + c, user, named[0])
            mark = jnp.where(chosen > 0.0, chosen - user * KEY, 0.0)
            top = jnp.floor(mark * (1.0 / 64.0))
            ends += [top, mark - top * 64.0]
            parts.append(jnp.where(lane_user == user, 1.0, 0.0).reshape(block // 8, 8, users))
        place = jnp.concatenate(parts, axis=1).reshape(2 * block, users).astype(BF16)
        span = pl.ds(b * 2 * block, 2 * block)
        place_ref[span, :] = place
        tail = jnp.where(
            tail_kind == 0,
            ends[0],
            jnp.where(tail_kind == 1, ends[1], jnp.where(tail_kind == 2, ends[2], ends[3])),
        )
        tail = jnp.where(tail_hit, tail, 0.0).reshape(groups, local, LANES)
        tail = jnp.sum(tail, axis=1)
        send_ref[b * groups : (b + 1) * groups, 2 * local : rows, :] = jnp.broadcast_to(
            tail[:, None, :], (groups, rows - 2 * local, width)
        ).astype(BF16)

    early = 6
    for b in range(early):
        assign(b)
    for load in loads[3:]:
        load.wait()
    pre = mm(feat_ref[...], wh_ref[...])
    half = pre.shape[1] // 2
    core = lax.axis_index("dev") % 2
    mine_ref[...] = jnp.where(core == 0, pre[:, 0:half], pre[:, half:])
    other_ref[...] = jnp.where(core == 0, pre[:, half:], pre[:, 0:half])
    for src, dst, i in ((mine_ref, mine_hbm, 0), (other_ref, other_hbm, 1)):
        stores.append(pltpu.make_async_copy(src, dst, out_sem.at[i]))
        stores[-1].start()
    hidden = (pre * jax.nn.sigmoid(pre)).astype(BF16)
    query = mm(hidden, wo_ref[...]).astype(BF16)
    blocks = clusters // block
    for b in range(blocks):
        if b + early < blocks:
            assign(b + early)
        if b + early == blocks:
            named_ref[...] = named[0]
            stores.append(pltpu.make_async_copy(named_ref, named_hbm, out_sem.at[2]))
            stores[-1].start()
        sent = mm(place_ref[b * 2 * block : (b + 1) * 2 * block, :], query).astype(BF16)
        span = pl.ds(b * groups, groups)
        send_ref[span, 0 : 2 * local, :] = sent.reshape(groups, 2 * local, width)
        if b % 4 == 3:
            span = pl.ds((b - 3) * groups, 4 * groups)
            stores.append(
                pltpu.make_async_copy(send_ref.at[span], send_hbm.at[span], send_sem.at[b // 4])
            )
            stores[-1].start()
    for store in stores:
        store.wait()


def route(routes, positives, cluster_slot, features, w_hidden, w_out, devices):
    users, visits = routes.shape
    clusters = cluster_slot.shape[0]
    width = w_out.shape[1]
    hid = w_hidden.shape[1]
    rows = 2 * clusters // devices + 8
    args = (
        routes.T,
        positives.T,
        cluster_slot.reshape(clusters // LANES, LANES),
        features,
        w_hidden,
        w_out,
    )
    outs = (
        jax.ShapeDtypeStruct((devices, rows, width), BF16),
        jax.ShapeDtypeStruct((LANES, LANES), F32),
        jax.ShapeDtypeStruct((users, hid // 2), F32),
        jax.ShapeDtypeStruct((users, hid // 2), F32),
    )
    return pl.pallas_call(
        route_body,
        out_shape=outs_hbm(outs),
        in_specs=hbm(6),
        out_specs=hbm(4),
        scratch_shapes=[pltpu.VMEM(a.shape, a.dtype) for a in args + outs]
        + [
            pltpu.VMEM((2 * clusters, users), BF16),
            pltpu.SemaphoreType.DMA((6,)),
            pltpu.SemaphoreType.DMA((3,)),
            pltpu.SemaphoreType.DMA((4,)),
        ],
        compiler_params=params(48),
        name="route",
    )(*in_hbm(args))


def table_body(ids_ref, counts_ref, mass_hbm, tabs_hbm, inv_ref, mass_ref, tabs_ref, sem):
    clusters, chunks, lanes = tabs_ref.shape
    inv_ref[...] = 1.0 / counts_ref[...].astype(F32)
    tabs_ref[...] = ((ids_ref[...] << 12) | counts_ref[...]).reshape(tabs_ref.shape)
    store = pltpu.make_async_copy(tabs_ref, tabs_hbm, sem.at[0])
    store.start()
    item_at = iota((LANES, LANES), 0)

    def cluster(k, carry):
        acc = jnp.zeros((LANES, LANES), F32)
        for h in range(chunks):
            at = k * chunks + h
            hit = item_at == ids_ref[pl.ds(at, 1), :]
            acc = acc + jnp.where(hit, inv_ref[pl.ds(at, 1), :], 0.0)
        mass_ref[k] = jnp.broadcast_to(jnp.sum(acc, axis=1, keepdims=True), acc.shape)
        return carry

    lax.fori_loop(0, clusters, cluster, 0)
    last = pltpu.make_async_copy(mass_ref, mass_hbm, sem.at[1])
    last.start()
    last.wait()
    store.wait()


def tables(sample_ids, sample_counts):
    clusters, samples = sample_ids.shape
    total = sample_ids.size // LANES
    outs = (
        jax.ShapeDtypeStruct((clusters, LANES, LANES), F32),
        jax.ShapeDtypeStruct((clusters, samples // LANES, LANES), jnp.int32),
    )
    return pl.pallas_call(
        table_body,
        out_shape=outs_hbm(outs),
        in_specs=vmem(2),
        out_specs=hbm(2),
        scratch_shapes=[pltpu.VMEM((total, LANES), F32)]
        + [pltpu.VMEM(a.shape, a.dtype) for a in outs]
        + [pltpu.SemaphoreType.DMA((2,))],
        compiler_params=params(16),
        cost_estimate=pl.CostEstimate(flops=30_000_000, bytes_accessed=1 << 20, transcendentals=0),
        name="tables",
    )(sample_ids.reshape(total, LANES), sample_counts.reshape(total, LANES))


def row_of(slot):
    return slot // 8 * 16 + slot % 8


def owner_body(
    got_ref,
    items_hbm,
    mass_hbm,
    tabs_hbm,
    dq_hbm,
    weight_hbm,
    q_hbm,
    loss_ref,
    got32_ref,
    dq32_ref,
    dq_ref,
    weight_ref,
    q_ref,
    items_ref,
    mass_ref,
    tabs_ref,
    losses_ref,
    load_sem,
    dq_sem,
    weight_sem,
    q_sem,
):
    loads = [
        pltpu.make_async_copy(tabs_hbm, tabs_ref, load_sem.at[0]),
        pltpu.make_async_copy(items_hbm, items_ref, load_sem.at[1]),
    ]
    for part in range(mass_ref.shape[0] // 4):
        span = pl.ds(part * 4, 4)
        loads.append(
            pltpu.make_async_copy(mass_hbm.at[span], mass_ref.at[span], load_sem.at[2 + part])
        )
    for load in loads:
        load.start()
    devices, rows, width = got_ref.shape
    local = q_ref.shape[0]
    chunks = tabs_ref.shape[1]
    pairs = 2 * devices
    got32_ref[...] = got_ref[...].astype(F32).reshape(devices * rows, width)
    tail = got32_ref[pl.ds(2 * local, devices, stride=rows), :].T
    marks = [
        tail[2 * c * local : (2 * c + 1) * local, :] * 64.0
        + tail[(2 * c + 1) * local : (2 * c + 2) * local, :]
        for c in range(2)
    ]
    targets = [jnp.maximum(mark - 1.0, 0.0).astype(jnp.int32) for mark in marks]
    item_at = iota((LANES, pairs), 0)
    row_at = iota((chunks, devices), 0)
    for load in loads[0:2]:
        load.wait()
    stores = []

    def fetch(k):
        packed = []
        for target in targets:
            at = target[k : k + 1, :]
            lane = jnp.broadcast_to(at & (LANES - 1), (chunks, devices))
            found = jnp.take_along_axis(tabs_ref[k], lane, axis=1)
            packed.append(jnp.sum(jnp.where(row_at == (at >> 7), found, 0), axis=0, keepdims=True))
        packed = jnp.concatenate(packed, axis=1)
        live = jnp.concatenate([mark[k : k + 1, :] for mark in marks], axis=1) > 0.0
        queries = jnp.concatenate(
            [
                got32_ref[pl.ds(row_of(k), devices, stride=rows), :],
                got32_ref[pl.ds(row_of(k) + 8, devices, stride=rows), :],
            ],
            axis=0,
        ).astype(BF16)
        q_ref[k] = queries
        stores.append(pltpu.make_async_copy(q_ref.at[k], q_hbm.at[k], q_sem.at[k]))
        stores[-1].start()
        scores = mm(items_ref[k * LANES : (k + 1) * LANES, :], queries, ((1,), (1,)))
        return live, packed, scores

    def soften(k, live, packed, scores):
        item = jnp.where(live, packed >> 12, -1)
        count = (packed & 4095).astype(F32)
        if k % 4 == 0:
            loads[2 + k // 4].wait()
        column = jnp.concatenate([mass_ref[k]] * (pairs // LANES), axis=1)
        masked = jnp.where(column > 0.0, scores, NONE)
        top = jnp.max(masked, axis=0, keepdims=True)
        expo = jnp.exp(masked - top) * column
        total = jnp.sum(expo, axis=0, keepdims=True)
        hit = item_at == item
        picked = jnp.sum(jnp.where(hit, scores, 0.0), axis=0, keepdims=True)
        losses_ref[k : k + 1, :] = jnp.log(total) + top - (picked - jnp.log(count))
        weight = (expo * (1.0 / total) - jnp.where(hit, 1.0, 0.0)).astype(BF16)
        weight_ref[k] = weight
        stores.append(pltpu.make_async_copy(weight_ref.at[k], weight_hbm.at[k], weight_sem.at[k]))
        stores[-1].start()
        return weight

    def give(k, weight):
        dq = mm(weight, items_ref[k * LANES : (k + 1) * LANES, :], ((0,), (0,)))
        dq32_ref[pl.ds(row_of(k), devices, stride=rows), :] = dq[0:devices, :]
        dq32_ref[pl.ds(row_of(k) + 8, devices, stride=rows), :] = dq[devices:pairs, :]
        if k % 8 == 7:
            at = row_of(k) - 7
            dq_ref[:, at : at + 16, :] = (
                dq32_ref[...].reshape(devices, rows, width)[:, at : at + 16, :].astype(BF16)
            )
            span = (slice(None), pl.ds(at, 16))
            stores.append(
                pltpu.make_async_copy(dq_ref.at[span], dq_hbm.at[span], dq_sem.at[k // 8])
            )
            stores[-1].start()

    fetched = [fetch(k) for k in range(AHEAD)]
    for k in range(local):
        if k + AHEAD < local:
            fetched.append(fetch(k + AHEAD))
        give(k, soften(k, *fetched[k]))
    live = jnp.concatenate(marks, axis=1) > 0.0
    total = jnp.sum(jnp.where(live, losses_ref[...], 0.0), axis=1, keepdims=True)
    loss_ref[...] = total / jnp.sum(jnp.where(live, 1.0, 0.0), axis=1, keepdims=True)
    for store in stores:
        store.wait()


def owner(got, items, mass, tabs):
    devices, rows, width = got.shape
    local = items.shape[0] // LANES
    outs = (
        jax.ShapeDtypeStruct((devices, 2 * local, width), BF16),
        jax.ShapeDtypeStruct((local, LANES, 2 * devices), BF16),
        jax.ShapeDtypeStruct((local, 2 * devices, width), BF16),
    )
    return pl.pallas_call(
        owner_body,
        out_shape=outs_hbm(outs) + (jax.ShapeDtypeStruct((local, 1), F32),),
        in_specs=vmem(1) + hbm(3),
        out_specs=hbm(3) + vmem(1),
        scratch_shapes=[
            pltpu.VMEM((devices * rows, width), F32),
            pltpu.VMEM((devices * rows, width), F32),
        ]
        + [pltpu.VMEM(a.shape, a.dtype) for a in outs + (items, mass, tabs)]
        + [
            pltpu.VMEM((local, 2 * devices), F32),
            pltpu.SemaphoreType.DMA((2 + local // 4,)),
            pltpu.SemaphoreType.DMA((local // 8,)),
            pltpu.SemaphoreType.DMA((local,)),
            pltpu.SemaphoreType.DMA((local,)),
        ],
        compiler_params=params(40),
        name="owner",
    )(got, *in_hbm((items, mass, tabs)))


def item_body(weight_ref, q_ref, grad_ref):
    for k in range(weight_ref.shape[0]):
        grad_ref[k * LANES : (k + 1) * LANES, :] = mm(weight_ref[k], q_ref[k])


def item_grads(weight, queries):
    local, pairs, width = queries.shape
    step = 4
    return pl.pallas_call(
        item_body,
        grid=(local // step,),
        out_shape=jax.ShapeDtypeStruct((local * LANES, width), F32),
        in_specs=[
            pl.BlockSpec((step, LANES, pairs), lambda k: (k, 0, 0)),
            pl.BlockSpec((step, pairs, width), lambda k: (k, 0, 0)),
        ],
        out_specs=pl.BlockSpec((step * LANES, width), lambda k: (k, 0)),
        compiler_params=params(8),
        cost_estimate=pl.CostEstimate(
            flops=135_000_000, bytes_accessed=3 << 20, transcendentals=0
        ),
        name="item_grads",
    )(*in_hbm((weight, queries)))


def ready_body(mine_ref, theirs_ref, hidden_ref, slope_ref):
    for i, ref in enumerate((mine_ref, theirs_ref)):
        pre = ref[...]
        sig = jax.nn.sigmoid(pre)
        hidden_ref[i] = (pre * sig).T.astype(BF16)
        slope_ref[i] = sig * (1.0 + pre * (1.0 - sig))


def ready(mine, theirs):
    users, half = mine.shape
    step = users // 2
    outs = (
        jax.ShapeDtypeStruct((2, half, users), BF16),
        jax.ShapeDtypeStruct((2, users, half), F32),
    )
    return pl.pallas_call(
        ready_body,
        grid=(users // step,),
        out_shape=outs_hbm(outs),
        in_specs=[pl.BlockSpec((step, half), lambda i: (i, 0))] * 2,
        out_specs=[
            pl.BlockSpec((2, half, step), lambda i: (0, 0, i)),
            pl.BlockSpec((2, step, half), lambda i: (0, i, 0)),
        ],
        compiler_params=params(16),
        cost_estimate=pl.CostEstimate(
            flops=3_000_000, bytes_accessed=3 << 20, transcendentals=1 << 19
        ),
        name="ready",
    )(*in_hbm((mine, theirs)))


def collect_body(back_ref, named_ref, dq_ref):
    devices, rows, width = back_ref.shape
    users = dq_ref.shape[0]
    block = LANES
    named = named_ref[...]
    lane_user = iota((block, users), 1).astype(F32)
    total = jnp.zeros((width, users), F32)
    group = 2 * block // rows
    for b in range(devices // group):
        parts = [
            jnp.where(lane_user == named[:, 2 * b + c : 2 * b + c + 1], 1.0, 0.0).reshape(
                block // 8, 8, users
            )
            for c in range(2)
        ]
        place = jnp.concatenate(parts, axis=1).reshape(2 * block, users).astype(BF16)
        back = back_ref[b * group : (b + 1) * group].reshape(2 * block, width)
        total = total + mm(back, place, ((0,), (0,)))
    dq_ref[...] = total.T.astype(BF16)


def collect(back, named, users):
    return pl.pallas_call(
        collect_body,
        out_shape=jax.ShapeDtypeStruct((users, back.shape[2]), BF16),
        in_specs=vmem(2),
        out_specs=vmem(1)[0],
        compiler_params=params(24),
        name="collect",
    )(back, named)


def tower_body(
    dq_ref,
    other_ref,
    hidden_hbm,
    slope_hbm,
    feat_hbm,
    feat_other_hbm,
    wo_hbm,
    grad_ref,
    hidden_ref,
    slope_ref,
    feat_ref,
    feat_other_ref,
    wo_ref,
    sem,
):
    users = dq_ref.shape[0]
    half = hidden_ref.shape[1]
    peers = grad_ref.shape[0]
    core = lax.axis_index("dev") % 2
    wo_at = wo_hbm.at[pl.ds(pl.multiple_of(core * half, half), half), :]
    loads = [
        pltpu.make_async_copy(src, dst, sem.at[i])
        for i, (src, dst) in enumerate(
            [
                (wo_at, wo_ref),
                (slope_hbm, slope_ref),
                (feat_hbm, feat_ref),
                (feat_other_hbm, feat_other_ref),
                (hidden_hbm, hidden_ref),
            ]
        )
    ]
    for load in loads:
        load.start()
    for load in loads[:2]:
        load.wait()
    w_out = wo_ref[...]
    dqs = (dq_ref[...], other_ref[...])
    dpres = [
        (mm(dq, w_out, ((1,), (1,))) * slope_ref[i]).astype(BF16) for i, dq in enumerate(dqs)
    ]
    loads[2].wait()
    big = mm(feat_ref[...], dpres[0])
    loads[3].wait()
    big = big + mm(feat_other_ref[...], dpres[1])
    loads[4].wait()
    small = mm(hidden_ref[0], dqs[0]) + mm(hidden_ref[1], dqs[1])
    tall = big.shape[0] // peers
    blocks = half // LANES
    for c in range(blocks):
        grad_ref[:, c * tall : (c + 1) * tall, :] = (
            big[:, c * LANES : (c + 1) * LANES].reshape(peers, tall, LANES).astype(BF16)
        )
    filled = half // 8
    at = blocks * tall
    grad_ref[0:filled, at : at + 8, :] = small.reshape(filled, 8, LANES).astype(BF16)
    grad_ref[filled:peers, at : at + 8, :] = jnp.zeros((peers - filled, 8, LANES), BF16)


def tower_back(dq, other, hidden, slope, features_t, features_other_t, w_out, peers):
    half = hidden.shape[1]
    rows = half * features_t.shape[0] // peers // LANES + 8
    held = (hidden, slope, features_t, features_other_t)
    return pl.pallas_call(
        tower_body,
        out_shape=jax.ShapeDtypeStruct((peers, rows, LANES), BF16),
        in_specs=vmem(2) + hbm(5),
        out_specs=vmem(1)[0],
        scratch_shapes=[pltpu.VMEM(a.shape, a.dtype) for a in held]
        + [pltpu.VMEM((half, w_out.shape[1]), BF16), pltpu.SemaphoreType.DMA((5,))],
        compiler_params=params(40),
        name="tower_back",
    )(dq, other, *in_hbm(held + (w_out,)))


def sum_body(parts_ref, out_ref):
    total = jnp.sum(parts_ref[...].astype(F32), axis=0, keepdims=True)
    out_ref[...] = jnp.broadcast_to(total, out_ref.shape).astype(BF16)


def sum_parts(parts):
    return pl.pallas_call(
        sum_body,
        out_shape=jax.ShapeDtypeStruct(parts.shape, BF16),
        in_specs=vmem(1),
        out_specs=vmem(1)[0],
        compiler_params=params(24),
        name="sum_parts",
    )(parts)


def spread_body(mine_ref, other_ref, hidden_ref, out_ref):
    peers = mine_ref.shape[0]
    core = lax.axis_index("dev") % 2
    half = out_ref.shape[0] // 2
    tall = hidden_ref.shape[0] // peers
    blocks = half // LANES
    filled = half // 8
    for side, ref in ((core, mine_ref), (1 - core, other_ref)):
        got = ref[...].astype(F32)
        for c in range(blocks):
            at = pl.multiple_of(side * half + c * LANES, LANES)
            hidden_ref[:, pl.ds(at, LANES)] = got[:, c * tall : (c + 1) * tall, :].reshape(
                hidden_ref.shape[0], LANES
            )
        at = blocks * tall
        out_ref[pl.ds(pl.multiple_of(side * half, half), half), :] = got[
            0:filled, at : at + 8, :
        ].reshape(half, LANES)


def spread(mine, other, hidden_shape, out_shape):
    return pl.pallas_call(
        spread_body,
        out_shape=(
            jax.ShapeDtypeStruct(hidden_shape, F32),
            jax.ShapeDtypeStruct(out_shape, F32),
        ),
        in_specs=vmem(2),
        out_specs=vmem(2),
        compiler_params=params(24),
        name="spread",
    )(mine, other)


def exchange(x):
    return lax.all_to_all(x, "dev", split_axis=0, concat_axis=0, tiled=True)


def exchange_peers(x):
    devices = lax.axis_size("dev")
    groups = [list(range(c, devices, 2)) for c in range(2)]
    return lax.all_to_all(
        x, "dev", split_axis=0, concat_axis=0, axis_index_groups=groups, tiled=True
    )


def swap(x):
    devices = lax.axis_size("dev")
    return lax.ppermute(x, "dev", [(d, d ^ 1) for d in range(devices)])


def local(
    features, w_hidden, w_out, items, routes, cluster_slot, sample_ids, sample_counts, positives
):
    devices = lax.axis_size("dev")
    features_other = swap(features)
    send, named, mine, other = route(
        routes, positives, cluster_slot, features, w_hidden, w_out, devices
    )
    mass, tabs = tables(sample_ids, sample_counts)
    got = exchange(send)
    theirs = swap(other)
    got, mass, tabs, theirs, features_other = lax.optimization_barrier(
        (got, *in_hbm((mass, tabs)), theirs, features_other)
    )
    dq_slots, weight, queries, losses = owner(got, items, mass, tabs)
    back = exchange(dq_slots)
    hidden, slope = ready(mine, theirs)
    item_grad = item_grads(weight, queries)
    features_t, features_other_t = features.T, features_other.T
    back, hidden, slope, item_grad, features_t, features_other_t = lax.optimization_barrier(
        (back, hidden, slope, item_grad, features_t, features_other_t)
    )
    dq = collect(back, named, features.shape[0])
    partial = tower_back(
        dq, swap(dq), hidden, slope, features_t, features_other_t, w_out, devices // 2
    )
    summed = exchange_peers(sum_parts(exchange_peers(partial)))
    grad_hidden, grad_out = spread(summed, swap(summed), w_hidden.shape, w_out.shape)
    slot_loss = losses[:, 0]
    return (slot_loss, grad_hidden, grad_out, item_grad)


def solution(mesh):
    in_specs = (
        P("dev", None),
        P(),
        P(),
        P("dev", None),
        P("dev", None),
        P(),
        P("dev", None),
        P("dev", None),
        P("dev", None),
    )
    out_specs = (P("dev"), P(), P(), P("dev", None))
    return jax.shard_map(local, mesh=mesh, in_specs=in_specs, out_specs=out_specs, check_vma=False)
```

time: 127 us -> 119 us (0.937)
  local copies, waits for them, and re-layouts: 13.9 us -> 2.56 us
  waiting for transfers between devices: 24.8 us -> 26.6 us
    unnamed x31 -> x9, local copies, waits for them, and re-layouts: 11.4 us -> 0.56 us
    pallas_call x2, Pallas kernels: 6.21 us -> 9.17 us  [the longest x1 6.73 us: tables(): pl.pallas_call(table_body, out_shape=outs_hbm(outs), in_specs=vmem(2), ou...]
    pallas_call x1, Pallas kernels: 7.92 us -> 5.13 us  [owner(): pl.pallas_call(owner_body, out_shape=outs_hbm(outs) + (jax.ShapeDtypeStru...]
    all_to_all x2, waiting for transfers between devices: 22.6 us -> 24.5 us  [exchange(): return lax.all_to_all(x, 'dev', split_axis=0, concat_axis=0, tiled=True)]
    pallas_call x1, Pallas kernels: 2.09 us -> 3.97 us  [item_grads(): pl.pallas_call(item_body, grid=(local // step,), out_shape=jax.ShapeDtype...]
    pallas_call x1, Pallas kernels: 8.03 us -> 6.43 us  [route(): pl.pallas_call(route_body, out_shape=outs_hbm(outs), in_specs=hbm(6), out...]
  transfers between devices with their start and end apart: 6 -> 6, of which waited for: 4 -> 4; matrix products, arithmetic and copies ran while one was open for 2% -> 3% of each run, Pallas kernels for 7% -> 11%
where the time goes in v3:
time: 119 us; the launch traced here: 118 us
  blocking collectives  34.1 us (29%)
  Pallas kernels  31.1 us (26%)
  waiting for transfers between devices  26.6 us (22%)
  starting transfers between devices  22.3 us (19%)
  local copies, waits for them, and re-layouts  2.56 us (2%)
    all_to_all x2, blocking collectives, exchange_peers(): lax.all_to_all(x, 'dev', split_axis=0, concat_axis=0, axis_index_groups=g...  34.1 us
    all_to_all x2, waiting for transfers between devices, exchange(): return lax.all_to_all(x, 'dev', split_axis=0, concat_axis=0, tiled=True)  24.5 us
    all_to_all x2, starting transfers between devices, exchange(): return lax.all_to_all(x, 'dev', split_axis=0, concat_axis=0, tiled=True)  16.1 us
    pallas_call x1, Pallas kernels, tables(): pl.pallas_call(table_body, out_shape=outs_hbm(outs), in_specs=vmem(2), ou...  6.73 us
    pallas_call x1, Pallas kernels, route(): pl.pallas_call(route_body, out_shape=outs_hbm(outs), in_specs=hbm(6), out...  6.43 us
    ppermute x4, starting transfers between devices, swap(): return lax.ppermute(x, 'dev', [(d, d ^ 1) for d in range(devices)])  6.21 us
    pallas_call x1, Pallas kernels, owner(): pl.pallas_call(owner_body, out_shape=outs_hbm(outs) + (jax.ShapeDtypeStru...  5.13 us
    pallas_call x1, Pallas kernels, item_grads(): pl.pallas_call(item_body, grid=(local // step,), out_shape=jax.ShapeDtype...  3.97 us
  transfers between devices with their start and end apart: 6, of which 4 were waited for; matrix products, arithmetic and copies ran while one was open for 3% of the time, Pallas kernels for 11%

profile of v3, /device:TPU:1, one launch (start us, length us, event | category | flops | bytes accessed | tf_op | source)
XLA Modules:
  0.0 118.1 jit_solution(10556708675594953251)
XLA Ops:
  0.6 6.4 %route.1 = (bf16[128,40,128]{2,1,0:T(8,128)(2,1)}, f32[128,128]{1,0:T(8,128)}, f32[512,256]{1,0:T(8,128)}, f32[512,256]{1,0:T(8,128)}) custom-call(s32[4,512]{1,0:T(4,128)} %bitcast.6, s32[4,512]{1,0:T(4,128)} %bitcast.7, s32[16,128]{1,0:T(8,128)} %bitcast.8, bf16[512,1024]{1,0:T(8,128)(2,1)} %feat_hbm.1, bf16[1024,512]{1,0:T(8,128)(2,1)} %wh_hbm.1, ...), custom_call_target="tpu_custom_call" | custom-call | tf_op jit(solution)/shard_map/route/pallas_call | solution.py:209
  7.1 11.5 %all-to-all-start = ((bf16[128,40,128]{2,1,0:T(8,128)(2,1)}), bf16[128,40,128]{2,1,0:T(8,128)(2,1)S(1)}, u32[]{:S(2)}, u32[]{:S(2)}) async-start(bf16[128,40,128]{2,1,0:T(8,128)(2,1)} %get-tuple-element.29), calls=%async_computation | async-start | bytes 2621440 | tf_op jit(solution)/shard_map/all_to_all | solution.py:641
  18.6 0.5 copy.15
  19.2 1.1 collective-permute-start.1
  20.4 1.0 reshape.18.ids_ref
  21.4 1.0 reshape.19.counts_ref
  22.4 6.7 %tables.1 = (f32[16,128,128]{2,1,0:T(8,128)}, s32[16,32,128]{2,1,0:T(8,128)}) custom-call(s32[512,128]{1,0:T(8,128)S(1)} %reshape.18.ids_ref, s32[512,128]{1,0:T(8,128)S(1)} %reshape.19.counts_ref), custom_call_target="tpu_custom_call" | custom-call | flops 30000000 | bytes 1048576 | tf_op jit(solution)/shard_map/tables/pallas_call | solution.py:257
  29.2 11.5 %all-to-all-done.got_ref = bf16[128,40,128]{2,1,0:T(8,128)(2,1)S(1)} async-done(((bf16[128,40,128]{2,1,0:T(8,128)(2,1)}), bf16[128,40,128]{2,1,0:T(8,128)(2,1)S(1)}, u32[]{:S(2)}, u32[]{:S(2)}) %all-to-all-start) | async-done | bytes 1310752 | tf_op jit(solution)/shard_map/all_to_all | solution.py:641
  40.7 5.1 %owner.1 = (bf16[128,32,128]{2,1,0:T(8,128)(2,1)}, bf16[16,128,256]{2,1,0:T(8,128)(2,1)}, bf16[16,256,128]{2,1,0:T(8,128)(2,1)}, f32[16,1]{1,0:T(8,128)S(1)}) custom-call(bf16[128,40,128]{2,1,0:T(8,128)(2,1)S(1)} %all-to-all-done.got_ref, bf16[2048,128]{1,0:T(8,128)(2,1)} %items_hbm.1, f32[16,128,128]{2,1,0:T(8,128)} %get-tuple-element.34.mass_hbm, ...), custom_call_target="tpu_custom_call" | custom-call | tf_op jit(solution)/shard_map/owner/pallas_call | solution.py:403
  45.8 4.6 %all-to-all-start.1 = ((bf16[128,32,128]{2,1,0:T(8,128)(2,1)}), bf16[128,32,128]{2,1,0:T(8,128)(2,1)S(1)}, u32[]{:S(2)}, u32[]{:S(2)}) async-start(bf16[128,32,128]{2,1,0:T(8,128)(2,1)} %get-tuple-element.37), calls=%async_computation.1 | async-start | bytes 2097152 | tf_op jit(solution)/shard_map/all_to_all | solution.py:641
  50.5 2.4 %ready.1 = (bf16[2,256,512]{2,1,0:T(8,128)(2,1)}, f32[2,512,256]{2,1,0:T(8,128)}) custom-call(f32[512,256]{1,0:T(8,128)} %get-tuple-element.38.mine_ref, f32[512,256]{1,0:T(8,128)} %copy-done.3), custom_call_target="tpu_custom_call" | custom-call | flops 3000000 | bytes 3145728 | tf_op jit(solution)/shard_map/ready/pallas_call | solution.py:465
  52.9 4.0 %item_grads.1 = f32[2048,128]{1,0:T(8,128)} custom-call(bf16[16,128,256]{2,1,0:T(8,128)(2,1)} %get-tuple-element.42.weight_ref, bf16[16,256,128]{2,1,0:T(8,128)(2,1)} %get-tuple-element.43.q_ref), custom_call_target="tpu_custom_call" | custom-call | flops 135000000 | bytes 3145728 | tf_op jit(solution)/shard_map/item_grads/pallas_call | solution.py:433
  56.9 13.0 %all-to-all-done.1.back_ref = bf16[128,32,128]{2,1,0:T(8,128)(2,1)S(1)} async-done(((bf16[128,32,128]{2,1,0:T(8,128)(2,1)}), bf16[128,32,128]{2,1,0:T(8,128)(2,1)S(1)}, u32[]{:S(2)}, u32[]{:S(2)}) %all-to-all-start.1) | async-done | bytes 1048608 | tf_op jit(solution)/shard_map/all_to_all | solution.py:641
  69.9 1.2 %collect.1.dq_ref = bf16[512,128]{1,0:T(8,128)(2,1)S(1)} custom-call(bf16[128,32,128]{2,1,0:T(8,128)(2,1)S(1)} %all-to-all-done.1.back_ref, f32[128,128]{1,0:T(8,128)S(1)} %copy-done), custom_call_target="tpu_custom_call" | custom-call | tf_op jit(solution)/shard_map/collect/pallas_call | solution.py:504
  71.1 1.4 %collective-permute-start.2 = (bf16[512,128]{1,0:T(8,128)(2,1)S(1)}, bf16[512,128]{1,0:T(8,128)(2,1)S(1)}, u32[]{:S(2)}, u32[]{:S(2)}) collective-permute-start(bf16[512,128]{1,0:T(8,128)(2,1)S(1)} %collect.1.dq_ref), channel_id=1, source_target_pairs={{0,1},{1,0},{2,3},{3,2},{4,5},{5,4},{6,7},{7,6},{8,9},{9,8},{10,11... | collective-permute-start | bytes 393224 | tf_op jit(solution)/shard_map/ppermute | solution.py:654
  72.5 1.0 collective-permute-done.2.other_ref
  73.5 3.3 %tower_back.1 = bf16[64,40,128]{2,1,0:T(8,128)(2,1)S(1)} custom-call(bf16[512,128]{1,0:T(8,128)(2,1)S(1)} %collect.1.dq_ref, bf16[512,128]{1,0:T(8,128)(2,1)S(1)} %collective-permute-done.2.other_ref, bf16[2,256,512]{2,1,0:T(8,128)(2,1)} %get-tuple-element.47.hidden_hbm, f32[2,512,256]{2,1,0:T(8,128)} %get-tuple-element.48.slope_hbm, ...), custom_call_target="tpu_custom_call" | custom-call | tf_op jit(solution)/shard_map/tower_back/pallas_call | solution.py:578
  76.9 17.6 %all_to_all.20.parts_ref = bf16[64,40,128]{2,1,0:T(8,128)(2,1)S(1)} all-to-all(bf16[64,40,128]{2,1,0:T(8,128)(2,1)S(1)} %tower_back.1), channel_id=1, replica_groups={{0,2,4,6,8,10,12,14,16,18,20,22,24,26,28,30,32,34,36,38,40,42,44,46,48,..., dimensions={0} | all-to-all | bytes 1310720 | tf_op jit(solution)/shard_map/all_to_all | solution.py:647
  94.5 0.1 sum_parts.1
  94.6 16.5 %all_to_all.21.mine_ref = bf16[64,40,128]{2,1,0:T(8,128)(2,1)S(1)} all-to-all(bf16[64,40,128]{2,1,0:T(8,128)(2,1)S(1)} %sum_parts.1), channel_id=1, replica_groups={{0,2,4,6,8,10,12,14,16,18,20,22,24,26,28,30,32,34,36,38,40,42,44,46,48,..., dimensions={0} | all-to-all | bytes 1310720 | tf_op jit(solution)/shard_map/all_to_all | solution.py:647
  111.1 3.5 %collective-permute-start.3 = (bf16[64,40,128]{2,1,0:T(8,128)(2,1)S(1)}, bf16[64,40,128]{2,1,0:T(8,128)(2,1)S(1)}, u32[]{:S(2)}, u32[]{:S(2)}) collective-permute-start(bf16[64,40,128]{2,1,0:T(8,128)(2,1)S(1)} %all_to_all.21.mine_ref), channel_id=1, source_target_pairs={{0,1},{1,0},{2,3},{3,2},{4,5},{5,4},{6,7},{7,6},{8,9},{9,8},{10,11... | collective-permute-start | bytes 1966088 | tf_op jit(solution)/shard_map/ppermute | solution.py:654
  114.7 0.6 reduce
  115.3 1.1 collective-permute-done.3.other_ref
  116.4 1.7 %spread.1 = (f32[1024,512]{1,0:T(8,128)}, f32[512,128]{1,0:T(8,128)}) custom-call(bf16[64,40,128]{2,1,0:T(8,128)(2,1)S(1)} %all_to_all.21.mine_ref, bf16[64,40,128]{2,1,0:T(8,128)(2,1)S(1)} %collective-permute-done.3.other_ref), custom_call_target="tpu_custom_call" | custom-call | tf_op jit(solution)/shard_map/spread/pallas_call | solution.py:627
  (11 shorter events, 0.1 us)
Async XLA Ops:
  7.1 11.5 %copy-start.1 = (bf16[512,1024]{1,0:T(8,128)(2,1)S(1)}, bf16[512,1024]{1,0:T(8,128)(2,1)}, u32[]{:S(2)}) copy-start(bf16[512,1024]{1,0:T(8,128)(2,1)} %feat_hbm.1) | copy-start | bytes 3145732
  7.1 33.6 %all-to-all-start = ((bf16[128,40,128]{2,1,0:T(8,128)(2,1)}), bf16[128,40,128]{2,1,0:T(8,128)(2,1)S(1)}, u32[]{:S(2)}, u32[]{:S(2)}) async-start(bf16[128,40,128]{2,1,0:T(8,128)(2,1)} %get-tuple-element.29), calls=%async_computation | async-start | bytes 2621440 | tf_op jit(solution)/shard_map/all_to_all | solution.py:641
  19.2 26.7 %copy-start.2 = (bf16[512,1024]{0,1:T(8,128)(2,1)}, bf16[512,1024]{0,1:T(8,128)(2,1)S(1)}, u32[]{:S(2)}) copy-start(bf16[512,1024]{0,1:T(8,128)(2,1)S(1)} %copy.15) | copy-start | bytes 3145732
  19.2 10.0 %collective-permute-start.1 = (bf16[512,1024]{0,1:T(8,128)(2,1)S(1)}, bf16[512,1024]{0,1:T(8,128)(2,1)}, u32[]{:S(2)}, u32[]{:S(2)}) collective-permute-start(bf16[512,1024]{0,1:T(8,128)(2,1)S(1)} %copy.15), channel_id=1, source_target_pairs={{0,1},{1,0},{2,3},{3,2},{4,5},{5,4},{6,7},{7,6},{8,9},{9,8},{10,11... | collective-permute-start | bytes 3145736 | tf_op jit(solution)/shard_map/ppermute | solution.py:654
  20.3 8.8 %collective-permute-start = (f32[512,256]{1,0:T(8,128)}, f32[512,256]{1,0:T(8,128)S(1)}, u32[]{:S(2)}, u32[]{:S(2)}) collective-permute-start(f32[512,256]{1,0:T(8,128)} %get-tuple-element.32), channel_id=1, source_target_pairs={{0,1},{1,0},{2,3},{3,2},{4,5},{5,4},{6,7},{7,6},{8,9},{9,8},{10,11... | collective-permute-start | bytes 1572872 | tf_op jit(solution)/shard_map/ppermute | solution.py:654
  29.1 16.7 %copy-start.3 = (f32[512,256]{1,0:T(8,128)}, f32[512,256]{1,0:T(8,128)S(1)}, u32[]{:S(2)}) copy-start(f32[512,256]{1,0:T(8,128)S(1)} %collective-permute-done.theirs_ref) | copy-start | bytes 1572868
  45.8 24.0 %all-to-all-start.1 = ((bf16[128,32,128]{2,1,0:T(8,128)(2,1)}), bf16[128,32,128]{2,1,0:T(8,128)(2,1)S(1)}, u32[]{:S(2)}, u32[]{:S(2)}) async-start(bf16[128,32,128]{2,1,0:T(8,128)(2,1)} %get-tuple-element.37), calls=%async_computation.1 | async-start | bytes 2097152 | tf_op jit(solution)/shard_map/all_to_all | solution.py:641
  52.9 17.0 %copy-start = (f32[128,128]{1,0:T(8,128)S(1)}, f32[128,128]{1,0:T(8,128)}, u32[]{:S(2)}) copy-start(f32[128,128]{1,0:T(8,128)} %get-tuple-element.46.named_ref) | copy-start | bytes 196612
  71.1 2.4 %collective-permute-start.2 = (bf16[512,128]{1,0:T(8,128)(2,1)S(1)}, bf16[512,128]{1,0:T(8,128)(2,1)S(1)}, u32[]{:S(2)}, u32[]{:S(2)}) collective-permute-start(bf16[512,128]{1,0:T(8,128)(2,1)S(1)} %collect.1.dq_ref), channel_id=1, source_target_pairs={{0,1},{1,0},{2,3},{3,2},{4,5},{5,4},{6,7},{7,6},{8,9},{9,8},{10,11... | collective-permute-start | bytes 393224 | tf_op jit(solution)/shard_map/ppermute | solution.py:654
  111.1 5.3 %collective-permute-start.3 = (bf16[64,40,128]{2,1,0:T(8,128)(2,1)S(1)}, bf16[64,40,128]{2,1,0:T(8,128)(2,1)S(1)}, u32[]{:S(2)}, u32[]{:S(2)}) collective-permute-start(bf16[64,40,128]{2,1,0:T(8,128)(2,1)S(1)} %all_to_all.21.mine_ref), channel_id=1, source_target_pairs={{0,1},{1,0},{2,3},{3,2},{4,5},{5,4},{6,7},{7,6},{8,9},{9,8},{10,11... | collective-permute-start | bytes 1966088 | tf_op jit(solution)/shard_map/ppermute | solution.py:654

commit v4 on v3

--- a/solution.py
+++ b/solution.py
@@ -1,3 +1,5 @@
+import functools
+
 import jax
 import jax.numpy as jnp
 from jax import lax
@@ -54,8 +56,6 @@
     wo_hbm,
     send_hbm,
     named_hbm,
-    mine_hbm,
-    other_hbm,
     routes_ref,
     pos_ref,
     cslot_ref,
@@ -64,8 +64,6 @@
     wo_ref,
     send_ref,
     named_ref,
-    mine_ref,
-    other_ref,
     place_ref,
     in_sem,
     out_sem,
@@ -111,11 +109,6 @@
     block = LANES
     groups = block // local
     sub = iota((block, users), 0).astype(F32)
-    lane_user = iota((block, users), 1).astype(F32)
-    tail_lane = iota((block, LANES), 1)
-    tail_row = iota((block, LANES), 0)
-    tail_hit = ((tail_lane & (local - 1)) == (tail_row & (local - 1))) & (tail_lane < 4 * local)
-    tail_kind = tail_lane // local
     stores = []
     named_lane = iota((block, LANES), 1)
     named = [jnp.zeros((block, LANES), F32)]
@@ -127,42 +120,40 @@
             key = jnp.where(slot_at == slots[r], keys[r], key)
         most = jnp.max(key, axis=1, keepdims=True)
         rest = jnp.sum(key, axis=1, keepdims=True) - most
-        ends = []
         parts = []
         for c, chosen in enumerate((most, rest)):
-            user = jnp.floor((chosen - 1.0) * (1.0 / KEY))
-            named[0] = jnp.where(named_lane == 2 * b + c, user, named[0])
-            mark = jnp.where(chosen > 0.0, chosen - user * KEY, 0.0)
-            top = jnp.floor(mark * (1.0 / 64.0))
-            ends += [top, mark - top * 64.0]
-            parts.append(jnp.where(lane_user == user, 1.0, 0.0).reshape(block // 8, 8, users))
+            named[0] = jnp.where(named_lane == 2 * b + c, chosen, named[0])
+            chosen = jnp.where(chosen > 0.0, chosen, -1.0)
+            parts.append(jnp.where(key == chosen, 1.0, 0.0).reshape(block // 8, 8, users))
         place = jnp.concatenate(parts, axis=1).reshape(2 * block, users).astype(BF16)
-        span = pl.ds(b * 2 * block, 2 * block)
-        place_ref[span, :] = place
-        tail = jnp.where(
-            tail_kind == 0,
-            ends[0],
-            jnp.where(tail_kind == 1, ends[1], jnp.where(tail_kind == 2, ends[2], ends[3])),
-        )
-        tail = jnp.where(tail_hit, tail, 0.0).reshape(groups, local, LANES)
-        tail = jnp.sum(tail, axis=1)
-        send_ref[b * groups : (b + 1) * groups, 2 * local : rows, :] = jnp.broadcast_to(
-            tail[:, None, :], (groups, rows - 2 * local, width)
-        ).astype(BF16)
-
-    early = 6
+        place_ref[b * 2 * block : (b + 1) * 2 * block, :] = place
+
+    def name_users():
+        user = jnp.floor((named[0] - 1.0) * (1.0 / KEY))
+        named_ref[...] = user
+        stores.append(pltpu.make_async_copy(named_ref, named_hbm, out_sem.at[0]))
+        stores[-1].start()
+        chosen = named[0].T
+        user = jnp.floor((chosen - 1.0) * (1.0 / KEY))
+        mark = jnp.where(chosen > 0.0, chosen - user * KEY, 0.0)
+        top = jnp.floor(mark * (1.0 / 64.0))
+        low = mark - top * 64.0
+        for b in range(clusters // block):
+            tail = jnp.concatenate([top[2 * b : 2 * b + 2], low[2 * b : 2 * b + 2]], axis=0)
+            tail = jnp.concatenate([tail, tail], axis=0)
+            send_ref[b * groups : (b + 1) * groups, 2 * local : rows, :] = jnp.broadcast_to(
+                tail[None], (groups, rows - 2 * local, width)
+            ).astype(BF16)
+        span = (slice(None), pl.ds(2 * local, rows - 2 * local))
+        stores.append(pltpu.make_async_copy(send_ref.at[span], send_hbm.at[span], out_sem.at[1]))
+        stores[-1].start()
+
+    early = 4
     for b in range(early):
         assign(b)
     for load in loads[3:]:
         load.wait()
     pre = mm(feat_ref[...], wh_ref[...])
-    half = pre.shape[1] // 2
-    core = lax.axis_index("dev") % 2
-    mine_ref[...] = jnp.where(core == 0, pre[:, 0:half], pre[:, half:])
-    other_ref[...] = jnp.where(core == 0, pre[:, half:], pre[:, 0:half])
-    for src, dst, i in ((mine_ref, mine_hbm, 0), (other_ref, other_hbm, 1)):
-        stores.append(pltpu.make_async_copy(src, dst, out_sem.at[i]))
-        stores[-1].start()
     hidden = (pre * jax.nn.sigmoid(pre)).astype(BF16)
     query = mm(hidden, wo_ref[...]).astype(BF16)
     blocks = clusters // block
@@ -170,14 +161,13 @@
         if b + early < blocks:
             assign(b + early)
         if b + early == blocks:
-            named_ref[...] = named[0]
-            stores.append(pltpu.make_async_copy(named_ref, named_hbm, out_sem.at[2]))
-            stores[-1].start()
+            name_users()
         sent = mm(place_ref[b * 2 * block : (b + 1) * 2 * block, :], query).astype(BF16)
-        span = pl.ds(b * groups, groups)
-        send_ref[span, 0 : 2 * local, :] = sent.reshape(groups, 2 * local, width)
+        send_ref[b * groups : (b + 1) * groups, 0 : 2 * local, :] = sent.reshape(
+            groups, 2 * local, width
+        )
         if b % 4 == 3:
-            span = pl.ds((b - 3) * groups, 4 * groups)
+            span = (pl.ds((b - 3) * groups, 4 * groups), pl.ds(0, 2 * local))
             stores.append(
                 pltpu.make_async_copy(send_ref.at[span], send_hbm.at[span], send_sem.at[b // 4])
             )
@@ -190,7 +180,6 @@
     users, visits = routes.shape
     clusters = cluster_slot.shape[0]
     width = w_out.shape[1]
-    hid = w_hidden.shape[1]
     rows = 2 * clusters // devices + 8
     args = (
         routes.T,
@@ -203,19 +192,17 @@
     outs = (
         jax.ShapeDtypeStruct((devices, rows, width), BF16),
         jax.ShapeDtypeStruct((LANES, LANES), F32),
-        jax.ShapeDtypeStruct((users, hid // 2), F32),
-        jax.ShapeDtypeStruct((users, hid // 2), F32),
     )
     return pl.pallas_call(
         route_body,
         out_shape=outs_hbm(outs),
         in_specs=hbm(6),
-        out_specs=hbm(4),
+        out_specs=hbm(2),
         scratch_shapes=[pltpu.VMEM(a.shape, a.dtype) for a in args + outs]
         + [
             pltpu.VMEM((2 * clusters, users), BF16),
             pltpu.SemaphoreType.DMA((6,)),
-            pltpu.SemaphoreType.DMA((3,)),
+            pltpu.SemaphoreType.DMA((2,)),
             pltpu.SemaphoreType.DMA((4,)),
         ],
         compiler_params=params(48),
@@ -311,12 +298,16 @@
     chunks = tabs_ref.shape[1]
     pairs = 2 * devices
     got32_ref[...] = got_ref[...].astype(F32).reshape(devices * rows, width)
-    tail = got32_ref[pl.ds(2 * local, devices, stride=rows), :].T
-    marks = [
-        tail[2 * c * local : (2 * c + 1) * local, :] * 64.0
-        + tail[(2 * c + 1) * local : (2 * c + 2) * local, :]
-        for c in range(2)
-    ]
+    place_at = lax.axis_index("dev") % (LANES // local) * local
+    tail_lane = iota((devices, LANES), 1)
+    tail = jnp.zeros((devices, LANES), F32)
+    for c in range(2):
+        top = got32_ref[pl.ds(2 * local + c, devices, stride=rows), :]
+        low = got32_ref[pl.ds(2 * local + 2 + c, devices, stride=rows), :]
+        moved = pltpu.roll(top * 64.0 + low, (LANES + c * local - place_at) % LANES, 1)
+        tail = jnp.where(tail_lane // local == c, moved, tail)
+    tail = tail.T
+    marks = [tail[c * local : (c + 1) * local, :] for c in range(2)]
     targets = [jnp.maximum(mark - 1.0, 0.0).astype(jnp.int32) for mark in marks]
     item_at = iota((LANES, pairs), 0)
     row_at = iota((chunks, devices), 0)
@@ -447,16 +438,21 @@
     )(*in_hbm((weight, queries)))
 
 
-def ready_body(mine_ref, theirs_ref, hidden_ref, slope_ref):
-    for i, ref in enumerate((mine_ref, theirs_ref)):
-        pre = ref[...]
+def ready_body(feat_ref, feat_other_ref, wh_ref, hidden_ref, slope_ref):
+    half = hidden_ref.shape[1]
+    core = lax.axis_index("dev") % 2
+    weight = wh_ref[:, pl.ds(pl.multiple_of(core * half, half), half)]
+    for i, ref in enumerate((feat_ref, feat_other_ref)):
+        pre = mm(weight, ref[...], ((0,), (0,)))
         sig = jax.nn.sigmoid(pre)
-        hidden_ref[i] = (pre * sig).T.astype(BF16)
-        slope_ref[i] = sig * (1.0 + pre * (1.0 - sig))
-
-
-def ready(mine, theirs):
-    users, half = mine.shape
+        hidden_ref[i] = (pre * sig).astype(BF16)
+        slope_ref[i] = (sig * (1.0 + pre * (1.0 - sig))).T
+
+
+def ready(features_t, features_other_t, w_hidden):
+    feats, users = features_t.shape
+    hid = w_hidden.shape[1]
+    half = hid // 2
     step = users // 2
     outs = (
         jax.ShapeDtypeStruct((2, half, users), BF16),
@@ -466,17 +462,18 @@
         ready_body,
         grid=(users // step,),
         out_shape=outs_hbm(outs),
-        in_specs=[pl.BlockSpec((step, half), lambda i: (i, 0))] * 2,
+        in_specs=[pl.BlockSpec((feats, step), lambda i: (0, i))] * 2
+        + [pl.BlockSpec((feats, hid), lambda i: (0, 0))],
         out_specs=[
             pl.BlockSpec((2, half, step), lambda i: (0, 0, i)),
             pl.BlockSpec((2, step, half), lambda i: (0, i, 0)),
         ],
-        compiler_params=params(16),
+        compiler_params=params(24),
         cost_estimate=pl.CostEstimate(
-            flops=3_000_000, bytes_accessed=3 << 20, transcendentals=1 << 19
+            flops=550_000_000, bytes_accessed=5 << 20, transcendentals=1 << 19
         ),
         name="ready",
-    )(*in_hbm((mine, theirs)))
+    )(*in_hbm((features_t, features_other_t, w_hidden)))
 
 
 def collect_body(back_ref, named_ref, dq_ref):
@@ -603,38 +600,62 @@
     )(parts)
 
 
-def spread_body(mine_ref, other_ref, hidden_ref, out_ref):
-    peers = mine_ref.shape[0]
-    core = lax.axis_index("dev") % 2
-    half = out_ref.shape[0] // 2
+def spread_body(side_of, got_ref, *refs):
+    hidden_hbm, out_hbm, hidden_ref, out_ref, sem = refs[-5:]
+    peers = got_ref.shape[0]
+    side = lax.axis_index("dev") % 2
+    side = side_of(side)
+    half = out_ref.shape[0]
     tall = hidden_ref.shape[0] // peers
     blocks = half // LANES
     filled = half // 8
-    for side, ref in ((core, mine_ref), (1 - core, other_ref)):
-        got = ref[...].astype(F32)
-        for c in range(blocks):
-            at = pl.multiple_of(side * half + c * LANES, LANES)
-            hidden_ref[:, pl.ds(at, LANES)] = got[:, c * tall : (c + 1) * tall, :].reshape(
-                hidden_ref.shape[0], LANES
+    stores = []
+    for c in range(blocks):
+        hidden_ref[:, c * LANES : (c + 1) * LANES] = (
+            got_ref[:, c * tall : (c + 1) * tall, :].astype(F32).reshape(-1, LANES)
+        )
+        at = pl.multiple_of(side * half + c * LANES, LANES)
+        stores.append(
+            pltpu.make_async_copy(
+                hidden_ref.at[:, pl.ds(c * LANES, LANES)],
+                hidden_hbm.at[:, pl.ds(at, LANES)],
+                sem.at[c],
             )
-        at = blocks * tall
-        out_ref[pl.ds(pl.multiple_of(side * half, half), half), :] = got[
-            0:filled, at : at + 8, :
-        ].reshape(half, LANES)
-
-
-def spread(mine, other, hidden_shape, out_shape):
-    return pl.pallas_call(
-        spread_body,
-        out_shape=(
-            jax.ShapeDtypeStruct(hidden_shape, F32),
-            jax.ShapeDtypeStruct(out_shape, F32),
-        ),
-        in_specs=vmem(2),
-        out_specs=vmem(2),
-        compiler_params=params(24),
+        )
+        stores[-1].start()
+    at = blocks * tall
+    out_ref[...] = got_ref[0:filled, at : at + 8, :].astype(F32).reshape(half, LANES)
+    stores.append(
+        pltpu.make_async_copy(
+            out_ref, out_hbm.at[pl.ds(pl.multiple_of(side * half, half), half), :], sem.at[blocks]
+        )
+    )
+    stores[-1].start()
+    for store in stores:
+        store.wait()
+
+
+def spread(got, side_of, hidden_shape, out_shape, begun=()):
+    half = out_shape[0] // 2
+    outs = (
+        jax.ShapeDtypeStruct(hidden_shape, F32),
+        jax.ShapeDtypeStruct(out_shape, F32),
+    )
+    return pl.pallas_call(
+        functools.partial(spread_body, side_of),
+        out_shape=outs_hbm(outs),
+        in_specs=vmem(1) + hbm(len(begun)),
+        out_specs=hbm(2),
+        scratch_shapes=[
+            pltpu.VMEM((hidden_shape[0], half), F32),
+            pltpu.VMEM((half, LANES), F32),
+            pltpu.SemaphoreType.DMA((half // LANES + 1,)),
+        ],
+        input_output_aliases={1 + i: i for i in range(len(begun))},
+        compiler_params=params(16),
+        cost_estimate=pl.CostEstimate(flops=300_000, bytes_accessed=2 << 20, transcendentals=0),
         name="spread",
-    )(mine, other)
+    )(got, *in_hbm(begun))
 
 
 def exchange(x):
@@ -658,30 +679,28 @@
     features, w_hidden, w_out, items, routes, cluster_slot, sample_ids, sample_counts, positives
 ):
     devices = lax.axis_size("dev")
-    features_other = swap(features)
-    send, named, mine, other = route(
-        routes, positives, cluster_slot, features, w_hidden, w_out, devices
-    )
+    features_t = features.T
+    features_other_t = swap(features_t)
+    send, named = route(routes, positives, cluster_slot, features, w_hidden, w_out, devices)
     mass, tabs = tables(sample_ids, sample_counts)
     got = exchange(send)
-    theirs = swap(other)
-    got, mass, tabs, theirs, features_other = lax.optimization_barrier(
-        (got, *in_hbm((mass, tabs)), theirs, features_other)
+    got, mass, tabs, features_other_t = lax.optimization_barrier(
+        (got, *in_hbm((mass, tabs)), features_other_t)
     )
     dq_slots, weight, queries, losses = owner(got, items, mass, tabs)
     back = exchange(dq_slots)
-    hidden, slope = ready(mine, theirs)
+    hidden, slope = ready(features_t, features_other_t, w_hidden)
     item_grad = item_grads(weight, queries)
-    features_t, features_other_t = features.T, features_other.T
-    back, hidden, slope, item_grad, features_t, features_other_t = lax.optimization_barrier(
-        (back, hidden, slope, item_grad, features_t, features_other_t)
-    )
+    back, hidden, slope, item_grad = lax.optimization_barrier((back, hidden, slope, item_grad))
     dq = collect(back, named, features.shape[0])
     partial = tower_back(
         dq, swap(dq), hidden, slope, features_t, features_other_t, w_out, devices // 2
     )
     summed = exchange_peers(sum_parts(exchange_peers(partial)))
-    grad_hidden, grad_out = spread(summed, swap(summed), w_hidden.shape, w_out.shape)
+    begun = spread(summed, lambda core: core, w_hidden.shape, w_out.shape)
+    grad_hidden, grad_out = spread(
+        swap(summed), lambda core: 1 - core, w_hidden.shape, w_out.shape, begun
+    )
     slot_loss = losses[:, 0]
     return (slot_loss, grad_hidden, grad_out, item_grad)
 

time: 119 us -> 118 us (level)
  waiting for transfers between devices: 26.6 us -> 24.1 us
  Pallas kernels: 31.1 us -> 32.4 us
    pallas_call x1, Pallas kernels: 2.44 us -> 3.92 us  [ready(): pl.pallas_call(ready_body, grid=(users // step,), out_shape=outs_hbm(outs...]
    all_to_all x2, waiting for transfers between devices: 24.5 us -> 23.1 us  [exchange(): return lax.all_to_all(x, 'dev', split_axis=0, concat_axis=0, tiled=True)]
    ppermute x4 -> x3, starting transfers between devices: 6.21 us -> 6.13 us  [swap(): return lax.ppermute(x, 'dev', [(d, d ^ 1) for d in range(devices)])]
  transfers between devices with their start and end apart: 6 -> 5, of which waited for: 4 -> 3; matrix products, arithmetic and copies ran while one was open for 3% -> 3% of each run, Pallas kernels for 11% -> 13%
where the time goes in v4:
time: 118 us; the launch traced here: 117 us
  blocking collectives  34.1 us (29%)
  Pallas kernels  32.4 us (27%)
  waiting for transfers between devices  24.1 us (20%)
  starting transfers between devices  22.2 us (19%)
  local copies, waits for them, and re-layouts  2.55 us (2%)
    all_to_all x2, blocking collectives, exchange_peers(): lax.all_to_all(x, 'dev', split_axis=0, concat_axis=0, axis_index_groups=g...  34.1 us
    all_to_all x2, waiting for transfers between devices, exchange(): return lax.all_to_all(x, 'dev', split_axis=0, concat_axis=0, tiled=True)  23.1 us
    all_to_all x2, starting transfers between devices, exchange(): return lax.all_to_all(x, 'dev', split_axis=0, concat_axis=0, tiled=True)  16.1 us
    pallas_call x1, Pallas kernels, tables(): pl.pallas_call(table_body, out_shape=outs_hbm(outs), in_specs=vmem(2), ou...  6.77 us
    ppermute x3, starting transfers between devices, swap(): return lax.ppermute(x, 'dev', [(d, d ^ 1) for d in range(devices)])  6.13 us
    pallas_call x1, Pallas kernels, route(): pl.pallas_call(route_body, out_shape=outs_hbm(outs), in_specs=hbm(6), out...  5.73 us
    pallas_call x1, Pallas kernels, owner(): pl.pallas_call(owner_body, out_shape=outs_hbm(outs) + (jax.ShapeDtypeStru...  5.23 us
    pallas_call x1, Pallas kernels, item_grads(): pl.pallas_call(item_body, grid=(local // step,), out_shape=jax.ShapeDtype...  3.94 us
  transfers between devices with their start and end apart: 5, of which 3 were waited for; matrix products, arithmetic and copies ran while one was open for 3% of the time, Pallas kernels for 13%

profile of v4, /device:TPU:1, one launch (start us, length us, event | category | flops | bytes accessed | tf_op | source)
XLA Modules:
  0.0 117.0 jit_solution(8793424907739616203)
XLA Ops:
  0.6 5.7 %route.1 = (bf16[128,40,128]{2,1,0:T(8,128)(2,1)}, f32[128,128]{1,0:T(8,128)}) custom-call(s32[4,512]{1,0:T(4,128)} %bitcast.7, s32[4,512]{1,0:T(4,128)} %bitcast.8, s32[16,128]{1,0:T(8,128)} %bitcast.9, bf16[512,1024]{1,0:T(8,128)(2,1)} %feat_hbm.1, bf16[1024,512]{1,0:T(8,128)(2,1)} %wh_ref.1, bf16[512,128]{1,0:T(8,128)(2,1)} %wo_hbm.3), custom_call_target="tpu_custom_call" | custom-call | tf_op jit(solution)/shard_map/route/pallas_call | solution.py:196
  6.4 11.5 %all-to-all-start = ((bf16[128,40,128]{2,1,0:T(8,128)(2,1)}), bf16[128,40,128]{2,1,0:T(8,128)(2,1)S(1)}, u32[]{:S(2)}, u32[]{:S(2)}) async-start(bf16[128,40,128]{2,1,0:T(8,128)(2,1)} %get-tuple-element.26), calls=%async_computation | async-start | bytes 2621440 | tf_op jit(solution)/shard_map/all_to_all | solution.py:662
  17.9 0.5 copy.16
  18.5 1.1 collective-permute-start
  19.6 1.0 reshape.18.ids_ref
  20.6 1.0 reshape.19.counts_ref
  21.6 6.8 %tables.1 = (f32[16,128,128]{2,1,0:T(8,128)}, s32[16,32,128]{2,1,0:T(8,128)}) custom-call(s32[512,128]{1,0:T(8,128)S(1)} %reshape.18.ids_ref, s32[512,128]{1,0:T(8,128)S(1)} %reshape.19.counts_ref), custom_call_target="tpu_custom_call" | custom-call | flops 30000000 | bytes 1048576 | tf_op jit(solution)/shard_map/tables/pallas_call | solution.py:244
  28.4 11.6 %all-to-all-done.got_ref = bf16[128,40,128]{2,1,0:T(8,128)(2,1)S(1)} async-done(((bf16[128,40,128]{2,1,0:T(8,128)(2,1)}), bf16[128,40,128]{2,1,0:T(8,128)(2,1)S(1)}, u32[]{:S(2)}, u32[]{:S(2)}) %all-to-all-start) | async-done | bytes 1310752 | tf_op jit(solution)/shard_map/all_to_all | solution.py:662
  40.0 5.2 %owner.1 = (bf16[128,32,128]{2,1,0:T(8,128)(2,1)}, bf16[16,128,256]{2,1,0:T(8,128)(2,1)}, bf16[16,256,128]{2,1,0:T(8,128)(2,1)}, f32[16,1]{1,0:T(8,128)S(1)}) custom-call(bf16[128,40,128]{2,1,0:T(8,128)(2,1)S(1)} %all-to-all-done.got_ref, bf16[2048,128]{1,0:T(8,128)(2,1)} %items_hbm.1, f32[16,128,128]{2,1,0:T(8,128)} %get-tuple-element.30.mass_hbm, ...), custom_call_target="tpu_custom_call" | custom-call | tf_op jit(solution)/shard_map/owner/pallas_call | solution.py:394
  45.2 4.6 %all-to-all-start.1 = ((bf16[128,32,128]{2,1,0:T(8,128)(2,1)}), bf16[128,32,128]{2,1,0:T(8,128)(2,1)S(1)}, u32[]{:S(2)}, u32[]{:S(2)}) async-start(bf16[128,32,128]{2,1,0:T(8,128)(2,1)} %get-tuple-element.33), calls=%async_computation.1 | async-start | bytes 2097152 | tf_op jit(solution)/shard_map/all_to_all | solution.py:662
  49.8 3.9 %item_grads.1 = f32[2048,128]{1,0:T(8,128)} custom-call(bf16[16,128,256]{2,1,0:T(8,128)(2,1)} %get-tuple-element.37.weight_ref, bf16[16,256,128]{2,1,0:T(8,128)(2,1)} %get-tuple-element.38.q_ref), custom_call_target="tpu_custom_call" | custom-call | flops 135000000 | bytes 3145728 | tf_op jit(solution)/shard_map/item_grads/pallas_call | solution.py:424
  53.8 3.9 %ready.1 = (bf16[2,256,512]{2,1,0:T(8,128)(2,1)}, f32[2,512,256]{2,1,0:T(8,128)}) custom-call(bf16[1024,512]{1,0:T(8,128)(2,1)} %bitcast.5, bf16[1024,512]{1,0:T(8,128)(2,1)} %collective-permute-done.feat_other_ref.feat_other_hbm, bf16[1024,512]{1,0:T(8,128)(2,1)} %wh_ref.1), custom_call_target="tpu_custom_call" | custom-call | flops 550000000 | bytes 5242880 | tf_op jit(solution)/shard_map/ready/pallas_call | solution.py:461
  57.7 11.5 %all-to-all-done.1.back_ref = bf16[128,32,128]{2,1,0:T(8,128)(2,1)S(1)} async-done(((bf16[128,32,128]{2,1,0:T(8,128)(2,1)}), bf16[128,32,128]{2,1,0:T(8,128)(2,1)S(1)}, u32[]{:S(2)}, u32[]{:S(2)}) %all-to-all-start.1) | async-done | bytes 1048608 | tf_op jit(solution)/shard_map/all_to_all | solution.py:662
  69.3 1.2 %collect.1.dq_ref = bf16[512,128]{1,0:T(8,128)(2,1)S(1)} custom-call(bf16[128,32,128]{2,1,0:T(8,128)(2,1)S(1)} %all-to-all-done.1.back_ref, f32[128,128]{1,0:T(8,128)S(1)} %copy-done), custom_call_target="tpu_custom_call" | custom-call | tf_op jit(solution)/shard_map/collect/pallas_call | solution.py:501
  70.5 1.4 %collective-permute-start.1 = (bf16[512,128]{1,0:T(8,128)(2,1)S(1)}, bf16[512,128]{1,0:T(8,128)(2,1)S(1)}, u32[]{:S(2)}, u32[]{:S(2)}) collective-permute-start(bf16[512,128]{1,0:T(8,128)(2,1)S(1)} %collect.1.dq_ref), channel_id=1, source_target_pairs={{0,1},{1,0},{2,3},{3,2},{4,5},{5,4},{6,7},{7,6},{8,9},{9,8},{10,11... | collective-permute-start | bytes 393224 | tf_op jit(solution)/shard_map/ppermute | solution.py:675
  71.9 1.0 collective-permute-done.1.other_ref
  72.9 3.3 %tower_back.1 = bf16[64,40,128]{2,1,0:T(8,128)(2,1)S(1)} custom-call(bf16[512,128]{1,0:T(8,128)(2,1)S(1)} %collect.1.dq_ref, bf16[512,128]{1,0:T(8,128)(2,1)S(1)} %collective-permute-done.1.other_ref, bf16[2,256,512]{2,1,0:T(8,128)(2,1)} %get-tuple-element.41.hidden_hbm, f32[2,512,256]{2,1,0:T(8,128)} %get-tuple-element.42.slope_hbm, ...), custom_call_target="tpu_custom_call" | custom-call | tf_op jit(solution)/shard_map/tower_back/pallas_call | solution.py:575
  76.3 17.6 %all_to_all.20.parts_ref = bf16[64,40,128]{2,1,0:T(8,128)(2,1)S(1)} all-to-all(bf16[64,40,128]{2,1,0:T(8,128)(2,1)S(1)} %tower_back.1), channel_id=1, replica_groups={{0,2,4,6,8,10,12,14,16,18,20,22,24,26,28,30,32,34,36,38,40,42,44,46,48,..., dimensions={0} | all-to-all | bytes 1310720 | tf_op jit(solution)/shard_map/all_to_all | solution.py:668
  93.9 0.1 sum_parts.1
  94.0 16.5 %all_to_all.21.got_ref = bf16[64,40,128]{2,1,0:T(8,128)(2,1)S(1)} all-to-all(bf16[64,40,128]{2,1,0:T(8,128)(2,1)S(1)} %sum_parts.1), channel_id=1, replica_groups={{0,2,4,6,8,10,12,14,16,18,20,22,24,26,28,30,32,34,36,38,40,42,44,46,48,..., dimensions={0} | all-to-all | bytes 1310720 | tf_op jit(solution)/shard_map/all_to_all | solution.py:668
  110.5 3.5 %collective-permute-start.2 = (bf16[64,40,128]{2,1,0:T(8,128)(2,1)S(1)}, bf16[64,40,128]{2,1,0:T(8,128)(2,1)S(1)}, u32[]{:S(2)}, u32[]{:S(2)}) collective-permute-start(bf16[64,40,128]{2,1,0:T(8,128)(2,1)S(1)} %all_to_all.21.got_ref), channel_id=1, source_target_pairs={{0,1},{1,0},{2,3},{3,2},{4,5},{5,4},{6,7},{7,6},{8,9},{9,8},{10,11... | collective-permute-start | bytes 1966088 | tf_op jit(solution)/shard_map/ppermute | solution.py:675
  114.1 0.6 reduce
  114.7 1.1 spread.2
  115.8 1.1 spread.3
  (8 shorter events, 0.0 us)
Async XLA Ops:
  0.6 17.3 %copy-start.2 = (bf16[512,1024]{1,0:T(8,128)(2,1)S(1)}, bf16[512,1024]{1,0:T(8,128)(2,1)}, u32[]{:S(2)}) copy-start(bf16[512,1024]{1,0:T(8,128)(2,1)} %feat_hbm.1) | copy-start | bytes 3145732
  6.4 33.6 %all-to-all-start = ((bf16[128,40,128]{2,1,0:T(8,128)(2,1)}), bf16[128,40,128]{2,1,0:T(8,128)(2,1)S(1)}, u32[]{:S(2)}, u32[]{:S(2)}) async-start(bf16[128,40,128]{2,1,0:T(8,128)(2,1)} %get-tuple-element.26), calls=%async_computation | async-start | bytes 2621440 | tf_op jit(solution)/shard_map/all_to_all | solution.py:662
  18.5 26.8 %copy-start.1 = (bf16[512,1024]{0,1:T(8,128)(2,1)}, bf16[512,1024]{0,1:T(8,128)(2,1)S(1)}, u32[]{:S(2)}) copy-start(bf16[512,1024]{0,1:T(8,128)(2,1)S(1)} %copy.16) | copy-start | bytes 3145732
  18.5 9.9 %collective-permute-start = (bf16[1024,512]{1,0:T(8,128)(2,1)S(1)}, bf16[1024,512]{1,0:T(8,128)(2,1)}, u32[]{:S(2)}, u32[]{:S(2)}) collective-permute-start(bf16[1024,512]{1,0:T(8,128)(2,1)S(1)} %bitcast.4), channel_id=1, source_target_pairs={{0,1},{1,0},{2,3},{3,2},{4,5},{5,4},{6,7},{7,6},{8,9},{9,8},{10,11... | collective-permute-start | bytes 3145736 | tf_op jit(solution)/shard_map/ppermute | solution.py:675
  45.2 24.0 %all-to-all-start.1 = ((bf16[128,32,128]{2,1,0:T(8,128)(2,1)}), bf16[128,32,128]{2,1,0:T(8,128)(2,1)S(1)}, u32[]{:S(2)}, u32[]{:S(2)}) async-start(bf16[128,32,128]{2,1,0:T(8,128)(2,1)} %get-tuple-element.33), calls=%async_computation.1 | async-start | bytes 2097152 | tf_op jit(solution)/shard_map/all_to_all | solution.py:662
  53.8 15.5 %copy-start = (f32[128,128]{1,0:T(8,128)S(1)}, f32[128,128]{1,0:T(8,128)}, u32[]{:S(2)}) copy-start(f32[128,128]{1,0:T(8,128)} %get-tuple-element.40.named_ref) | copy-start | bytes 196612
  70.5 2.4 %collective-permute-start.1 = (bf16[512,128]{1,0:T(8,128)(2,1)S(1)}, bf16[512,128]{1,0:T(8,128)(2,1)S(1)}, u32[]{:S(2)}, u32[]{:S(2)}) collective-permute-start(bf16[512,128]{1,0:T(8,128)(2,1)S(1)} %collect.1.dq_ref), channel_id=1, source_target_pairs={{0,1},{1,0},{2,3},{3,2},{4,5},{5,4},{6,7},{7,6},{8,9},{9,8},{10,11... | collective-permute-start | bytes 393224 | tf_op jit(solution)/shard_map/ppermute | solution.py:675
  110.5 5.3 %collective-permute-start.2 = (bf16[64,40,128]{2,1,0:T(8,128)(2,1)S(1)}, bf16[64,40,128]{2,1,0:T(8,128)(2,1)S(1)}, u32[]{:S(2)}, u32[]{:S(2)}) collective-permute-start(bf16[64,40,128]{2,1,0:T(8,128)(2,1)S(1)} %all_to_all.21.got_ref), channel_id=1, source_target_pairs={{0,1},{1,0},{2,3},{3,2},{4,5},{5,4},{6,7},{7,6},{8,9},{9,8},{10,11... | collective-permute-start | bytes 1966088 | tf_op jit(solution)/shard_map/ppermute | solution.py:675

commit v5 on v4

--- a/solution.py
+++ b/solution.py
@@ -438,15 +438,16 @@
     )(*in_hbm((weight, queries)))
 
 
-def ready_body(feat_ref, feat_other_ref, wh_ref, hidden_ref, slope_ref):
-    half = hidden_ref.shape[1]
+def ready_body(feat_ref, feat_other_ref, wh_ref, *outs):
+    half = outs[0].shape[0]
     core = lax.axis_index("dev") % 2
     weight = wh_ref[:, pl.ds(pl.multiple_of(core * half, half), half)]
     for i, ref in enumerate((feat_ref, feat_other_ref)):
+        hidden_ref, slope_ref = outs[2 * i : 2 * i + 2]
         pre = mm(weight, ref[...], ((0,), (0,)))
         sig = jax.nn.sigmoid(pre)
-        hidden_ref[i] = (pre * sig).astype(BF16)
-        slope_ref[i] = (sig * (1.0 + pre * (1.0 - sig))).T
+        hidden_ref[...] = (pre * sig).astype(BF16)
+        slope_ref[...] = (sig * (1.0 + pre * (1.0 - sig))).T
 
 
 def ready(features_t, features_other_t, w_hidden):
@@ -455,9 +456,9 @@
     half = hid // 2
     step = users // 2
     outs = (
-        jax.ShapeDtypeStruct((2, half, users), BF16),
-        jax.ShapeDtypeStruct((2, users, half), F32),
-    )
+        jax.ShapeDtypeStruct((half, users), BF16),
+        jax.ShapeDtypeStruct((users, half), F32),
+    ) * 2
     return pl.pallas_call(
         ready_body,
         grid=(users // step,),
@@ -465,9 +466,10 @@
         in_specs=[pl.BlockSpec((feats, step), lambda i: (0, i))] * 2
         + [pl.BlockSpec((feats, hid), lambda i: (0, 0))],
         out_specs=[
-            pl.BlockSpec((2, half, step), lambda i: (0, 0, i)),
-            pl.BlockSpec((2, step, half), lambda i: (0, i, 0)),
-        ],
+            pl.BlockSpec((half, step), lambda i: (0, i)),
+            pl.BlockSpec((step, half), lambda i: (i, 0)),
+        ]
+        * 2,
         compiler_params=params(24),
         cost_estimate=pl.CostEstimate(
             flops=550_000_000, bytes_accessed=5 << 20, transcendentals=1 << 19
@@ -508,25 +510,21 @@
     )(back, named)
 
 
-def tower_body(
+def own_body(
     dq_ref,
-    other_ref,
     hidden_hbm,
     slope_hbm,
     feat_hbm,
-    feat_other_hbm,
     wo_hbm,
-    grad_ref,
+    big_ref,
+    small_ref,
     hidden_ref,
     slope_ref,
     feat_ref,
-    feat_other_ref,
     wo_ref,
     sem,
 ):
-    users = dq_ref.shape[0]
-    half = hidden_ref.shape[1]
-    peers = grad_ref.shape[0]
+    half = hidden_ref.shape[0]
     core = lax.axis_index("dev") % 2
     wo_at = wo_hbm.at[pl.ds(pl.multiple_of(core * half, half), half), :]
     loads = [
@@ -536,7 +534,6 @@
                 (wo_at, wo_ref),
                 (slope_hbm, slope_ref),
                 (feat_hbm, feat_ref),
-                (feat_other_hbm, feat_other_ref),
                 (hidden_hbm, hidden_ref),
             ]
         )
@@ -545,17 +542,46 @@
         load.start()
     for load in loads[:2]:
         load.wait()
-    w_out = wo_ref[...]
-    dqs = (dq_ref[...], other_ref[...])
-    dpres = [
-        (mm(dq, w_out, ((1,), (1,))) * slope_ref[i]).astype(BF16) for i, dq in enumerate(dqs)
-    ]
+    dq = dq_ref[...]
+    dpre = (mm(dq, wo_ref[...], ((1,), (1,))) * slope_ref[...]).astype(BF16)
     loads[2].wait()
-    big = mm(feat_ref[...], dpres[0])
+    big_ref[...] = mm(feat_ref[...], dpre)
     loads[3].wait()
-    big = big + mm(feat_other_ref[...], dpres[1])
-    loads[4].wait()
-    small = mm(hidden_ref[0], dqs[0]) + mm(hidden_ref[1], dqs[1])
+    small_ref[...] = mm(hidden_ref[...], dq)
+
+
+def tower_own(dq, hidden, slope, features_t, w_out):
+    half = hidden.shape[0]
+    held = (hidden, slope, features_t)
+    return pl.pallas_call(
+        own_body,
+        out_shape=(
+            jax.ShapeDtypeStruct((features_t.shape[0], half), F32),
+            jax.ShapeDtypeStruct((half, dq.shape[1]), F32),
+        ),
+        in_specs=vmem(1) + hbm(4),
+        out_specs=vmem(2),
+        scratch_shapes=[pltpu.VMEM(a.shape, a.dtype) for a in held]
+        + [pltpu.VMEM((half, w_out.shape[1]), BF16), pltpu.SemaphoreType.DMA((4,))],
+        compiler_params=params(16),
+        cost_estimate=pl.CostEstimate(
+            flops=340_000_000, bytes_accessed=3 << 20, transcendentals=0
+        ),
+        name="tower_own",
+    )(dq, *in_hbm(held + (w_out,)))
+
+
+def other_body(
+    dq_ref, big_ref, small_ref, hidden_ref, slope_ref, feat_ref, wo_ref, grad_ref
+):
+    half = hidden_ref.shape[0]
+    peers = grad_ref.shape[0]
+    core = lax.axis_index("dev") % 2
+    w_out = wo_ref[pl.ds(pl.multiple_of(core * half, half), half), :]
+    dq = dq_ref[...]
+    dpre = (mm(dq, w_out, ((1,), (1,))) * slope_ref[...]).astype(BF16)
+    big = big_ref[...] + mm(feat_ref[...], dpre)
+    small = small_ref[...] + mm(hidden_ref[...], dq)
     tall = big.shape[0] // peers
     blocks = half // LANES
     for c in range(blocks):
@@ -568,20 +594,17 @@
     grad_ref[filled:peers, at : at + 8, :] = jnp.zeros((peers - filled, 8, LANES), BF16)
 
 
-def tower_back(dq, other, hidden, slope, features_t, features_other_t, w_out, peers):
-    half = hidden.shape[1]
+def tower_other(dq, big, small, hidden, slope, features_t, w_out, peers):
+    half = hidden.shape[0]
     rows = half * features_t.shape[0] // peers // LANES + 8
-    held = (hidden, slope, features_t, features_other_t)
-    return pl.pallas_call(
-        tower_body,
+    return pl.pallas_call(
+        other_body,
         out_shape=jax.ShapeDtypeStruct((peers, rows, LANES), BF16),
-        in_specs=vmem(2) + hbm(5),
+        in_specs=vmem(7),
         out_specs=vmem(1)[0],
-        scratch_shapes=[pltpu.VMEM(a.shape, a.dtype) for a in held]
-        + [pltpu.VMEM((half, w_out.shape[1]), BF16), pltpu.SemaphoreType.DMA((5,))],
-        compiler_params=params(40),
-        name="tower_back",
-    )(dq, other, *in_hbm(held + (w_out,)))
+        compiler_params=params(16),
+        name="tower_other",
+    )(dq, big, small, hidden, slope, features_t, w_out)
 
 
 def sum_body(parts_ref, out_ref):
@@ -689,12 +712,14 @@
     )
     dq_slots, weight, queries, losses = owner(got, items, mass, tabs)
     back = exchange(dq_slots)
-    hidden, slope = ready(features_t, features_other_t, w_hidden)
+    prepared = ready(features_t, features_other_t, w_hidden)
     item_grad = item_grads(weight, queries)
-    back, hidden, slope, item_grad = lax.optimization_barrier((back, hidden, slope, item_grad))
+    back, prepared, item_grad = lax.optimization_barrier((back, prepared, item_grad))
     dq = collect(back, named, features.shape[0])
-    partial = tower_back(
-        dq, swap(dq), hidden, slope, features_t, features_other_t, w_out, devices // 2
+    dq_other = swap(dq)
+    big, small = tower_own(dq, *prepared[0:2], features_t, w_out)
+    partial = tower_other(
+        dq_other, big, small, *prepared[2:4], features_other_t, w_out, devices // 2
     )
     summed = exchange_peers(sum_parts(exchange_peers(partial)))
     begun = spread(summed, lambda core: core, w_hidden.shape, w_out.shape)

time: 118 us -> 117 us (level)
    pallas_call x1 -> x2, Pallas kernels: 3.33 us -> 3.06 us  [the longest x1 2.28 us: tower_own(): pl.pallas_call(own_body, out_shape=(jax.ShapeDtypeStruct((features_t.shap...]
  transfers between devices with their start and end apart: 5 -> 5, of which waited for: 3 -> 2; matrix products, arithmetic and copies ran while one was open for 3% -> 2% of each run, Pallas kernels for 13% -> 15%
where the time goes in v5:
time: 117 us; the launch traced here: 116 us
  blocking collectives  34.7 us (30%)
  Pallas kernels  32.1 us (27%)
  waiting for transfers between devices  24.3 us (21%)
  starting transfers between devices  21.9 us (19%)
  local copies, waits for them, and re-layouts  1.49 us (1%)
    all_to_all x2, blocking collectives, exchange_peers(): lax.all_to_all(x, 'dev', split_axis=0, concat_axis=0, axis_index_groups=g...  34.7 us
    all_to_all x2, waiting for transfers between devices, exchange(): return lax.all_to_all(x, 'dev', split_axis=0, concat_axis=0, tiled=True)  24.3 us
    all_to_all x2, starting transfers between devices, exchange(): return lax.all_to_all(x, 'dev', split_axis=0, concat_axis=0, tiled=True)  16.1 us
    pallas_call x1, Pallas kernels, tables(): pl.pallas_call(table_body, out_shape=outs_hbm(outs), in_specs=vmem(2), ou...  6.73 us
    ppermute x3, starting transfers between devices, swap(): return lax.ppermute(x, 'dev', [(d, d ^ 1) for d in range(devices)])  5.81 us
    pallas_call x1, Pallas kernels, route(): pl.pallas_call(route_body, out_shape=outs_hbm(outs), in_specs=hbm(6), out...  5.73 us
    pallas_call x1, Pallas kernels, owner(): pl.pallas_call(owner_body, out_shape=outs_hbm(outs) + (jax.ShapeDtypeStru...  5.23 us
    pallas_call x1, Pallas kernels, item_grads(): pl.pallas_call(item_body, grid=(local // step,), out_shape=jax.ShapeDtype...  3.95 us
  transfers between devices with their start and end apart: 5, of which 2 were waited for; matrix products, arithmetic and copies ran while one was open for 2% of the time, Pallas kernels for 15%

profile of v5, /device:TPU:1, one launch (start us, length us, event | category | flops | bytes accessed | tf_op | source)
XLA Modules:
  0.0 116.2 jit_solution(14863324395564048980)
XLA Ops:
  0.6 5.7 %route.1 = (bf16[128,40,128]{2,1,0:T(8,128)(2,1)}, f32[128,128]{1,0:T(8,128)}) custom-call(s32[4,512]{1,0:T(4,128)} %bitcast.4, s32[4,512]{1,0:T(4,128)} %bitcast.5, s32[16,128]{1,0:T(8,128)} %bitcast.6, bf16[512,1024]{1,0:T(8,128)(2,1)} %feat_hbm.1, bf16[1024,512]{1,0:T(8,128)(2,1)} %wh_ref.1, bf16[512,128]{1,0:T(8,128)(2,1)} %wo_ref.1), custom_call_target="tpu_custom_call" | custom-call | tf_op jit(solution)/shard_map/route/pallas_call | solution.py:196
  6.4 0.0 copy-start.8
  6.4 11.5 %all-to-all-start = ((bf16[128,40,128]{2,1,0:T(8,128)(2,1)}), bf16[128,40,128]{2,1,0:T(8,128)(2,1)S(1)}, u32[]{:S(2)}, u32[]{:S(2)}) async-start(bf16[128,40,128]{2,1,0:T(8,128)(2,1)} %get-tuple-element.32), calls=%async_computation | async-start | bytes 2621440 | tf_op jit(solution)/shard_map/all_to_all | solution.py:685
  17.9 1.4 %copy.16 = bf16[512,1024]{0,1:T(8,128)(2,1)} copy(bf16[512,1024]{1,0:T(8,128)(2,1)S(1)} %copy-done.6) | data formatting | bytes 2097152 | tf_op args[0]
  19.3 1.1 collective-permute-start
  20.5 6.7 %tables.1 = (f32[16,128,128]{2,1,0:T(8,128)}, s32[16,32,128]{2,1,0:T(8,128)}) custom-call(s32[512,128]{1,0:T(8,128)S(1)} %reshape.18.ids_ref, s32[512,128]{1,0:T(8,128)S(1)} %reshape.19.counts_ref), custom_call_target="tpu_custom_call" | custom-call | flops 30000000 | bytes 1048576 | tf_op jit(solution)/shard_map/tables/pallas_call | solution.py:244
  27.2 12.8 %all-to-all-done.got_ref = bf16[128,40,128]{2,1,0:T(8,128)(2,1)S(1)} async-done(((bf16[128,40,128]{2,1,0:T(8,128)(2,1)}), bf16[128,40,128]{2,1,0:T(8,128)(2,1)S(1)}, u32[]{:S(2)}, u32[]{:S(2)}) %all-to-all-start) | async-done | bytes 1310752 | tf_op jit(solution)/shard_map/all_to_all | solution.py:685
  40.0 5.2 %owner.1 = (bf16[128,32,128]{2,1,0:T(8,128)(2,1)}, bf16[16,128,256]{2,1,0:T(8,128)(2,1)}, bf16[16,256,128]{2,1,0:T(8,128)(2,1)}, f32[16,1]{1,0:T(8,128)S(1)}) custom-call(bf16[128,40,128]{2,1,0:T(8,128)(2,1)S(1)} %all-to-all-done.got_ref, bf16[2048,128]{1,0:T(8,128)(2,1)} %items_hbm.1, f32[16,128,128]{2,1,0:T(8,128)} %get-tuple-element.36.mass_hbm, ...), custom_call_target="tpu_custom_call" | custom-call | tf_op jit(solution)/shard_map/owner/pallas_call | solution.py:394
  45.3 4.6 %all-to-all-start.1 = ((bf16[128,32,128]{2,1,0:T(8,128)(2,1)}), bf16[128,32,128]{2,1,0:T(8,128)(2,1)S(1)}, u32[]{:S(2)}, u32[]{:S(2)}) async-start(bf16[128,32,128]{2,1,0:T(8,128)(2,1)} %get-tuple-element.39), calls=%async_computation.1 | async-start | bytes 2097152 | tf_op jit(solution)/shard_map/all_to_all | solution.py:685
  49.9 3.9 %item_grads.1 = f32[2048,128]{1,0:T(8,128)} custom-call(bf16[16,128,256]{2,1,0:T(8,128)(2,1)} %get-tuple-element.45.weight_ref, bf16[16,256,128]{2,1,0:T(8,128)(2,1)} %get-tuple-element.46.q_ref), custom_call_target="tpu_custom_call" | custom-call | flops 135000000 | bytes 3145728 | tf_op jit(solution)/shard_map/item_grads/pallas_call | solution.py:424
  53.8 3.9 %ready.1 = (bf16[256,512]{1,0:T(8,128)(2,1)}, f32[512,256]{1,0:T(8,128)}, bf16[256,512]{1,0:T(8,128)(2,1)}, f32[512,256]{1,0:T(8,128)}) custom-call(bf16[1024,512]{1,0:T(8,128)(2,1)} %bitcast.3.feat_ref.feat_hbm, bf16[1024,512]{1,0:T(8,128)(2,1)} %copy-done, bf16[1024,512]{1,0:T(8,128)(2,1)} %wh_ref.1), custom_call_target="tpu_custom_call" | custom-call | flops 550000000 | bytes 5242880 | tf_op jit(solution)/shard_map/ready/pallas_call | solution.py:462
  57.8 11.5 %all-to-all-done.1.back_ref = bf16[128,32,128]{2,1,0:T(8,128)(2,1)S(1)} async-done(((bf16[128,32,128]{2,1,0:T(8,128)(2,1)}), bf16[128,32,128]{2,1,0:T(8,128)(2,1)S(1)}, u32[]{:S(2)}, u32[]{:S(2)}) %all-to-all-start.1) | async-done | bytes 1048608 | tf_op jit(solution)/shard_map/all_to_all | solution.py:685
  69.3 1.2 %collect.1.dq_ref = bf16[512,128]{1,0:T(8,128)(2,1)S(1)} custom-call(bf16[128,32,128]{2,1,0:T(8,128)(2,1)S(1)} %all-to-all-done.1.back_ref, f32[128,128]{1,0:T(8,128)S(1)} %copy-done.5), custom_call_target="tpu_custom_call" | custom-call | tf_op jit(solution)/shard_map/collect/pallas_call | solution.py:503
  70.5 1.4 %collective-permute-start.1 = (bf16[512,128]{1,0:T(8,128)(2,1)S(1)}, bf16[512,128]{1,0:T(8,128)(2,1)S(1)}, u32[]{:S(2)}, u32[]{:S(2)}) collective-permute-start(bf16[512,128]{1,0:T(8,128)(2,1)S(1)} %collect.1.dq_ref), channel_id=1, source_target_pairs={{0,1},{1,0},{2,3},{3,2},{4,5},{5,4},{6,7},{7,6},{8,9},{9,8},{10,11... | collective-permute-start | bytes 393224 | tf_op jit(solution)/shard_map/ppermute | solution.py:698
  72.0 2.3 %tower_own.1 = (f32[1024,256]{1,0:T(8,128)S(1)}, f32[256,128]{1,0:T(8,128)S(1)}) custom-call(bf16[512,128]{1,0:T(8,128)(2,1)S(1)} %collect.1.dq_ref, bf16[256,512]{1,0:T(8,128)(2,1)} %get-tuple-element.49.hidden_hbm, f32[512,256]{1,0:T(8,128)} %get-tuple-element.50.slope_hbm, bf16[1024,512]{1,0:T(8,128)(2,1)} %bitcast.3.feat_ref.feat_hbm, ...), custom_call_target="tpu_custom_call" | custom-call | flops 340000000 | bytes 3145728 | tf_op jit(solution)/shard_map/tower_own/pallas_call | solution.py:556
  74.3 0.8 tower_other.1
  75.1 17.7 %all_to_all.20.parts_ref = bf16[64,40,128]{2,1,0:T(8,128)(2,1)S(1)} all-to-all(bf16[64,40,128]{2,1,0:T(8,128)(2,1)S(1)} %tower_other.1), channel_id=1, replica_groups={{0,2,4,6,8,10,12,14,16,18,20,22,24,26,28,30,32,34,36,38,40,42,44,46,48,..., dimensions={0} | all-to-all | bytes 1310720 | tf_op jit(solution)/shard_map/all_to_all | solution.py:691
  92.8 0.1 sum_parts.1
  92.9 17.1 %all_to_all.21.got_ref = bf16[64,40,128]{2,1,0:T(8,128)(2,1)S(1)} all-to-all(bf16[64,40,128]{2,1,0:T(8,128)(2,1)S(1)} %sum_parts.1), channel_id=1, replica_groups={{0,2,4,6,8,10,12,14,16,18,20,22,24,26,28,30,32,34,36,38,40,42,44,46,48,..., dimensions={0} | all-to-all | bytes 1310720 | tf_op jit(solution)/shard_map/all_to_all | solution.py:691
  110.0 3.3 %collective-permute-start.2 = (bf16[64,40,128]{2,1,0:T(8,128)(2,1)S(1)}, bf16[64,40,128]{2,1,0:T(8,128)(2,1)S(1)}, u32[]{:S(2)}, u32[]{:S(2)}) collective-permute-start(bf16[64,40,128]{2,1,0:T(8,128)(2,1)S(1)} %all_to_all.21.got_ref), channel_id=1, source_target_pairs={{0,1},{1,0},{2,3},{3,2},{4,5},{5,4},{6,7},{7,6},{8,9},{9,8},{10,11... | collective-permute-start | bytes 1966088 | tf_op jit(solution)/shard_map/ppermute | solution.py:698
  113.3 0.6 reduce
  113.9 1.1 spread.2
  115.0 0.0 collective-permute-done.2.got_ref
  115.0 1.1 spread.3
  (21 shorter events, 0.1 us)
Async XLA Ops:
  0.6 17.3 %copy-start.6 = (bf16[512,1024]{1,0:T(8,128)(2,1)S(1)}, bf16[512,1024]{1,0:T(8,128)(2,1)}, u32[]{:S(2)}) copy-start(bf16[512,1024]{1,0:T(8,128)(2,1)} %feat_hbm.1) | copy-start | bytes 3145732
  6.4 14.0 %copy-start.7 = (s32[16,4096]{1,0:T(8,128)S(1)}, s32[16,4096]{1,0:T(8,128)}, u32[]{:S(2)}) copy-start(s32[16,4096]{1,0:T(8,128)} %param.15) | copy-start | bytes 786436
  6.4 14.0 %copy-start.8 = (s32[16,4096]{1,0:T(8,128)S(1)}, s32[16,4096]{1,0:T(8,128)}, u32[]{:S(2)}) copy-start(s32[16,4096]{1,0:T(8,128)} %param.16) | copy-start | bytes 786436
  6.4 33.6 %all-to-all-start = ((bf16[128,40,128]{2,1,0:T(8,128)(2,1)}), bf16[128,40,128]{2,1,0:T(8,128)(2,1)S(1)}, u32[]{:S(2)}, u32[]{:S(2)}) async-start(bf16[128,40,128]{2,1,0:T(8,128)(2,1)} %get-tuple-element.32), calls=%async_computation | async-start | bytes 2621440 | tf_op jit(solution)/shard_map/all_to_all | solution.py:685
  19.3 7.9 %collective-permute-start = (bf16[1024,512]{1,0:T(8,128)(2,1)}, bf16[1024,512]{1,0:T(8,128)(2,1)S(1)}, u32[]{:S(2)}, u32[]{:S(2)}) collective-permute-start(bf16[1024,512]{1,0:T(8,128)(2,1)} %bitcast.3.feat_ref.feat_hbm), channel_id=1, source_target_pairs={{0,1},{1,0},{2,3},{3,2},{4,5},{5,4},{6,7},{7,6},{8,9},{9,8},{10,11... | collective-permute-start | bytes 3145736 | tf_op jit(solution)/shard_map/ppermute | solution.py:698
  27.2 18.0 %copy-start = (bf16[1024,512]{1,0:T(8,128)(2,1)}, bf16[1024,512]{1,0:T(8,128)(2,1)S(1)}, u32[]{:S(2)}) copy-start(bf16[1024,512]{1,0:T(8,128)(2,1)S(1)} %collective-permute-done.feat_other_ref.feat_ref) | copy-start | bytes 3145732
  45.3 24.0 %all-to-all-start.1 = ((bf16[128,32,128]{2,1,0:T(8,128)(2,1)}), bf16[128,32,128]{2,1,0:T(8,128)(2,1)S(1)}, u32[]{:S(2)}, u32[]{:S(2)}) async-start(bf16[128,32,128]{2,1,0:T(8,128)(2,1)} %get-tuple-element.39), calls=%async_computation.1 | async-start | bytes 2097152 | tf_op jit(solution)/shard_map/all_to_all | solution.py:685
  53.8 15.5 %copy-start.5 = (f32[128,128]{1,0:T(8,128)S(1)}, f32[128,128]{1,0:T(8,128)}, u32[]{:S(2)}) copy-start(f32[128,128]{1,0:T(8,128)} %get-tuple-element.48.named_ref) | copy-start | bytes 196612
  57.7 16.5 %copy-start.1 = (bf16[1024,512]{1,0:T(8,128)(2,1)S(1)}, bf16[1024,512]{1,0:T(8,128)(2,1)}, u32[]{:S(2)}) copy-start(bf16[1024,512]{1,0:T(8,128)(2,1)} %copy-done) | copy-start | bytes 3145732
  57.7 16.5 %copy-start.2 = (bf16[512,128]{1,0:T(8,128)(2,1)S(1)}, bf16[512,128]{1,0:T(8,128)(2,1)}, u32[]{:S(2)}) copy-start(bf16[512,128]{1,0:T(8,128)(2,1)} %wo_ref.1) | copy-start | bytes 393220
  57.8 16.5 %copy-start.3 = (f32[512,256]{1,0:T(8,128)S(1)}, f32[512,256]{1,0:T(8,128)}, u32[]{:S(2)}) copy-start(f32[512,256]{1,0:T(8,128)} %get-tuple-element.54.slope_ref) | copy-start | bytes 1572868
  57.8 16.5 %copy-start.4 = (bf16[256,512]{1,0:T(8,128)(2,1)S(1)}, bf16[256,512]{1,0:T(8,128)(2,1)}, u32[]{:S(2)}) copy-start(bf16[256,512]{1,0:T(8,128)(2,1)} %get-tuple-element.53.hidden_ref) | copy-start | bytes 786436
  70.5 3.7 %collective-permute-start.1 = (bf16[512,128]{1,0:T(8,128)(2,1)S(1)}, bf16[512,128]{1,0:T(8,128)(2,1)S(1)}, u32[]{:S(2)}, u32[]{:S(2)}) collective-permute-start(bf16[512,128]{1,0:T(8,128)(2,1)S(1)} %collect.1.dq_ref), channel_id=1, source_target_pairs={{0,1},{1,0},{2,3},{3,2},{4,5},{5,4},{6,7},{7,6},{8,9},{9,8},{10,11... | collective-permute-start | bytes 393224 | tf_op jit(solution)/shard_map/ppermute | solution.py:698
  110.0 5.0 %collective-permute-start.2 = (bf16[64,40,128]{2,1,0:T(8,128)(2,1)S(1)}, bf16[64,40,128]{2,1,0:T(8,128)(2,1)S(1)}, u32[]{:S(2)}, u32[]{:S(2)}) collective-permute-start(bf16[64,40,128]{2,1,0:T(8,128)(2,1)S(1)} %all_to_all.21.got_ref), channel_id=1, source_target_pairs={{0,1},{1,0},{2,3},{3,2},{4,5},{5,4},{6,7},{7,6},{8,9},{9,8},{10,11... | collective-permute-start | bytes 1966088 | tf_op jit(solution)/shard_map/ppermute | solution.py:698

commit v6 on v5

--- a/solution.py
+++ b/solution.py
@@ -11,7 +11,7 @@
 BF16 = jnp.bfloat16
 NONE = -3.0e38
 KEY = 4096
-AHEAD = 1
+AHEAD = 3
 LANES = 128
 
 
@@ -25,6 +25,10 @@
 
 def outs_hbm(arrays):
     return tuple(pltpu.HBM(a.shape, a.dtype) for a in arrays)
+
+
+def outs_vmem(arrays):
+    return tuple(pltpu.VMEM(a.shape, a.dtype) for a in arrays)
 
 
 def hbm(count):
@@ -478,46 +482,14 @@
     )(*in_hbm((features_t, features_other_t, w_hidden)))
 
 
-def collect_body(back_ref, named_ref, dq_ref):
-    devices, rows, width = back_ref.shape
-    users = dq_ref.shape[0]
-    block = LANES
-    named = named_ref[...]
-    lane_user = iota((block, users), 1).astype(F32)
-    total = jnp.zeros((width, users), F32)
-    group = 2 * block // rows
-    for b in range(devices // group):
-        parts = [
-            jnp.where(lane_user == named[:, 2 * b + c : 2 * b + c + 1], 1.0, 0.0).reshape(
-                block // 8, 8, users
-            )
-            for c in range(2)
-        ]
-        place = jnp.concatenate(parts, axis=1).reshape(2 * block, users).astype(BF16)
-        back = back_ref[b * group : (b + 1) * group].reshape(2 * block, width)
-        total = total + mm(back, place, ((0,), (0,)))
-    dq_ref[...] = total.T.astype(BF16)
-
-
-def collect(back, named, users):
-    return pl.pallas_call(
-        collect_body,
-        out_shape=jax.ShapeDtypeStruct((users, back.shape[2]), BF16),
-        in_specs=vmem(2),
-        out_specs=vmem(1)[0],
-        compiler_params=params(24),
-        name="collect",
-    )(back, named)
-
-
-def own_body(
-    dq_ref,
+def collect_body(
+    back_ref,
+    named_ref,
     hidden_hbm,
     slope_hbm,
     feat_hbm,
     wo_hbm,
-    big_ref,
-    small_ref,
+    dq_ref,
     hidden_ref,
     slope_ref,
     feat_ref,
@@ -540,35 +512,73 @@
     ]
     for load in loads:
         load.start()
-    for load in loads[:2]:
+    devices, rows, width = back_ref.shape
+    users = dq_ref.shape[0]
+    block = LANES
+    named = named_ref[...]
+    lane_user = iota((block, users), 1).astype(F32)
+    total = jnp.zeros((width, users), F32)
+    group = 2 * block // rows
+    for b in range(devices // group):
+        parts = [
+            jnp.where(lane_user == named[:, 2 * b + c : 2 * b + c + 1], 1.0, 0.0).reshape(
+                block // 8, 8, users
+            )
+            for c in range(2)
+        ]
+        place = jnp.concatenate(parts, axis=1).reshape(2 * block, users).astype(BF16)
+        back = back_ref[b * group : (b + 1) * group].reshape(2 * block, width)
+        total = total + mm(back, place, ((0,), (0,)))
+    dq_ref[...] = total.T.astype(BF16)
+    for load in loads:
         load.wait()
+
+
+def collect(back, named, hidden, slope, features_t, w_out):
+    half, users = hidden.shape
+    width = back.shape[2]
+    return pl.pallas_call(
+        collect_body,
+        out_shape=outs_vmem(
+            (
+                jax.ShapeDtypeStruct((users, width), BF16),
+                hidden,
+                slope,
+                features_t,
+                jax.ShapeDtypeStruct((half, width), BF16),
+            )
+        ),
+        in_specs=vmem(2) + hbm(4),
+        out_specs=vmem(5),
+        scratch_shapes=[pltpu.SemaphoreType.DMA((4,))],
+        compiler_params=params(24),
+        name="collect",
+    )(back, named, *in_hbm((hidden, slope, features_t, w_out)))
+
+
+def own_body(dq_ref, hidden_ref, slope_ref, feat_ref, wo_ref, big_ref, small_ref):
     dq = dq_ref[...]
     dpre = (mm(dq, wo_ref[...], ((1,), (1,))) * slope_ref[...]).astype(BF16)
-    loads[2].wait()
     big_ref[...] = mm(feat_ref[...], dpre)
-    loads[3].wait()
     small_ref[...] = mm(hidden_ref[...], dq)
 
 
-def tower_own(dq, hidden, slope, features_t, w_out):
+def tower_own(dq, hidden, slope, features_t, w_half):
     half = hidden.shape[0]
-    held = (hidden, slope, features_t)
     return pl.pallas_call(
         own_body,
         out_shape=(
             jax.ShapeDtypeStruct((features_t.shape[0], half), F32),
             jax.ShapeDtypeStruct((half, dq.shape[1]), F32),
         ),
-        in_specs=vmem(1) + hbm(4),
+        in_specs=vmem(5),
         out_specs=vmem(2),
-        scratch_shapes=[pltpu.VMEM(a.shape, a.dtype) for a in held]
-        + [pltpu.VMEM((half, w_out.shape[1]), BF16), pltpu.SemaphoreType.DMA((4,))],
         compiler_params=params(16),
         cost_estimate=pl.CostEstimate(
             flops=340_000_000, bytes_accessed=3 << 20, transcendentals=0
         ),
         name="tower_own",
-    )(dq, *in_hbm(held + (w_out,)))
+    )(dq, hidden, slope, features_t, w_half)
 
 
 def other_body(
@@ -576,10 +586,8 @@
 ):
     half = hidden_ref.shape[0]
     peers = grad_ref.shape[0]
-    core = lax.axis_index("dev") % 2
-    w_out = wo_ref[pl.ds(pl.multiple_of(core * half, half), half), :]
     dq = dq_ref[...]
-    dpre = (mm(dq, w_out, ((1,), (1,))) * slope_ref[...]).astype(BF16)
+    dpre = (mm(dq, wo_ref[...], ((1,), (1,))) * slope_ref[...]).astype(BF16)
     big = big_ref[...] + mm(feat_ref[...], dpre)
     small = small_ref[...] + mm(hidden_ref[...], dq)
     tall = big.shape[0] // peers
@@ -594,7 +602,7 @@
     grad_ref[filled:peers, at : at + 8, :] = jnp.zeros((peers - filled, 8, LANES), BF16)
 
 
-def tower_other(dq, big, small, hidden, slope, features_t, w_out, peers):
+def tower_other(dq, big, small, hidden, slope, features_t, w_half, peers):
     half = hidden.shape[0]
     rows = half * features_t.shape[0] // peers // LANES + 8
     return pl.pallas_call(
@@ -604,7 +612,7 @@
         out_specs=vmem(1)[0],
         compiler_params=params(16),
         name="tower_other",
-    )(dq, big, small, hidden, slope, features_t, w_out)
+    )(dq, big, small, hidden, slope, features_t, w_half)
 
 
 def sum_body(parts_ref, out_ref):
@@ -715,11 +723,11 @@
     prepared = ready(features_t, features_other_t, w_hidden)
     item_grad = item_grads(weight, queries)
     back, prepared, item_grad = lax.optimization_barrier((back, prepared, item_grad))
-    dq = collect(back, named, features.shape[0])
+    dq, *held, w_half = collect(back, named, *prepared[0:2], features_t, w_out)
     dq_other = swap(dq)
-    big, small = tower_own(dq, *prepared[0:2], features_t, w_out)
+    big, small = tower_own(dq, *held, w_half)
     partial = tower_other(
-        dq_other, big, small, *prepared[2:4], features_other_t, w_out, devices // 2
+        dq_other, big, small, *prepared[2:4], features_other_t, w_half, devices // 2
     )
     summed = exchange_peers(sum_parts(exchange_peers(partial)))
     begun = spread(summed, lambda core: core, w_hidden.shape, w_out.shape)

time: 117 us -> 116 us (level)
    pallas_call x1, Pallas kernels: 2.28 us -> 0.76 us  [tower_own(): pl.pallas_call(own_body, out_shape=(jax.ShapeDtypeStruct((features_t.shap...]
    pallas_call x1, Pallas kernels: 1.23 us -> 2.48 us  [collect(): pl.pallas_call(collect_body, out_shape=outs_vmem((jax.ShapeDtypeStruct((u...]
  transfers between devices with their start and end apart: 5 -> 5, of which waited for: 2 -> 3; matrix products, arithmetic and copies ran while one was open for 2% -> 2% of each run, Pallas kernels for 15% -> 14%
where the time goes in v6:
time: 116 us
  blocking collectives  34.1 us (29%)
  Pallas kernels  31.6 us (27%)
  waiting for transfers between devices  24.6 us (21%)
  starting transfers between devices  22.1 us (19%)
  local copies, waits for them, and re-layouts  1.48 us (1%)
    all_to_all x2, blocking collectives, exchange_peers(): lax.all_to_all(x, 'dev', split_axis=0, concat_axis=0, axis_index_groups=g...  34.1 us
    all_to_all x2, waiting for transfers between devices, exchange(): return lax.all_to_all(x, 'dev', split_axis=0, concat_axis=0, tiled=True)  24.3 us
    all_to_all x2, starting transfers between devices, exchange(): return lax.all_to_all(x, 'dev', split_axis=0, concat_axis=0, tiled=True)  16.1 us
    pallas_call x1, Pallas kernels, tables(): pl.pallas_call(table_body, out_shape=outs_hbm(outs), in_specs=vmem(2), ou...  6.73 us
    ppermute x3, starting transfers between devices, swap(): return lax.ppermute(x, 'dev', [(d, d ^ 1) for d in range(devices)])  6.04 us
    pallas_call x1, Pallas kernels, route(): pl.pallas_call(route_body, out_shape=outs_hbm(outs), in_specs=hbm(6), out...  5.73 us
    pallas_call x1, Pallas kernels, owner(): pl.pallas_call(owner_body, out_shape=outs_hbm(outs) + (jax.ShapeDtypeStru...  5.05 us
    pallas_call x1, Pallas kernels, item_grads(): pl.pallas_call(item_body, grid=(local // step,), out_shape=jax.ShapeDtype...  3.94 us
  transfers between devices with their start and end apart: 5, of which 3 were waited for; matrix products, arithmetic and copies ran while one was open for 2% of the time, Pallas kernels for 14%

profile of v6, /device:TPU:1, one launch (start us, length us, event | category | flops | bytes accessed | tf_op | source)
XLA Modules:
  0.0 115.6 jit_solution(11058458882460220821)
XLA Ops:
  0.6 5.7 %route.1 = (bf16[128,40,128]{2,1,0:T(8,128)(2,1)}, f32[128,128]{1,0:T(8,128)}) custom-call(s32[4,512]{1,0:T(4,128)} %bitcast.4, s32[4,512]{1,0:T(4,128)} %bitcast.5, s32[16,128]{1,0:T(8,128)} %bitcast.6, bf16[512,1024]{1,0:T(8,128)(2,1)} %feat_hbm.1, bf16[1024,512]{1,0:T(8,128)(2,1)} %wh_ref.1, bf16[512,128]{1,0:T(8,128)(2,1)} %wo_hbm.3), custom_call_target="tpu_custom_call" | custom-call | tf_op jit(solution)/shard_map/route/pallas_call | solution.py:200
  6.4 11.5 %all-to-all-start = ((bf16[128,40,128]{2,1,0:T(8,128)(2,1)}), bf16[128,40,128]{2,1,0:T(8,128)(2,1)S(1)}, u32[]{:S(2)}, u32[]{:S(2)}) async-start(bf16[128,40,128]{2,1,0:T(8,128)(2,1)} %get-tuple-element.37), calls=%async_computation | async-start | bytes 2621440 | tf_op jit(solution)/shard_map/all_to_all | solution.py:693
  17.9 1.4 %copy.16 = bf16[512,1024]{0,1:T(8,128)(2,1)} copy(bf16[512,1024]{1,0:T(8,128)(2,1)S(1)} %copy-done.5) | data formatting | bytes 2097152 | tf_op args[0]
  19.3 1.1 collective-permute-start
  20.5 6.7 %tables.1 = (f32[16,128,128]{2,1,0:T(8,128)}, s32[16,32,128]{2,1,0:T(8,128)}) custom-call(s32[512,128]{1,0:T(8,128)S(1)} %reshape.18.ids_ref, s32[512,128]{1,0:T(8,128)S(1)} %reshape.19.counts_ref), custom_call_target="tpu_custom_call" | custom-call | flops 30000000 | bytes 1048576 | tf_op jit(solution)/shard_map/tables/pallas_call | solution.py:248
  27.2 12.8 %all-to-all-done.got_ref = bf16[128,40,128]{2,1,0:T(8,128)(2,1)S(1)} async-done(((bf16[128,40,128]{2,1,0:T(8,128)(2,1)}), bf16[128,40,128]{2,1,0:T(8,128)(2,1)S(1)}, u32[]{:S(2)}, u32[]{:S(2)}) %all-to-all-start) | async-done | bytes 1310752 | tf_op jit(solution)/shard_map/all_to_all | solution.py:693
  40.0 5.1 %owner.1 = (bf16[128,32,128]{2,1,0:T(8,128)(2,1)}, bf16[16,128,256]{2,1,0:T(8,128)(2,1)}, bf16[16,256,128]{2,1,0:T(8,128)(2,1)}, f32[16,1]{1,0:T(8,128)S(1)}) custom-call(bf16[128,40,128]{2,1,0:T(8,128)(2,1)S(1)} %all-to-all-done.got_ref, bf16[2048,128]{1,0:T(8,128)(2,1)} %items_hbm.1, f32[16,128,128]{2,1,0:T(8,128)} %get-tuple-element.41.mass_hbm, ...), custom_call_target="tpu_custom_call" | custom-call | tf_op jit(solution)/shard_map/owner/pallas_call | solution.py:398
  45.1 4.6 %all-to-all-start.1 = ((bf16[128,32,128]{2,1,0:T(8,128)(2,1)}), bf16[128,32,128]{2,1,0:T(8,128)(2,1)S(1)}, u32[]{:S(2)}, u32[]{:S(2)}) async-start(bf16[128,32,128]{2,1,0:T(8,128)(2,1)} %get-tuple-element.44), calls=%async_computation.1 | async-start | bytes 2097152 | tf_op jit(solution)/shard_map/all_to_all | solution.py:693
  49.7 3.9 %item_grads.1 = f32[2048,128]{1,0:T(8,128)} custom-call(bf16[16,128,256]{2,1,0:T(8,128)(2,1)} %get-tuple-element.50.weight_ref, bf16[16,256,128]{2,1,0:T(8,128)(2,1)} %get-tuple-element.51.q_ref), custom_call_target="tpu_custom_call" | custom-call | flops 135000000 | bytes 3145728 | tf_op jit(solution)/shard_map/item_grads/pallas_call | solution.py:428
  53.6 3.9 %ready.1 = (bf16[256,512]{1,0:T(8,128)(2,1)}, f32[512,256]{1,0:T(8,128)}, bf16[256,512]{1,0:T(8,128)(2,1)}, f32[512,256]{1,0:T(8,128)}) custom-call(bf16[1024,512]{1,0:T(8,128)(2,1)} %bitcast.3.feat_ref.feat_hbm, bf16[1024,512]{1,0:T(8,128)(2,1)} %copy-done, bf16[1024,512]{1,0:T(8,128)(2,1)} %wh_ref.1), custom_call_target="tpu_custom_call" | custom-call | flops 550000000 | bytes 5242880 | tf_op jit(solution)/shard_map/ready/pallas_call | solution.py:466
  57.6 11.5 %all-to-all-done.1.back_ref = bf16[128,32,128]{2,1,0:T(8,128)(2,1)S(1)} async-done(((bf16[128,32,128]{2,1,0:T(8,128)(2,1)}), bf16[128,32,128]{2,1,0:T(8,128)(2,1)S(1)}, u32[]{:S(2)}, u32[]{:S(2)}) %all-to-all-start.1) | async-done | bytes 1048608 | tf_op jit(solution)/shard_map/all_to_all | solution.py:693
  69.1 2.5 %collect.1 = (bf16[512,128]{1,0:T(8,128)(2,1)S(1)}, bf16[256,512]{1,0:T(8,128)(2,1)S(1)}, f32[512,256]{1,0:T(8,128)S(1)}, bf16[1024,512]{1,0:T(8,128)(2,1)S(1)}, bf16[256,128]{1,0:T(8,128)(2,1)S(1)}) custom-call(bf16[128,32,128]{2,1,0:T(8,128)(2,1)S(1)} %all-to-all-done.1.back_ref, f32[128,128]{1,0:T(8,128)S(1)} %copy-done.4, ...), custom_call_target="tpu_custom_call" | custom-call | tf_op jit(solution)/shard_map/collect/pallas_call | solution.py:540
  71.6 1.4 %collective-permute-start.1 = (bf16[512,128]{1,0:T(8,128)(2,1)S(1)}, bf16[512,128]{1,0:T(8,128)(2,1)S(1)}, u32[]{:S(2)}, u32[]{:S(2)}) collective-permute-start(bf16[512,128]{1,0:T(8,128)(2,1)S(1)} %get-tuple-element.56.dq_ref), channel_id=1, source_target_pairs={{0,1},{1,0},{2,3},{3,2},{4,5},{5,4},{6,7},{7,6},{8,9},{9,8},{10,11... | collective-permute-start | bytes 393224 | tf_op jit(solution)/shard_map/ppermute | solution.py:706
  73.0 0.8 tower_own.1
  73.8 0.2 collective-permute-done.1.dq_ref
  74.0 0.8 tower_other.1
  74.8 17.6 %all_to_all.20.parts_ref = bf16[64,40,128]{2,1,0:T(8,128)(2,1)S(1)} all-to-all(bf16[64,40,128]{2,1,0:T(8,128)(2,1)S(1)} %tower_other.1), channel_id=1, replica_groups={{0,2,4,6,8,10,12,14,16,18,20,22,24,26,28,30,32,34,36,38,40,42,44,46,48,..., dimensions={0} | all-to-all | bytes 1310720 | tf_op jit(solution)/shard_map/all_to_all | solution.py:699
  92.4 0.1 sum_parts.1
  92.6 16.5 %all_to_all.21.got_ref = bf16[64,40,128]{2,1,0:T(8,128)(2,1)S(1)} all-to-all(bf16[64,40,128]{2,1,0:T(8,128)(2,1)S(1)} %sum_parts.1), channel_id=1, replica_groups={{0,2,4,6,8,10,12,14,16,18,20,22,24,26,28,30,32,34,36,38,40,42,44,46,48,..., dimensions={0} | all-to-all | bytes 1310720 | tf_op jit(solution)/shard_map/all_to_all | solution.py:699
  109.1 3.5 %collective-permute-start.2 = (bf16[64,40,128]{2,1,0:T(8,128)(2,1)S(1)}, bf16[64,40,128]{2,1,0:T(8,128)(2,1)S(1)}, u32[]{:S(2)}, u32[]{:S(2)}) collective-permute-start(bf16[64,40,128]{2,1,0:T(8,128)(2,1)S(1)} %all_to_all.21.got_ref), channel_id=1, source_target_pairs={{0,1},{1,0},{2,3},{3,2},{4,5},{5,4},{6,7},{7,6},{8,9},{9,8},{10,11... | collective-permute-start | bytes 1966088 | tf_op jit(solution)/shard_map/ppermute | solution.py:706
  112.6 0.6 reduce
  113.2 1.1 spread.2
  114.3 0.0 collective-permute-done.2.got_ref
  114.3 1.1 spread.3
  (19 shorter events, 0.1 us)
Async XLA Ops:
  0.6 17.3 %copy-start.5 = (bf16[512,1024]{1,0:T(8,128)(2,1)S(1)}, bf16[512,1024]{1,0:T(8,128)(2,1)}, u32[]{:S(2)}) copy-start(bf16[512,1024]{1,0:T(8,128)(2,1)} %feat_hbm.1) | copy-start | bytes 3145732
  6.4 14.0 %copy-start.6 = (s32[16,4096]{1,0:T(8,128)S(1)}, s32[16,4096]{1,0:T(8,128)}, u32[]{:S(2)}) copy-start(s32[16,4096]{1,0:T(8,128)} %param.15) | copy-start | bytes 786436
  6.4 14.0 %copy-start.7 = (s32[16,4096]{1,0:T(8,128)S(1)}, s32[16,4096]{1,0:T(8,128)}, u32[]{:S(2)}) copy-start(s32[16,4096]{1,0:T(8,128)} %param.16) | copy-start | bytes 786436
  6.4 33.6 %all-to-all-start = ((bf16[128,40,128]{2,1,0:T(8,128)(2,1)}), bf16[128,40,128]{2,1,0:T(8,128)(2,1)S(1)}, u32[]{:S(2)}, u32[]{:S(2)}) async-start(bf16[128,40,128]{2,1,0:T(8,128)(2,1)} %get-tuple-element.37), calls=%async_computation | async-start | bytes 2621440 | tf_op jit(solution)/shard_map/all_to_all | solution.py:693
  19.3 7.9 %collective-permute-start = (bf16[1024,512]{1,0:T(8,128)(2,1)}, bf16[1024,512]{1,0:T(8,128)(2,1)S(1)}, u32[]{:S(2)}, u32[]{:S(2)}) collective-permute-start(bf16[1024,512]{1,0:T(8,128)(2,1)} %bitcast.3.feat_ref.feat_hbm), channel_id=1, source_target_pairs={{0,1},{1,0},{2,3},{3,2},{4,5},{5,4},{6,7},{7,6},{8,9},{9,8},{10,11... | collective-permute-start | bytes 3145736 | tf_op jit(solution)/shard_map/ppermute | solution.py:706
  27.2 17.9 %copy-start = (bf16[1024,512]{1,0:T(8,128)(2,1)}, bf16[1024,512]{1,0:T(8,128)(2,1)S(1)}, u32[]{:S(2)}) copy-start(bf16[1024,512]{1,0:T(8,128)(2,1)S(1)} %collective-permute-done.feat_other_ref.feat_ref) | copy-start | bytes 3145732
  45.1 24.0 %all-to-all-start.1 = ((bf16[128,32,128]{2,1,0:T(8,128)(2,1)}), bf16[128,32,128]{2,1,0:T(8,128)(2,1)S(1)}, u32[]{:S(2)}, u32[]{:S(2)}) async-start(bf16[128,32,128]{2,1,0:T(8,128)(2,1)} %get-tuple-element.44), calls=%async_computation.1 | async-start | bytes 2097152 | tf_op jit(solution)/shard_map/all_to_all | solution.py:693
  53.6 15.5 %copy-start.4 = (f32[128,128]{1,0:T(8,128)S(1)}, f32[128,128]{1,0:T(8,128)}, u32[]{:S(2)}) copy-start(f32[128,128]{1,0:T(8,128)} %get-tuple-element.53.named_ref) | copy-start | bytes 196612
  69.1 4.9 %copy-start.1 = (bf16[1024,512]{1,0:T(8,128)(2,1)S(1)}, bf16[1024,512]{1,0:T(8,128)(2,1)}, u32[]{:S(2)}) copy-start(bf16[1024,512]{1,0:T(8,128)(2,1)} %copy-done) | copy-start | bytes 3145732
  69.1 4.9 %copy-start.2 = (f32[512,256]{1,0:T(8,128)S(1)}, f32[512,256]{1,0:T(8,128)}, u32[]{:S(2)}) copy-start(f32[512,256]{1,0:T(8,128)} %get-tuple-element.64.slope_ref) | copy-start | bytes 1572868
  69.1 4.9 %copy-start.3 = (bf16[256,512]{1,0:T(8,128)(2,1)S(1)}, bf16[256,512]{1,0:T(8,128)(2,1)}, u32[]{:S(2)}) copy-start(bf16[256,512]{1,0:T(8,128)(2,1)} %get-tuple-element.63.hidden_ref) | copy-start | bytes 786436
  71.6 2.4 %collective-permute-start.1 = (bf16[512,128]{1,0:T(8,128)(2,1)S(1)}, bf16[512,128]{1,0:T(8,128)(2,1)S(1)}, u32[]{:S(2)}, u32[]{:S(2)}) collective-permute-start(bf16[512,128]{1,0:T(8,128)(2,1)S(1)} %get-tuple-element.56.dq_ref), channel_id=1, source_target_pairs={{0,1},{1,0},{2,3},{3,2},{4,5},{5,4},{6,7},{7,6},{8,9},{9,8},{10,11... | collective-permute-start | bytes 393224 | tf_op jit(solution)/shard_map/ppermute | solution.py:706
  109.1 5.3 %collective-permute-start.2 = (bf16[64,40,128]{2,1,0:T(8,128)(2,1)S(1)}, bf16[64,40,128]{2,1,0:T(8,128)(2,1)S(1)}, u32[]{:S(2)}, u32[]{:S(2)}) collective-permute-start(bf16[64,40,128]{2,1,0:T(8,128)(2,1)S(1)} %all_to_all.21.got_ref), channel_id=1, source_target_pairs={{0,1},{1,0},{2,3},{3,2},{4,5},{5,4},{6,7},{7,6},{8,9},{9,8},{10,11... | collective-permute-start | bytes 1966088 | tf_op jit(solution)/shard_map/ppermute | solution.py:706

commit v7 on v6

--- a/solution.py
+++ b/solution.py
@@ -11,7 +11,7 @@
 BF16 = jnp.bfloat16
 NONE = -3.0e38
 KEY = 4096
-AHEAD = 3
+AHEAD = 4
 LANES = 128
 
 

time: 116 us -> 116 us (level)
  no operation moved by 1% of the time
where the time goes in v7:
time: 116 us
  blocking collectives  34.1 us (29%)
  Pallas kernels  31.6 us (27%)
  waiting for transfers between devices  24.6 us (21%)
  starting transfers between devices  22.2 us (19%)
  local copies, waits for them, and re-layouts  1.48 us (1%)
    all_to_all x2, blocking collectives, exchange_peers(): lax.all_to_all(x, 'dev', split_axis=0, concat_axis=0, axis_index_groups=g...  34.1 us
    all_to_all x2, waiting for transfers between devices, exchange(): return lax.all_to_all(x, 'dev', split_axis=0, concat_axis=0, tiled=True)  24.3 us
    all_to_all x2, starting transfers between devices, exchange(): return lax.all_to_all(x, 'dev', split_axis=0, concat_axis=0, tiled=True)  16.1 us
    pallas_call x1, Pallas kernels, tables(): pl.pallas_call(table_body, out_shape=outs_hbm(outs), in_specs=vmem(2), ou...  6.73 us
    ppermute x3, starting transfers between devices, swap(): return lax.ppermute(x, 'dev', [(d, d ^ 1) for d in range(devices)])  6.04 us
    pallas_call x1, Pallas kernels, route(): pl.pallas_call(route_body, out_shape=outs_hbm(outs), in_specs=hbm(6), out...  5.73 us
    pallas_call x1, Pallas kernels, owner(): pl.pallas_call(owner_body, out_shape=outs_hbm(outs) + (jax.ShapeDtypeStru...  5.01 us
    pallas_call x1, Pallas kernels, item_grads(): pl.pallas_call(item_body, grid=(local // step,), out_shape=jax.ShapeDtype...  3.95 us
  transfers between devices with their start and end apart: 5, of which 3 were waited for; matrix products, arithmetic and copies ran while one was open for 2% of the time, Pallas kernels for 14%

profile of v7, /device:TPU:1, one launch (start us, length us, event | category | flops | bytes accessed | tf_op | source)
XLA Modules:
  0.0 115.5 jit_solution(15046386366792975124)
XLA Ops:
  0.6 5.7 %route.1 = (bf16[128,40,128]{2,1,0:T(8,128)(2,1)}, f32[128,128]{1,0:T(8,128)}) custom-call(s32[4,512]{1,0:T(4,128)} %bitcast.4, s32[4,512]{1,0:T(4,128)} %bitcast.5, s32[16,128]{1,0:T(8,128)} %bitcast.6, bf16[512,1024]{1,0:T(8,128)(2,1)} %feat_hbm.1, bf16[1024,512]{1,0:T(8,128)(2,1)} %wh_ref.1, bf16[512,128]{1,0:T(8,128)(2,1)} %wo_hbm.3), custom_call_target="tpu_custom_call" | custom-call | tf_op jit(solution)/shard_map/route/pallas_call | solution.py:200
  6.4 11.5 %all-to-all-start = ((bf16[128,40,128]{2,1,0:T(8,128)(2,1)}), bf16[128,40,128]{2,1,0:T(8,128)(2,1)S(1)}, u32[]{:S(2)}, u32[]{:S(2)}) async-start(bf16[128,40,128]{2,1,0:T(8,128)(2,1)} %get-tuple-element.37), calls=%async_computation | async-start | bytes 2621440 | tf_op jit(solution)/shard_map/all_to_all | solution.py:693
  17.9 1.4 %copy.16 = bf16[512,1024]{0,1:T(8,128)(2,1)} copy(bf16[512,1024]{1,0:T(8,128)(2,1)S(1)} %copy-done.5) | data formatting | bytes 2097152 | tf_op args[0]
  19.3 1.1 collective-permute-start
  20.5 6.7 %tables.1 = (f32[16,128,128]{2,1,0:T(8,128)}, s32[16,32,128]{2,1,0:T(8,128)}) custom-call(s32[512,128]{1,0:T(8,128)S(1)} %reshape.18.ids_ref, s32[512,128]{1,0:T(8,128)S(1)} %reshape.19.counts_ref), custom_call_target="tpu_custom_call" | custom-call | flops 30000000 | bytes 1048576 | tf_op jit(solution)/shard_map/tables/pallas_call | solution.py:248
  27.2 12.8 %all-to-all-done.got_ref = bf16[128,40,128]{2,1,0:T(8,128)(2,1)S(1)} async-done(((bf16[128,40,128]{2,1,0:T(8,128)(2,1)}), bf16[128,40,128]{2,1,0:T(8,128)(2,1)S(1)}, u32[]{:S(2)}, u32[]{:S(2)}) %all-to-all-start) | async-done | bytes 1310752 | tf_op jit(solution)/shard_map/all_to_all | solution.py:693
  40.0 5.0 %owner.1 = (bf16[128,32,128]{2,1,0:T(8,128)(2,1)}, bf16[16,128,256]{2,1,0:T(8,128)(2,1)}, bf16[16,256,128]{2,1,0:T(8,128)(2,1)}, f32[16,1]{1,0:T(8,128)S(1)}) custom-call(bf16[128,40,128]{2,1,0:T(8,128)(2,1)S(1)} %all-to-all-done.got_ref, bf16[2048,128]{1,0:T(8,128)(2,1)} %items_hbm.1, f32[16,128,128]{2,1,0:T(8,128)} %get-tuple-element.41.mass_hbm, ...), custom_call_target="tpu_custom_call" | custom-call | tf_op jit(solution)/shard_map/owner/pallas_call | solution.py:398
  45.0 4.6 %all-to-all-start.1 = ((bf16[128,32,128]{2,1,0:T(8,128)(2,1)}), bf16[128,32,128]{2,1,0:T(8,128)(2,1)S(1)}, u32[]{:S(2)}, u32[]{:S(2)}) async-start(bf16[128,32,128]{2,1,0:T(8,128)(2,1)} %get-tuple-element.44), calls=%async_computation.1 | async-start | bytes 2097152 | tf_op jit(solution)/shard_map/all_to_all | solution.py:693
  49.7 3.9 %item_grads.1 = f32[2048,128]{1,0:T(8,128)} custom-call(bf16[16,128,256]{2,1,0:T(8,128)(2,1)} %get-tuple-element.50.weight_ref, bf16[16,256,128]{2,1,0:T(8,128)(2,1)} %get-tuple-element.51.q_ref), custom_call_target="tpu_custom_call" | custom-call | flops 135000000 | bytes 3145728 | tf_op jit(solution)/shard_map/item_grads/pallas_call | solution.py:428
  53.6 3.9 %ready.1 = (bf16[256,512]{1,0:T(8,128)(2,1)}, f32[512,256]{1,0:T(8,128)}, bf16[256,512]{1,0:T(8,128)(2,1)}, f32[512,256]{1,0:T(8,128)}) custom-call(bf16[1024,512]{1,0:T(8,128)(2,1)} %bitcast.3.feat_ref.feat_hbm, bf16[1024,512]{1,0:T(8,128)(2,1)} %copy-done, bf16[1024,512]{1,0:T(8,128)(2,1)} %wh_ref.1), custom_call_target="tpu_custom_call" | custom-call | flops 550000000 | bytes 5242880 | tf_op jit(solution)/shard_map/ready/pallas_call | solution.py:466
  57.5 11.5 %all-to-all-done.1.back_ref = bf16[128,32,128]{2,1,0:T(8,128)(2,1)S(1)} async-done(((bf16[128,32,128]{2,1,0:T(8,128)(2,1)}), bf16[128,32,128]{2,1,0:T(8,128)(2,1)S(1)}, u32[]{:S(2)}, u32[]{:S(2)}) %all-to-all-start.1) | async-done | bytes 1048608 | tf_op jit(solution)/shard_map/all_to_all | solution.py:693
  69.1 2.5 %collect.1 = (bf16[512,128]{1,0:T(8,128)(2,1)S(1)}, bf16[256,512]{1,0:T(8,128)(2,1)S(1)}, f32[512,256]{1,0:T(8,128)S(1)}, bf16[1024,512]{1,0:T(8,128)(2,1)S(1)}, bf16[256,128]{1,0:T(8,128)(2,1)S(1)}) custom-call(bf16[128,32,128]{2,1,0:T(8,128)(2,1)S(1)} %all-to-all-done.1.back_ref, f32[128,128]{1,0:T(8,128)S(1)} %copy-done.4, ...), custom_call_target="tpu_custom_call" | custom-call | tf_op jit(solution)/shard_map/collect/pallas_call | solution.py:540
  71.6 1.4 %collective-permute-start.1 = (bf16[512,128]{1,0:T(8,128)(2,1)S(1)}, bf16[512,128]{1,0:T(8,128)(2,1)S(1)}, u32[]{:S(2)}, u32[]{:S(2)}) collective-permute-start(bf16[512,128]{1,0:T(8,128)(2,1)S(1)} %get-tuple-element.56.dq_ref), channel_id=1, source_target_pairs={{0,1},{1,0},{2,3},{3,2},{4,5},{5,4},{6,7},{7,6},{8,9},{9,8},{10,11... | collective-permute-start | bytes 393224 | tf_op jit(solution)/shard_map/ppermute | solution.py:706
  73.0 0.8 tower_own.1
  73.8 0.2 collective-permute-done.1.dq_ref
  74.0 0.8 tower_other.1
  74.8 17.6 %all_to_all.20.parts_ref = bf16[64,40,128]{2,1,0:T(8,128)(2,1)S(1)} all-to-all(bf16[64,40,128]{2,1,0:T(8,128)(2,1)S(1)} %tower_other.1), channel_id=1, replica_groups={{0,2,4,6,8,10,12,14,16,18,20,22,24,26,28,30,32,34,36,38,40,42,44,46,48,..., dimensions={0} | all-to-all | bytes 1310720 | tf_op jit(solution)/shard_map/all_to_all | solution.py:699
  92.4 0.1 sum_parts.1
  92.5 16.5 %all_to_all.21.got_ref = bf16[64,40,128]{2,1,0:T(8,128)(2,1)S(1)} all-to-all(bf16[64,40,128]{2,1,0:T(8,128)(2,1)S(1)} %sum_parts.1), channel_id=1, replica_groups={{0,2,4,6,8,10,12,14,16,18,20,22,24,26,28,30,32,34,36,38,40,42,44,46,48,..., dimensions={0} | all-to-all | bytes 1310720 | tf_op jit(solution)/shard_map/all_to_all | solution.py:699
  109.0 3.5 %collective-permute-start.2 = (bf16[64,40,128]{2,1,0:T(8,128)(2,1)S(1)}, bf16[64,40,128]{2,1,0:T(8,128)(2,1)S(1)}, u32[]{:S(2)}, u32[]{:S(2)}) collective-permute-start(bf16[64,40,128]{2,1,0:T(8,128)(2,1)S(1)} %all_to_all.21.got_ref), channel_id=1, source_target_pairs={{0,1},{1,0},{2,3},{3,2},{4,5},{5,4},{6,7},{7,6},{8,9},{9,8},{10,11... | collective-permute-start | bytes 1966088 | tf_op jit(solution)/shard_map/ppermute | solution.py:706
  112.6 0.6 reduce
  113.2 1.1 spread.2
  114.3 0.0 collective-permute-done.2.got_ref
  114.3 1.1 spread.3
  (19 shorter events, 0.1 us)
Async XLA Ops:
  0.6 17.3 %copy-start.5 = (bf16[512,1024]{1,0:T(8,128)(2,1)S(1)}, bf16[512,1024]{1,0:T(8,128)(2,1)}, u32[]{:S(2)}) copy-start(bf16[512,1024]{1,0:T(8,128)(2,1)} %feat_hbm.1) | copy-start | bytes 3145732
  6.4 14.0 %copy-start.6 = (s32[16,4096]{1,0:T(8,128)S(1)}, s32[16,4096]{1,0:T(8,128)}, u32[]{:S(2)}) copy-start(s32[16,4096]{1,0:T(8,128)} %param.15) | copy-start | bytes 786436
  6.4 14.0 %copy-start.7 = (s32[16,4096]{1,0:T(8,128)S(1)}, s32[16,4096]{1,0:T(8,128)}, u32[]{:S(2)}) copy-start(s32[16,4096]{1,0:T(8,128)} %param.16) | copy-start | bytes 786436
  6.4 33.6 %all-to-all-start = ((bf16[128,40,128]{2,1,0:T(8,128)(2,1)}), bf16[128,40,128]{2,1,0:T(8,128)(2,1)S(1)}, u32[]{:S(2)}, u32[]{:S(2)}) async-start(bf16[128,40,128]{2,1,0:T(8,128)(2,1)} %get-tuple-element.37), calls=%async_computation | async-start | bytes 2621440 | tf_op jit(solution)/shard_map/all_to_all | solution.py:693
  19.3 7.9 %collective-permute-start = (bf16[1024,512]{1,0:T(8,128)(2,1)}, bf16[1024,512]{1,0:T(8,128)(2,1)S(1)}, u32[]{:S(2)}, u32[]{:S(2)}) collective-permute-start(bf16[1024,512]{1,0:T(8,128)(2,1)} %bitcast.3.feat_ref.feat_hbm), channel_id=1, source_target_pairs={{0,1},{1,0},{2,3},{3,2},{4,5},{5,4},{6,7},{7,6},{8,9},{9,8},{10,11... | collective-permute-start | bytes 3145736 | tf_op jit(solution)/shard_map/ppermute | solution.py:706
  27.2 17.8 %copy-start = (bf16[1024,512]{1,0:T(8,128)(2,1)}, bf16[1024,512]{1,0:T(8,128)(2,1)S(1)}, u32[]{:S(2)}) copy-start(bf16[1024,512]{1,0:T(8,128)(2,1)S(1)} %collective-permute-done.feat_other_ref.feat_ref) | copy-start | bytes 3145732
  45.0 24.0 %all-to-all-start.1 = ((bf16[128,32,128]{2,1,0:T(8,128)(2,1)}), bf16[128,32,128]{2,1,0:T(8,128)(2,1)S(1)}, u32[]{:S(2)}, u32[]{:S(2)}) async-start(bf16[128,32,128]{2,1,0:T(8,128)(2,1)} %get-tuple-element.44), calls=%async_computation.1 | async-start | bytes 2097152 | tf_op jit(solution)/shard_map/all_to_all | solution.py:693
  53.6 15.5 %copy-start.4 = (f32[128,128]{1,0:T(8,128)S(1)}, f32[128,128]{1,0:T(8,128)}, u32[]{:S(2)}) copy-start(f32[128,128]{1,0:T(8,128)} %get-tuple-element.53.named_ref) | copy-start | bytes 196612
  69.1 4.9 %copy-start.1 = (bf16[1024,512]{1,0:T(8,128)(2,1)S(1)}, bf16[1024,512]{1,0:T(8,128)(2,1)}, u32[]{:S(2)}) copy-start(bf16[1024,512]{1,0:T(8,128)(2,1)} %copy-done) | copy-start | bytes 3145732
  69.1 4.9 %copy-start.2 = (f32[512,256]{1,0:T(8,128)S(1)}, f32[512,256]{1,0:T(8,128)}, u32[]{:S(2)}) copy-start(f32[512,256]{1,0:T(8,128)} %get-tuple-element.64.slope_ref) | copy-start | bytes 1572868
  69.1 4.9 %copy-start.3 = (bf16[256,512]{1,0:T(8,128)(2,1)S(1)}, bf16[256,512]{1,0:T(8,128)(2,1)}, u32[]{:S(2)}) copy-start(bf16[256,512]{1,0:T(8,128)(2,1)} %get-tuple-element.63.hidden_ref) | copy-start | bytes 786436
  71.6 2.4 %collective-permute-start.1 = (bf16[512,128]{1,0:T(8,128)(2,1)S(1)}, bf16[512,128]{1,0:T(8,128)(2,1)S(1)}, u32[]{:S(2)}, u32[]{:S(2)}) collective-permute-start(bf16[512,128]{1,0:T(8,128)(2,1)S(1)} %get-tuple-element.56.dq_ref), channel_id=1, source_target_pairs={{0,1},{1,0},{2,3},{3,2},{4,5},{5,4},{6,7},{7,6},{8,9},{9,8},{10,11... | collective-permute-start | bytes 393224 | tf_op jit(solution)/shard_map/ppermute | solution.py:706
  109.0 5.3 %collective-permute-start.2 = (bf16[64,40,128]{2,1,0:T(8,128)(2,1)S(1)}, bf16[64,40,128]{2,1,0:T(8,128)(2,1)S(1)}, u32[]{:S(2)}, u32[]{:S(2)}) collective-permute-start(bf16[64,40,128]{2,1,0:T(8,128)(2,1)S(1)} %all_to_all.21.got_ref), channel_id=1, source_target_pairs={{0,1},{1,0},{2,3},{3,2},{4,5},{5,4},{6,7},{7,6},{8,9},{9,8},{10,11... | collective-permute-start | bytes 1966088 | tf_op jit(solution)/shard_map/ppermute | solution.py:706

commit v8 on v7

--- a/solution.py
+++ b/solution.py
@@ -11,7 +11,7 @@
 BF16 = jnp.bfloat16
 NONE = -3.0e38
 KEY = 4096
-AHEAD = 4
+AHEAD = 6
 LANES = 128
 
 

time: 116 us -> 116 us (level)
  no operation moved by 1% of the time
where the time goes in v8:
time: 116 us
  blocking collectives  34.1 us (29%)
  Pallas kernels  31.6 us (27%)
  waiting for transfers between devices  24.6 us (21%)
  starting transfers between devices  22.2 us (19%)
  local copies, waits for them, and re-layouts  1.48 us (1%)
    all_to_all x2, blocking collectives, exchange_peers(): lax.all_to_all(x, 'dev', split_axis=0, concat_axis=0, axis_index_groups=g...  34.1 us
    all_to_all x2, waiting for transfers between devices, exchange(): return lax.all_to_all(x, 'dev', split_axis=0, concat_axis=0, tiled=True)  24.3 us
    all_to_all x2, starting transfers between devices, exchange(): return lax.all_to_all(x, 'dev', split_axis=0, concat_axis=0, tiled=True)  16.1 us
    pallas_call x1, Pallas kernels, tables(): pl.pallas_call(table_body, out_shape=outs_hbm(outs), in_specs=vmem(2), ou...  6.73 us
    ppermute x3, starting transfers between devices, swap(): return lax.ppermute(x, 'dev', [(d, d ^ 1) for d in range(devices)])  6.05 us
    pallas_call x1, Pallas kernels, route(): pl.pallas_call(route_body, out_shape=outs_hbm(outs), in_specs=hbm(6), out...  5.73 us
    pallas_call x1, Pallas kernels, owner(): pl.pallas_call(owner_body, out_shape=outs_hbm(outs) + (jax.ShapeDtypeStru...  5.02 us
    pallas_call x1, Pallas kernels, item_grads(): pl.pallas_call(item_body, grid=(local // step,), out_shape=jax.ShapeDtype...  3.94 us
  transfers between devices with their start and end apart: 5, of which 3 were waited for; matrix products, arithmetic and copies ran while one was open for 2% of the time, Pallas kernels for 14%

profile of v8, /device:TPU:1, one launch (start us, length us, event | category | flops | bytes accessed | tf_op | source)
XLA Modules:
  0.0 115.5 jit_solution(14040567092557720325)
XLA Ops:
  0.6 5.7 %route.1 = (bf16[128,40,128]{2,1,0:T(8,128)(2,1)}, f32[128,128]{1,0:T(8,128)}) custom-call(s32[4,512]{1,0:T(4,128)} %bitcast.4, s32[4,512]{1,0:T(4,128)} %bitcast.5, s32[16,128]{1,0:T(8,128)} %bitcast.6, bf16[512,1024]{1,0:T(8,128)(2,1)} %feat_hbm.1, bf16[1024,512]{1,0:T(8,128)(2,1)} %wh_ref.1, bf16[512,128]{1,0:T(8,128)(2,1)} %wo_hbm.3), custom_call_target="tpu_custom_call" | custom-call | tf_op jit(solution)/shard_map/route/pallas_call | solution.py:200
  6.4 11.5 %all-to-all-start = ((bf16[128,40,128]{2,1,0:T(8,128)(2,1)}), bf16[128,40,128]{2,1,0:T(8,128)(2,1)S(1)}, u32[]{:S(2)}, u32[]{:S(2)}) async-start(bf16[128,40,128]{2,1,0:T(8,128)(2,1)} %get-tuple-element.37), calls=%async_computation | async-start | bytes 2621440 | tf_op jit(solution)/shard_map/all_to_all | solution.py:693
  17.9 1.4 %copy.16 = bf16[512,1024]{0,1:T(8,128)(2,1)} copy(bf16[512,1024]{1,0:T(8,128)(2,1)S(1)} %copy-done.5) | data formatting | bytes 2097152 | tf_op args[0]
  19.3 1.1 collective-permute-start
  20.5 6.7 %tables.1 = (f32[16,128,128]{2,1,0:T(8,128)}, s32[16,32,128]{2,1,0:T(8,128)}) custom-call(s32[512,128]{1,0:T(8,128)S(1)} %reshape.18.ids_ref, s32[512,128]{1,0:T(8,128)S(1)} %reshape.19.counts_ref), custom_call_target="tpu_custom_call" | custom-call | flops 30000000 | bytes 1048576 | tf_op jit(solution)/shard_map/tables/pallas_call | solution.py:248
  27.2 12.8 %all-to-all-done.got_ref = bf16[128,40,128]{2,1,0:T(8,128)(2,1)S(1)} async-done(((bf16[128,40,128]{2,1,0:T(8,128)(2,1)}), bf16[128,40,128]{2,1,0:T(8,128)(2,1)S(1)}, u32[]{:S(2)}, u32[]{:S(2)}) %all-to-all-start) | async-done | bytes 1310752 | tf_op jit(solution)/shard_map/all_to_all | solution.py:693
  40.0 5.0 %owner.1 = (bf16[128,32,128]{2,1,0:T(8,128)(2,1)}, bf16[16,128,256]{2,1,0:T(8,128)(2,1)}, bf16[16,256,128]{2,1,0:T(8,128)(2,1)}, f32[16,1]{1,0:T(8,128)S(1)}) custom-call(bf16[128,40,128]{2,1,0:T(8,128)(2,1)S(1)} %all-to-all-done.got_ref, bf16[2048,128]{1,0:T(8,128)(2,1)} %items_hbm.1, f32[16,128,128]{2,1,0:T(8,128)} %get-tuple-element.41.mass_hbm, ...), custom_call_target="tpu_custom_call" | custom-call | tf_op jit(solution)/shard_map/owner/pallas_call | solution.py:398
  45.0 4.6 %all-to-all-start.1 = ((bf16[128,32,128]{2,1,0:T(8,128)(2,1)}), bf16[128,32,128]{2,1,0:T(8,128)(2,1)S(1)}, u32[]{:S(2)}, u32[]{:S(2)}) async-start(bf16[128,32,128]{2,1,0:T(8,128)(2,1)} %get-tuple-element.44), calls=%async_computation.1 | async-start | bytes 2097152 | tf_op jit(solution)/shard_map/all_to_all | solution.py:693
  49.7 3.9 %item_grads.1 = f32[2048,128]{1,0:T(8,128)} custom-call(bf16[16,128,256]{2,1,0:T(8,128)(2,1)} %get-tuple-element.50.weight_ref, bf16[16,256,128]{2,1,0:T(8,128)(2,1)} %get-tuple-element.51.q_ref), custom_call_target="tpu_custom_call" | custom-call | flops 135000000 | bytes 3145728 | tf_op jit(solution)/shard_map/item_grads/pallas_call | solution.py:428
  53.6 3.9 %ready.1 = (bf16[256,512]{1,0:T(8,128)(2,1)}, f32[512,256]{1,0:T(8,128)}, bf16[256,512]{1,0:T(8,128)(2,1)}, f32[512,256]{1,0:T(8,128)}) custom-call(bf16[1024,512]{1,0:T(8,128)(2,1)} %bitcast.3.feat_ref.feat_hbm, bf16[1024,512]{1,0:T(8,128)(2,1)} %copy-done, bf16[1024,512]{1,0:T(8,128)(2,1)} %wh_ref.1), custom_call_target="tpu_custom_call" | custom-call | flops 550000000 | bytes 5242880 | tf_op jit(solution)/shard_map/ready/pallas_call | solution.py:466
  57.5 11.5 %all-to-all-done.1.back_ref = bf16[128,32,128]{2,1,0:T(8,128)(2,1)S(1)} async-done(((bf16[128,32,128]{2,1,0:T(8,128)(2,1)}), bf16[128,32,128]{2,1,0:T(8,128)(2,1)S(1)}, u32[]{:S(2)}, u32[]{:S(2)}) %all-to-all-start.1) | async-done | bytes 1048608 | tf_op jit(solution)/shard_map/all_to_all | solution.py:693
  69.1 2.5 %collect.1 = (bf16[512,128]{1,0:T(8,128)(2,1)S(1)}, bf16[256,512]{1,0:T(8,128)(2,1)S(1)}, f32[512,256]{1,0:T(8,128)S(1)}, bf16[1024,512]{1,0:T(8,128)(2,1)S(1)}, bf16[256,128]{1,0:T(8,128)(2,1)S(1)}) custom-call(bf16[128,32,128]{2,1,0:T(8,128)(2,1)S(1)} %all-to-all-done.1.back_ref, f32[128,128]{1,0:T(8,128)S(1)} %copy-done.4, ...), custom_call_target="tpu_custom_call" | custom-call | tf_op jit(solution)/shard_map/collect/pallas_call | solution.py:540
  71.6 1.4 %collective-permute-start.1 = (bf16[512,128]{1,0:T(8,128)(2,1)S(1)}, bf16[512,128]{1,0:T(8,128)(2,1)S(1)}, u32[]{:S(2)}, u32[]{:S(2)}) collective-permute-start(bf16[512,128]{1,0:T(8,128)(2,1)S(1)} %get-tuple-element.56.dq_ref), channel_id=1, source_target_pairs={{0,1},{1,0},{2,3},{3,2},{4,5},{5,4},{6,7},{7,6},{8,9},{9,8},{10,11... | collective-permute-start | bytes 393224 | tf_op jit(solution)/shard_map/ppermute | solution.py:706
  73.0 0.8 tower_own.1
  73.8 0.2 collective-permute-done.1.dq_ref
  74.0 0.8 tower_other.1
  74.8 17.6 %all_to_all.20.parts_ref = bf16[64,40,128]{2,1,0:T(8,128)(2,1)S(1)} all-to-all(bf16[64,40,128]{2,1,0:T(8,128)(2,1)S(1)} %tower_other.1), channel_id=1, replica_groups={{0,2,4,6,8,10,12,14,16,18,20,22,24,26,28,30,32,34,36,38,40,42,44,46,48,..., dimensions={0} | all-to-all | bytes 1310720 | tf_op jit(solution)/shard_map/all_to_all | solution.py:699
  92.4 0.1 sum_parts.1
  92.5 16.5 %all_to_all.21.got_ref = bf16[64,40,128]{2,1,0:T(8,128)(2,1)S(1)} all-to-all(bf16[64,40,128]{2,1,0:T(8,128)(2,1)S(1)} %sum_parts.1), channel_id=1, replica_groups={{0,2,4,6,8,10,12,14,16,18,20,22,24,26,28,30,32,34,36,38,40,42,44,46,48,..., dimensions={0} | all-to-all | bytes 1310720 | tf_op jit(solution)/shard_map/all_to_all | solution.py:699
  109.0 3.5 %collective-permute-start.2 = (bf16[64,40,128]{2,1,0:T(8,128)(2,1)S(1)}, bf16[64,40,128]{2,1,0:T(8,128)(2,1)S(1)}, u32[]{:S(2)}, u32[]{:S(2)}) collective-permute-start(bf16[64,40,128]{2,1,0:T(8,128)(2,1)S(1)} %all_to_all.21.got_ref), channel_id=1, source_target_pairs={{0,1},{1,0},{2,3},{3,2},{4,5},{5,4},{6,7},{7,6},{8,9},{9,8},{10,11... | collective-permute-start | bytes 1966088 | tf_op jit(solution)/shard_map/ppermute | solution.py:706
  112.6 0.6 reduce
  113.2 1.1 spread.2
  114.3 0.0 collective-permute-done.2.got_ref
  114.3 1.1 spread.3
  (19 shorter events, 0.1 us)
Async XLA Ops:
  0.6 17.3 %copy-start.5 = (bf16[512,1024]{1,0:T(8,128)(2,1)S(1)}, bf16[512,1024]{1,0:T(8,128)(2,1)}, u32[]{:S(2)}) copy-start(bf16[512,1024]{1,0:T(8,128)(2,1)} %feat_hbm.1) | copy-start | bytes 3145732
  6.4 14.0 %copy-start.6 = (s32[16,4096]{1,0:T(8,128)S(1)}, s32[16,4096]{1,0:T(8,128)}, u32[]{:S(2)}) copy-start(s32[16,4096]{1,0:T(8,128)} %param.15) | copy-start | bytes 786436
  6.4 14.0 %copy-start.7 = (s32[16,4096]{1,0:T(8,128)S(1)}, s32[16,4096]{1,0:T(8,128)}, u32[]{:S(2)}) copy-start(s32[16,4096]{1,0:T(8,128)} %param.16) | copy-start | bytes 786436
  6.4 33.6 %all-to-all-start = ((bf16[128,40,128]{2,1,0:T(8,128)(2,1)}), bf16[128,40,128]{2,1,0:T(8,128)(2,1)S(1)}, u32[]{:S(2)}, u32[]{:S(2)}) async-start(bf16[128,40,128]{2,1,0:T(8,128)(2,1)} %get-tuple-element.37), calls=%async_computation | async-start | bytes 2621440 | tf_op jit(solution)/shard_map/all_to_all | solution.py:693
  19.3 7.9 %collective-permute-start = (bf16[1024,512]{1,0:T(8,128)(2,1)}, bf16[1024,512]{1,0:T(8,128)(2,1)S(1)}, u32[]{:S(2)}, u32[]{:S(2)}) collective-permute-start(bf16[1024,512]{1,0:T(8,128)(2,1)} %bitcast.3.feat_ref.feat_hbm), channel_id=1, source_target_pairs={{0,1},{1,0},{2,3},{3,2},{4,5},{5,4},{6,7},{7,6},{8,9},{9,8},{10,11... | collective-permute-start | bytes 3145736 | tf_op jit(solution)/shard_map/ppermute | solution.py:706
  27.2 17.8 %copy-start = (bf16[1024,512]{1,0:T(8,128)(2,1)}, bf16[1024,512]{1,0:T(8,128)(2,1)S(1)}, u32[]{:S(2)}) copy-start(bf16[1024,512]{1,0:T(8,128)(2,1)S(1)} %collective-permute-done.feat_other_ref.feat_ref) | copy-start | bytes 3145732
  45.0 24.0 %all-to-all-start.1 = ((bf16[128,32,128]{2,1,0:T(8,128)(2,1)}), bf16[128,32,128]{2,1,0:T(8,128)(2,1)S(1)}, u32[]{:S(2)}, u32[]{:S(2)}) async-start(bf16[128,32,128]{2,1,0:T(8,128)(2,1)} %get-tuple-element.44), calls=%async_computation.1 | async-start | bytes 2097152 | tf_op jit(solution)/shard_map/all_to_all | solution.py:693
  53.6 15.5 %copy-start.4 = (f32[128,128]{1,0:T(8,128)S(1)}, f32[128,128]{1,0:T(8,128)}, u32[]{:S(2)}) copy-start(f32[128,128]{1,0:T(8,128)} %get-tuple-element.53.named_ref) | copy-start | bytes 196612
  69.1 4.9 %copy-start.1 = (bf16[1024,512]{1,0:T(8,128)(2,1)S(1)}, bf16[1024,512]{1,0:T(8,128)(2,1)}, u32[]{:S(2)}) copy-start(bf16[1024,512]{1,0:T(8,128)(2,1)} %copy-done) | copy-start | bytes 3145732
  69.1 4.9 %copy-start.2 = (f32[512,256]{1,0:T(8,128)S(1)}, f32[512,256]{1,0:T(8,128)}, u32[]{:S(2)}) copy-start(f32[512,256]{1,0:T(8,128)} %get-tuple-element.64.slope_ref) | copy-start | bytes 1572868
  69.1 4.9 %copy-start.3 = (bf16[256,512]{1,0:T(8,128)(2,1)S(1)}, bf16[256,512]{1,0:T(8,128)(2,1)}, u32[]{:S(2)}) copy-start(bf16[256,512]{1,0:T(8,128)(2,1)} %get-tuple-element.63.hidden_ref) | copy-start | bytes 786436
  71.6 2.4 %collective-permute-start.1 = (bf16[512,128]{1,0:T(8,128)(2,1)S(1)}, bf16[512,128]{1,0:T(8,128)(2,1)S(1)}, u32[]{:S(2)}, u32[]{:S(2)}) collective-permute-start(bf16[512,128]{1,0:T(8,128)(2,1)S(1)} %get-tuple-element.56.dq_ref), channel_id=1, source_target_pairs={{0,1},{1,0},{2,3},{3,2},{4,5},{5,4},{6,7},{7,6},{8,9},{9,8},{10,11... | collective-permute-start | bytes 393224 | tf_op jit(solution)/shard_map/ppermute | solution.py:706
  109.0 5.3 %collective-permute-start.2 = (bf16[64,40,128]{2,1,0:T(8,128)(2,1)S(1)}, bf16[64,40,128]{2,1,0:T(8,128)(2,1)S(1)}, u32[]{:S(2)}, u32[]{:S(2)}) collective-permute-start(bf16[64,40,128]{2,1,0:T(8,128)(2,1)S(1)} %all_to_all.21.got_ref), channel_id=1, source_target_pairs={{0,1},{1,0},{2,3},{3,2},{4,5},{5,4},{6,7},{7,6},{8,9},{9,8},{10,11... | collective-permute-start | bytes 1966088 | tf_op jit(solution)/shard_map/ppermute | solution.py:706
